TPU v7x, 128 devices: a whole 4x4x4 slice. The times are simulated.
128 devices in a mesh: dp: 8 (over x, z_lo), ctx: 16 (over z_hi, y, core).
Axes of the slice: x: 4, y: 4, z: 4 (z_hi: 2, z_lo: 2; z = z_hi * 2 + z_lo), core: 2. Of those that a mesh axis runs over, the one named last changes fastest.
Arguments:
- tokens: bfloat16 [8, 8192, 1024], P('dp', 'ctx'), may hold values from -900 to 900
- grad_output: bfloat16 [8, 8192, 1024], P('dp', 'ctx'), may hold values from -6 to 6
- session_ids: int32 [8], P('dp'), may hold values from 0 to 63
- session_table: bfloat16 [64, 1024], replicated, may hold values from -6 to 6
- norm_gain: bfloat16 [1024], P('dp'), may hold values from 0.099609375 to 1.8984375
- input_weight: bfloat16 [1024, 2304], P('dp'), may hold values from -0.1875 to 0.1875
- step_weight: bfloat16 [1024, 16], P('dp'), may hold values from -1 to 1
- head_params: float32 [3, 16], replicated, may hold values from -9 to 4
- gate_gain: bfloat16 [1024], P('dp'), may hold values from 0.099609375 to 1.8984375
- output_weight: bfloat16 [1024, 1024], P('dp'), may hold values from -0.1875 to 0.1875
Outputs:
- tokens_grad: bfloat16 [8, 8192, 1024], P('dp', 'ctx')
- norm_grad: float32 [1024], P(('dp', 'ctx'))
- input_grad: float32 [1024, 2304], P(('dp', 'ctx'))
- step_grad: float32 [1024, 16], P(('dp', 'ctx'))
- head_grad: float32 [3, 16], replicated
- gate_grad: float32 [1024], P(('dp', 'ctx'))
- output_grad: float32 [1024, 1024], P(('dp', 'ctx'))
- table_grad: float32 [64, 1024], P(None, ('dp', 'ctx'))
All inputs are finite; a program needn't handle non-finite values.
Results may differ from a plain program's by a relative error of at most 0.005.
The roundings to bfloat16 on the way count: a program that leaves them out, or rounds other values in their place, can miss the bound.
Values may be sent and summed in bfloat16 or wider, within the bound.
No kernel may reach another device: no remote copies, remote signals or barrier semaphores. Data moves between devices by JAX's collectives and lax.ppermute only.
A program may use at most 128 MiB of HBM per device.

v0:
```python
import math

import jax
import jax.numpy as jnp
from jax import lax
from jax.sharding import PartitionSpec as P

epsilon = 1e-05


def carried_in(value, axis, join, neutral, backward):
    count, mine = (lax.axis_size(axis), lax.axis_index(axis))
    pieces = jax.tree.map(lambda part: lax.all_gather(part, axis), value)
    if backward:
        pieces = jax.tree.map(lambda part: part[::-1], pieces)
        mine = count - 1 - mine
    so_far = jax.tree.map(
        lambda part, zero: jnp.full_like(part, 0) + jnp.asarray(zero, part.dtype), value, neutral
    )

    def step(position, so_far):
        longer = join(so_far, jax.tree.map(lambda part: part[position], pieces))
        return jax.tree.map(lambda new, old: jnp.where(position < mine, new, old), longer, so_far)

    return lax.fori_loop(0, count - 1, step, so_far)


def normalize(quantity_items):
    factor = lax.rsqrt(jnp.mean(quantity_items * quantity_items, axis=-1, keepdims=True) + epsilon)
    return (quantity_items * factor, factor)


def block_prep(value_raw, step_raw, head_params):
    length = value_raw.shape[0]
    num_heads = step_raw.shape[1]
    activated = jax.nn.silu(value_raw)
    step_size = jax.nn.softplus(step_raw + head_params[0][None, :])
    log_rate = -jnp.exp(head_params[1])[None, :] * step_size
    log_decay = jnp.cumsum(log_rate, axis=0)
    scaled_in = step_size[:, :, None] * activated.reshape(length, num_heads, -1)
    return (activated, log_decay, scaled_in)


def state_block(value_raw, in_map, out_map, step_raw, head_params, state_in):
    length = value_raw.shape[0]
    num_heads = step_raw.shape[1]
    activated, log_decay, scaled_in = block_prep(value_raw, step_raw, head_params)
    positions = jnp.arange(length)
    causal = positions[:, None] >= positions[None, :]
    decay_log = log_decay.T
    decay_gap = jnp.where(causal[None], decay_log[:, :, None] - decay_log[:, None, :], 0.0)
    mask_decay = jnp.where(causal[None], jnp.exp(decay_gap), 0.0)
    scores = jnp.dot(out_map, in_map.T, precision=lax.Precision.HIGHEST)
    weighted = mask_decay * scores[None]
    result = jnp.einsum("hqk,khp->qhp", weighted, scaled_in, precision=lax.Precision.HIGHEST)
    carried = jnp.einsum("qn,hpn->qhp", out_map, state_in, precision=lax.Precision.HIGHEST)
    result = result + jnp.exp(log_decay)[:, :, None] * carried
    result = result + head_params[2][None, :, None] * activated.reshape(length, num_heads, -1)
    decay_tail = jnp.exp(log_decay[-1][None, :] - log_decay)
    fresh = jnp.einsum(
        "kh,khp,kn->hpn", decay_tail, scaled_in, in_map, precision=lax.Precision.HIGHEST
    )
    state_out = jnp.exp(log_decay[-1])[:, None, None] * state_in + fresh
    return (result.reshape(length, -1), state_out)


def blocks_all(value_raw, in_map, out_map, step_raw, head_params, state_in):

    def per_sequence(pieces):
        return state_block(pieces[0], pieces[1], pieces[2], pieces[3], head_params, pieces[4])

    runner = jax.checkpoint(per_sequence)
    return lax.map(runner, (value_raw, in_map, out_map, step_raw, state_in))


def combine_states(earlier, later):
    return (earlier[0] * later[0], later[0][:, :, None, None] * earlier[1] + later[1])


def per_device(
    tokens,
    grad_output,
    session_ids,
    session_table,
    norm_gain,
    input_weight,
    step_weight,
    head_params,
    gate_gain,
    output_weight,
):
    norm_low, input_full, step_full, gate_low, output_full = (
        lax.all_gather(norm_gain, "dp", axis=0, tiled=True),
        lax.all_gather(input_weight, "dp", axis=0, tiled=True),
        lax.all_gather(step_weight, "dp", axis=0, tiled=True),
        lax.all_gather(gate_gain, "dp", axis=0, tiled=True),
        lax.all_gather(output_weight, "dp", axis=0, tiled=True),
    )
    norm_full = norm_low.astype(jnp.float32)
    gate_full = gate_low.astype(jnp.float32)
    num_seqs, num_bins, model_width = tokens.shape
    inner_width = output_full.shape[0]
    state_width = (input_full.shape[1] - 2 * inner_width) // 2
    num_heads = step_full.shape[1]
    sessions = session_table.shape[0]
    grad_scale = 1.0 / math.sqrt(num_seqs * num_bins * lax.axis_size("dp") * lax.axis_size("ctx"))
    session_hot = (session_ids[:, None] == jnp.arange(sessions)[None, :]).astype(jnp.float32)
    table_rows = jnp.dot(
        session_hot, session_table.astype(jnp.float32), precision=lax.Precision.HIGHEST
    )
    layer_in = tokens.astype(jnp.float32) + table_rows[:, None, :]
    normed, in_scale = normalize(layer_in)
    norm_act = (normed * norm_full[None, None, :]).astype(jnp.bfloat16)
    projected = jnp.einsum("sqd,de->sqe", norm_act, input_full, preferred_element_type=jnp.float32)
    step_raw = jnp.einsum("sqd,dh->sqh", norm_act, step_full, preferred_element_type=jnp.float32)
    gate_pre = projected[:, :, :inner_width]
    value_raw = projected[:, :, inner_width : 2 * inner_width]
    in_map = projected[:, :, 2 * inner_width : 2 * inner_width + state_width]
    out_map = projected[:, :, 2 * inner_width + state_width :]
    activated, log_decay, scaled_in = jax.vmap(block_prep, in_axes=(0, 0, None))(
        value_raw, step_raw, head_params
    )
    decay_total = jnp.exp(log_decay[:, -1, :])
    decay_tail = jnp.exp(log_decay[:, -1:, :] - log_decay)
    state_local = jnp.einsum(
        "skh,skhp,skn->shpn", decay_tail, scaled_in, in_map, precision=lax.Precision.HIGHEST
    )
    identity = (jnp.ones_like(decay_total), jnp.zeros_like(state_local))
    state_in = carried_in((decay_total, state_local), "ctx", combine_states, identity, False)[1]
    outputs, core_back = jax.vjp(
        blocks_all, value_raw, in_map, out_map, step_raw, head_params, state_in
    )
    ssd_out = outputs[0]
    gated = ssd_out * jax.nn.silu(gate_pre)
    gated_norm, gate_scale = normalize(gated)
    mixed_out = (gated_norm * gate_full[None, None, :]).astype(jnp.bfloat16)
    grad_mixed = jnp.einsum(
        "sqd,ed->sqe", grad_output, output_full, preferred_element_type=jnp.float32
    )
    term_output = (
        jnp.einsum("sqe,sqd->ed", mixed_out, grad_output, preferred_element_type=jnp.float32)
        * grad_scale
    )
    term_gate = jnp.sum(grad_mixed * gated_norm, axis=(0, 1)) * grad_scale
    grad_gnorm = grad_mixed * gate_full[None, None, :]
    grad_gated = gate_scale * (
        grad_gnorm - gated_norm * jnp.mean(grad_gnorm * gated_norm, axis=-1, keepdims=True)
    )
    gate_sig = jax.nn.sigmoid(gate_pre)
    grad_ssd = grad_gated * jax.nn.silu(gate_pre)
    grad_gate = grad_gated * ssd_out * gate_sig * (1.0 + gate_pre * (1.0 - gate_sig))
    heads_view = grad_ssd.reshape(num_seqs, num_bins, num_heads, -1)
    adjoint_local = jnp.einsum(
        "sqh,sqhp,sqn->shpn",
        jnp.exp(log_decay),
        heads_view,
        out_map,
        precision=lax.Precision.HIGHEST,
    )
    adjoint_out = carried_in((decay_total, adjoint_local), "ctx", combine_states, identity, True)[1]
    grad_value, grad_in_map, grad_out_map, grad_step_raw, grad_heads, unused_state = core_back(
        (grad_ssd, adjoint_out)
    )
    grad_proj = jnp.concatenate([grad_gate, grad_value, grad_in_map, grad_out_map], axis=2).astype(
        jnp.bfloat16
    )
    grad_step_low = grad_step_raw.astype(jnp.bfloat16)
    grad_act = jnp.einsum("sqe,de->sqd", grad_proj, input_full, preferred_element_type=jnp.float32)
    grad_act = grad_act + jnp.einsum(
        "sqh,dh->sqd", grad_step_low, step_full, preferred_element_type=jnp.float32
    )
    term_input = (
        jnp.einsum("sqd,sqe->de", norm_act, grad_proj, preferred_element_type=jnp.float32)
        * grad_scale
    )
    term_step = (
        jnp.einsum("sqd,sqh->dh", norm_act, grad_step_low, preferred_element_type=jnp.float32)
        * grad_scale
    )
    term_norm = jnp.sum(grad_act * normed, axis=(0, 1)) * grad_scale
    grad_normed = grad_act * norm_full[None, None, :]
    grad_input = in_scale * (
        grad_normed - normed * jnp.mean(grad_normed * normed, axis=-1, keepdims=True)
    )
    term_table = (
        jnp.dot(session_hot.T, jnp.sum(grad_input, axis=1), precision=lax.Precision.HIGHEST)
        * grad_scale
    )
    totals = (
        lax.psum_scatter(term_norm, ("dp", "ctx"), scatter_dimension=0, tiled=True),
        lax.psum_scatter(term_input, ("dp", "ctx"), scatter_dimension=0, tiled=True),
        lax.psum_scatter(term_step, ("dp", "ctx"), scatter_dimension=0, tiled=True),
        lax.psum_scatter(term_gate, ("dp", "ctx"), scatter_dimension=0, tiled=True),
        lax.psum_scatter(term_output, ("dp", "ctx"), scatter_dimension=0, tiled=True),
        lax.psum_scatter(term_table, ("dp", "ctx"), scatter_dimension=1, tiled=True),
    )
    head_grad = lax.psum(grad_heads * grad_scale, ("dp", "ctx"))
    return (
        grad_input.astype(jnp.bfloat16),
        totals[0],
        totals[1],
        totals[2],
        head_grad,
        totals[3],
        totals[4],
        totals[5],
    )


def solution(mesh):
    placed = (
        P("dp", "ctx", None),
        P("dp", "ctx", None),
        P("dp"),
        P(),
        P("dp"),
        P("dp", None),
        P("dp", None),
        P(),
        P("dp"),
        P("dp", None),
    )
    return jax.shard_map(
        per_device,
        mesh=mesh,
        in_specs=placed,
        out_specs=(
            P("dp", "ctx", None),
            P(("dp", "ctx")),
            P(("dp", "ctx"), None),
            P(("dp", "ctx"), None),
            P(),
            P(("dp", "ctx")),
            P(("dp", "ctx"), None),
            P(None, ("dp", "ctx")),
        ),
        check_vma=False,
    )
```

profile of v0, /device:TPU:0, one launch (start us, length us, event | category | flops | bytes accessed | tf_op | source)
XLA Modules:
  0.0 1931.9 jit_solution(15579320906667247064)
XLA Ops:
  8.6 19.8 %all-gather.2 = bf16[8,1,128]{2,1,0:T(2,128)(2,1)S(1)} all-gather(bf16[1,1,128]{2,1,0:T(2,128)(2,1)} %bitcast.353), channel_id=1, replica_groups=mesh['dp'=8,'ctx'=16] {'dp'}, dimensions={0}, use_global_device_ids=true | all-gather | bytes 2304 | tf_op jit(solution)/shard_map/all_gather | solution.py:93
  28.4 31.4 %all_gather.34 = bf16[1024,16]{0,1:T(8,128)(2,1)S(1)} all-gather(bf16[128,16]{0,1:T(8,128)(2,1)} %param.20), channel_id=1, replica_groups=mesh['dp'=8,'ctx'=16] {'dp'}, dimensions={0}, use_global_device_ids=true | all-gather | bytes 36864 | tf_op jit(solution)/shard_map/all_gather | solution.py:95
  67.8 44.5 %all-gather.9.cloned.1.call-done = bf16[1024,2304]{1,0:T(8,128)(2,1)} async-done(((bf16[128,2304]{1,0:T(8,128)(2,1)}), bf16[1024,2304]{1,0:T(8,128)(2,1)}) %all-gather.9.cloned.1.call-update) | async-done | bytes 4718608 | tf_op jit(solution)/shard_map/all_gather | solution.py:94
  112.3 5.0 convolution_bitcast_fusion
  122.0 4.2 fusion.42
  128.8 17.5 all-gather.3
  146.4 24.8 %all_gather.36 = f32[16,1,16]{2,1,0:T(1,128)S(1)} all-gather(f32[1,1,16]{2,1,0:T(1,128)S(1)} %copy-done.36), channel_id=1, replica_groups=mesh['dp'=8,'ctx'=16] {'ctx'}, dimensions={0}, use_global_device_ids=true | all-gather | bytes 1088 | tf_op jit(solution)/shard_map/all_gather | solution.py:13
  176.2 24.3 %all-gather.13.cloned.1.call-done = f32[256,64,128]{2,1,0:T(8,128)} async-done(((f32[16,64,128]{2,1,0:T(8,128)}), f32[256,64,128]{2,1,0:T(8,128)}) %all-gather.13.cloned.1.call-update) | async-done | bytes 8388624 | tf_op jit(solution)/shard_map/all_gather | solution.py:13
  200.5 18.3 while.20
  221.8 20.8 %fusion.33 = f32[512,16,64]{0,2,1:T(8,128)} fusion(f32[512,16,64]{0,2,1:T(8,128)S(1)} %fusion.89, f32[512,512]{1,0:T(8,128)S(1)} %fusion.123, f32[16,512]{1,0:T(8,128)S(1)} %copy_bitcast_fusion.1, pred[512,512]{1,0:T(8,128)(4,1)S(1)} %iota_compare_fusion, f32[512,16,64]{0,2,1:T(8,128)S(1)} %bitcast.323, f32[16]{0:T(128)S(1)} %copy-done.37, ...), kind=kOutput, calls=%fused_computation.52 | convolution fusion | flops 3244818432 | bytes 7700544 | tf_op jit(solution)/shard_map/jvp()/while/body/eval_jaxpr/hqk,khp->qhp/dot_general | solution.py:55
  242.6 3.3 copy.161
  245.9 4.2 multiply_reduce_fusion.5
  251.7 4.5 fusion.27
  256.3 4.7 fusion.82
  263.9 4.2 fusion.39
  269.8 71.8 %all-gather.15.cloned.1.call-done = f32[256,64,128]{2,1,0:T(8,128)} async-done(((f32[16,64,128]{2,1,0:T(8,128)}), f32[256,64,128]{2,1,0:T(8,128)}) %all-gather.15.cloned.1.call-update) | async-done | bytes 8388624 | tf_op jit(solution)/shard_map/all_gather | solution.py:13
  341.6 8.3 rev.7
  349.8 18.2 while.21
  378.3 3.6 multiply_reduce_fusion.3
  386.8 5.9 fusion.56
  392.7 23.9 %fusion.13 = (f32[16,512]{1,0:T(8,128)S(1)}, f32[16,512]{1,0:T(8,128)S(1)}, f32[512,512]{1,0:T(8,128)S(1)}) fusion(f32[512,512]{1,0:T(8,128)} %fusion.135, f32[16,512]{1,0:T(8,128)S(1)} %get-tuple-element.498, pred[512,512]{1,0:T(8,128)(4,1)S(1)} %copy-done.23, f32[16,64,512]{2,1,0:T(8,128)S(1)} %bitcast.316, f32[512,16,64]{0,2,1:T(8,128)} %bitcast.320, ...), kind=kOutput, calls=%fused_computation.19 | convolution fusion | flops 3267608576 | bytes 6684672 | tf_op jit(solution)/shard_map/transpose(jvp())/while/body/eval_jaxpr/checkpoint/hqk,khp->qhp/dot_general | solution.py:55
  416.6 17.2 multiply_reduce_fusion.1
  433.8 3.1 copy.169
  437.3 5.0 fusion.59
  448.1 5.2 reduce-window.52
  461.1 5.4 fusion.83
  470.2 3.5 convolution_multiply_fusion.1
  475.2 7.6 convolution_multiply_fusion
  483.8 65.7 %all-reduce.9 = (f32[1024]{0:T(1024)S(1)}, f32[3,16]{1,0:T(4,128)}, f32[1024]{0:T(1024)S(1)}) all-reduce(f32[1024]{0:T(1024)S(1)} %broadcast_multiply_fusion.2, f32[3,16]{1,0:T(4,128)S(1)} %add_multiply_fusion, f32[1024]{0:T(1024)S(1)} %broadcast_multiply_fusion.1), channel_id=4, replica_groups=mesh['dp'=8,'ctx'=16] {'dp','ctx'}, use_global_device_ids=true, to_apply=%region_24.25.clone | all-reduce | flops 2096 | bytes 16768
  550.6 65.1 %all-reduce.13.cloned.1.call-done = (f32[1024,16]{1,0:T(8,128)}, f32[64,1024]{0,1:T(8,128)}) async-done(((f32[1024,16]{1,0:T(8,128)}, f32[64,1024]{0,1:T(8,128)}), (f32[1024,16]{1,0:T(8,128)}, f32[64,1024]{0,1:T(8,128)})) %all-reduce.13.cloned.1.call-update) | async-done | bytes 327696
  618.2 650.1 %reduce-scatter.5.cloned.1.call-done = f32[8,1024]{1,0:T(8,128)} async-done(((f32[1024,1024]{1,0:T(8,128)}), f32[8,1024]{1,0:T(8,128)}) %reduce-scatter.5.cloned.1.call-update) | async-done | bytes 32784 | tf_op jit(solution)/shard_map/reduce_scatter | solution.py:194
  1268.3 656.2 %reduce-scatter.3.cloned.1.call-done = f32[8,2304]{1,0:T(8,128)} async-done(((f32[1024,2304]{1,0:T(8,128)}), f32[8,2304]{1,0:T(8,128)}) %reduce-scatter.3.cloned.1.call-update) | async-done | bytes 73744 | tf_op jit(solution)/shard_map/reduce_scatter | solution.py:191
  (237 shorter events, 104.2 us)
Async XLA Ops:
  7.2 244.6 %copy-start = (bf16[1,512,1024]{2,1,0:T(8,128)(2,1)S(1)}, bf16[1,512,1024]{2,1,0:T(8,128)(2,1)}, u32[]{:S(2)}) copy-start(bf16[1,512,1024]{2,1,0:T(8,128)(2,1)} %param.15) | copy-start | bytes 3145732
  7.2 105.2 %all-gather.9.cloned.1.call-start = ((), (), s32[]{:S(2)}) async-start(), calls=%async_computation.2 | async-start | bytes 5308416 | tf_op jit(solution)/shard_map/all_gather | solution.py:94
  7.9 192.6 %all-gather.13.cloned.1.call-start = ((), (), s32[]{:S(2)}) async-start(), calls=%async_computation.6 | async-start | bytes 8912896 | tf_op jit(solution)/shard_map/all_gather | solution.py:13
  59.7 5.7 copy-start.24
  63.7 48.7 %copy-start.9 = (bf16[1,512,1024]{2,1,0:T(8,128)(2,1)S(1)}, bf16[1,512,1024]{2,1,0:T(8,128)(2,1)}, u32[]{:S(2)}) copy-start(bf16[1,512,1024]{2,1,0:T(8,128)(2,1)} %param.14) | copy-start | bytes 3145732
  65.5 302.9 %copy-start.21 = (f32[512,16]{0,1:T(8,128)}, f32[512,16]{0,1:T(8,128)S(1)}, u32[]{:S(2)}) copy-start(f32[512,16]{0,1:T(8,128)S(1)} %fusion.129) | copy-start | bytes 98308
  122.0 5.0 copy-start.32
  122.0 6.8 copy-start.35
  122.0 24.4 %copy-start.36 = (f32[1,1,16]{2,1,0:T(1,128)S(1)}, f32[1,1,16]{2,1,0:T(1,128)}, u32[]{:S(2)}) copy-start(f32[1,1,16]{2,1,0:T(1,128)} %get-tuple-element.489) | copy-start | bytes 196
  126.2 125.5 %all-gather.11.cloned.1.call-start = ((), (), s32[]{:S(2)}) async-start(), calls=%async_computation.3 | async-start | bytes 2359296 | tf_op jit(solution)/shard_map/all_gather | solution.py:97
  127.0 214.6 %all-gather.15.cloned.1.call-start = ((), (), s32[]{:S(2)}) async-start(), calls=%async_computation.7 | async-start | bytes 8912896 | tf_op jit(solution)/shard_map/all_gather | solution.py:13
  128.7 93.0 %copy-start.22 = (pred[512,512]{1,0:T(8,128)(4,1)}, pred[512,512]{1,0:T(8,128)(4,1)S(1)}, u32[]{:S(2)}) copy-start(pred[512,512]{1,0:T(8,128)(4,1)S(1)} %iota_compare_fusion) | copy-start | bytes 786436
  218.8 2.9 copy-start.17
  218.8 2.9 copy-start.37
  250.1 6.1 copy-start.26
  251.7 4.5 copy-start.2
  251.7 4.5 copy-start.5
  268.1 347.6 %all-reduce.13.cloned.1.call-start = ((), (), s32[]{:S(2)}) async-start(), calls=%async_computation.8 | async-start | bytes 2097152
  349.8 18.2 copy-start.28
  378.3 3.6 copy-start.6
  386.8 5.9 copy-start.8
  386.8 5.9 copy-start.23
  392.7 23.9 %copy-start.12 = (f32[512,1024]{0,1:T(8,128)S(1)}, f32[512,1024]{0,1:T(8,128)}, u32[]{:S(2)}) copy-start(f32[512,1024]{0,1:T(8,128)} %copy.170) | copy-start | bytes 6291460
  392.7 23.9 %copy-start.18 = (f32[512,16,64]{0,2,1:T(8,128)S(1)}, f32[512,16,64]{0,2,1:T(8,128)}, u32[]{:S(2)}) copy-start(f32[512,16,64]{0,2,1:T(8,128)} %fusion.85) | copy-start | bytes 6291460
  392.7 23.9 %copy-start.19 = (f32[512,512]{1,0:T(8,128)S(1)}, f32[512,512]{1,0:T(8,128)}, u32[]{:S(2)}) copy-start(f32[512,512]{1,0:T(8,128)} %fusion.135) | copy-start | bytes 3145732
  416.6 25.8 %copy-start.16 = (f32[512,512]{1,0:T(8,128)}, f32[512,512]{1,0:T(8,128)S(1)}, u32[]{:S(2)}) copy-start(f32[512,512]{1,0:T(8,128)S(1)} %get-tuple-element.437) | copy-start | bytes 3145732
  445.1 13.1 copy-start.1
  461.0 5.4 copy-start.15
  461.1 5.4 copy-start.10
  461.1 5.4 copy-start.25
  470.1 798.1 %reduce-scatter.5.cloned.1.call-start = ((), (), s32[]{:S(2)}) async-start(), calls=%async_computation.5 | async-start | bytes 4227072 | tf_op jit(solution)/shard_map/reduce_scatter | solution.py:194
  473.7 1450.8 %reduce-scatter.3.cloned.1.call-start = ((), (), s32[]{:S(2)}) async-start(), calls=%async_computation.4 | async-start | bytes 9510912 | tf_op jit(solution)/shard_map/reduce_scatter | solution.py:191
  (13 other events, 26.3 us)
Sparse Core Ops, SparseCore 0:
  9.6 102.6 all-gather.8
  126.4 74.1 all-gather.12
  202.2 49.5 all-gather.10
  268.2 73.3 all-gather.14
  470.3 145.3 all-reduce.12
  618.5 649.7 reduce-scatter.4
  1271.2 653.2 reduce-scatter.2
where the time goes:
time: 1940 us; the launch traced here: 1930 us
  waiting for transfers between devices  1520 us (78%)
  blocking collectives  159 us (8%)
  matrix products  133 us (7%)
  other arithmetic  69.8 us (4%)
  local copies, waits for them, and re-layouts  37.9 us (2%)
    reduce_scatter x1, waiting for transfers between devices, per_device(): lax.psum_scatter(term_input, ('dp', 'ctx'), scatter_dimension=0, tiled=True)  656 us
    reduce_scatter x1, waiting for transfers between devices, per_device(): lax.psum_scatter(term_output, ('dp', 'ctx'), scatter_dimension=0, tiled=T...  650 us
    all_gather x2, waiting for transfers between devices, carried_in(): pieces = jax.tree.map(lambda part: lax.all_gather(part, axis), value)  96.1 us
    unnamed x8, waiting for transfers between devices  66.5 us
    unnamed x1, blocking collectives  65.7 us
    dot_general x3, matrix products, state_block(): jnp.einsum('hqk,khp->qhp', weighted, scaled_in, precision=lax.Precision.H...  61.9 us
    all_gather x1, waiting for transfers between devices, per_device(): lax.all_gather(input_weight, 'dp', axis=0, tiled=True)  44.5 us
  transfers between devices with their start and end apart: 7, of which 7 were waited for; matrix products, arithmetic and copies ran while one was open for 4% of the time, Pallas kernels for 0%

commit v1 on v0

v1 whole, which is shorter than its diff:
```python
import functools
import math

import jax
import jax.numpy as jnp
from jax import lax
from jax.experimental import pallas as pl
from jax.experimental.pallas import tpu as pltpu
from jax.sharding import PartitionSpec as P

epsilon = 1e-05
ALL = ("dp", "ctx")
Q = 128
F32 = jnp.float32
LOW = jnp.bfloat16
NN = (((1,), (0,)), ((), ()))
NT = (((1,), (1,)), ((), ()))


def dot(a, b, dims=NN):
    return lax.dot_general(a, b, dims, preferred_element_type=F32)


def split(x):
    high = x.astype(LOW)
    return high, (x - high.astype(F32)).astype(LOW)


def dot3(a, b, dims=NN):
    (ah, al), (bh, bl) = split(a), split(b)
    return dot(ah, bh, dims) + dot(ah, bl, dims) + dot(al, bh, dims)


def thirds(x):
    high = x.astype(LOW)
    rest = x - high.astype(F32)
    mid = rest.astype(LOW)
    return high, mid, (rest - mid.astype(F32)).astype(LOW)


def select_dot(x, chosen, dims=NN):
    high, mid, low = thirds(x)
    return dot(high, chosen, dims) + dot(mid, chosen, dims) + dot(low, chosen, dims)


def select_left(chosen, x):
    high, mid, low = thirds(x)
    return dot(chosen, high) + dot(chosen, mid) + dot(chosen, low)


def sigmoid(x):
    return 1.0 / (1.0 + jnp.exp(-x))


def softplus(x):
    u = jnp.exp(-jnp.abs(x))
    w = 1.0 + u
    log1p = jnp.where(w == 1.0, u, jnp.log(w) * (u / jnp.where(w == 1.0, 1.0, w - 1.0)))
    return jnp.maximum(x, 0.0) + log1p


def iota(dim, shape=(Q, Q)):
    return lax.broadcasted_iota(jnp.int32, shape, dim)


def rows_of(c):
    return pl.ds(pl.multiple_of(c * Q, Q), Q)


def assemble(core, mine, other, whole):
    half = mine.shape[1]
    first = pl.multiple_of(core * half, half)
    second = pl.multiple_of((1 - core) * half, half)
    for i in range(mine.shape[0]):
        whole[pl.ds(2 * half * i + first, half), :] = mine[i]
        whole[pl.ds(2 * half * i + second, half), :] = other[i]


def prep_kernel(
    core_ref, tok, row, mine, other, hp, spread,
    wide, act_low, scale, value, in_map, out_map, step_raw, step, decay, fresh, packed, gains,
    state, total,
):
    assemble(core_ref[0], mine, other, wide)
    small = wide[:, 1280:1408].astype(F32).T
    gains[0:1, :] = small[16:17, :]
    gains[1:2, :] = small[17:18, :]
    state[...] = jnp.zeros_like(state)
    total[...] = jnp.zeros_like(total)
    ones_low = (iota(0) >= iota(1)).astype(F32).astype(LOW)
    used = iota(1) < 16

    def body(c, carry):
        rows = rows_of(c)
        x = tok[rows, :].astype(F32) + row[0:1, :]
        factor = lax.rsqrt(jnp.mean(x * x, axis=1, keepdims=True) + epsilon)
        low = (x * factor * gains[0:1, :]).astype(LOW)
        act_low[rows, :] = low
        scale[rows, :] = jnp.broadcast_to(factor, (Q, 128))
        value_c = dot(low, wide[:, :1024])
        value[rows, :] = value_c
        rest = dot(low, wide[:, 1024:1408])
        in_c = rest[:, 0:128]
        in_map[rows, :] = in_c
        out_map[rows, :] = rest[:, 128:256]
        raw = jnp.where(used, rest[:, 256:384] + hp[0:1, :], 0.0)
        step_raw[rows, :] = raw
        size = jnp.where(used, softplus(raw), 0.0)
        step[rows, :] = size
        logs = select_left(ones_low, -jnp.exp(hp[1:2, :]) * size)
        decay[rows, :] = logs
        last = logs[Q - 1 : Q, :]
        weight = select_dot(jnp.exp(last - logs) * size, spread[...])
        activated = value_c * sigmoid(value_c)
        fresh_c = dot3(in_c.T, weight * activated)
        fresh[rows, :] = fresh_c
        through = select_dot(jnp.broadcast_to(jnp.exp(last), (8, 128)), spread[...])[0:1, :]
        state[...] = through * state[...] + fresh_c
        total[...] = total[...] + last
        return carry

    lax.fori_loop(0, tok.shape[0] // Q, body, 0)
    packed[:, :1024] = state[...]
    packed[:, 1024:1152] = jnp.broadcast_to(jnp.exp(total[0:1, :]), (128, 128))


def scan_forward(pieces, spread, carried, decays):
    count = pieces.shape[0]
    rates = jnp.concatenate([pieces[j, 0:1, 1024:1152] for j in range(count)], axis=0)
    decays[...] = select_dot(rates, spread[...])
    held = jnp.zeros((8, 1024), F32)
    for j in range(count):
        carried[j] = held
        held = decays[j : j + 1, :] * held + pieces[j, :, :1024]


def scan_backward(pieces, decays, carried):
    count = pieces.shape[0]
    held = jnp.zeros((8, 1024), F32)
    for j in range(count - 1, -1, -1):
        carried[j] = held
        held = decays[j : j + 1, :] * held + pieces[j]


def pair_gaps(logs, logs_t, pair, transposed):
    gaps = []
    for head in (2 * pair, 2 * pair + 1):
        column = jnp.broadcast_to(logs[:, head : head + 1], (Q, Q))
        across = jnp.broadcast_to(logs_t[head : head + 1, :], (Q, Q))
        if transposed:
            gap = jnp.where(iota(1) >= iota(0), across - column, -1e30)
        else:
            gap = jnp.where(iota(0) >= iota(1), column - across, -1e30)
        gaps.append(jnp.exp(gap))
    return gaps


def by_head(x, axis):
    first = iota(1) < 64
    return jnp.concatenate([jnp.where(first, x, 0.0), jnp.where(first, 0.0, x)], axis=axis)


def widen(row, spread):
    return select_dot(jnp.broadcast_to(row, (8, 128)), spread)[0:1, :]


def local_kernel(value, in_map, out_map, step, decay, fresh, spread, y_local, states, ssd, scaled, held):
    held[...] = jnp.zeros_like(held)

    def body(c, carry):
        rows = rows_of(c)
        states[rows, :] = held[...]
        logs = decay[rows, :]
        logs_t = logs.T
        value_c = value[rows, :]
        scaled[...] = select_dot(step[rows, :], spread[...]) * (value_c * sigmoid(value_c))
        reach = select_dot(jnp.exp(logs), spread[...])
        out_c = out_map[rows, :]
        scores = dot3(out_c, in_map[rows, :], NT)
        for pair in range(8):
            lanes = slice(128 * pair, 128 * pair + 128)
            one, two = pair_gaps(logs, logs_t, pair, False)
            weighted = jnp.concatenate([one * scores, two * scores], axis=1)
            ssd[:, lanes] = dot3(weighted, by_head(scaled[:, lanes], 0))
        y_local[rows, :] = ssd[...] + reach * dot3(out_c, held[...])
        through = widen(jnp.exp(logs[Q - 1 : Q, :]), spread[...])
        held[...] = through * held[...] + fresh[rows, :]
        return carry

    lax.fori_loop(0, value.shape[0] // Q, body, 0)


def mix_kernel(
    place_ref, act_low, mine, other, grad_out, value, out_map, decay, y_local,
    states_local, state_in, gains, hp, spread,
    gate_whole, mixed, grad_gate, grad_ssd, out_dot, adjoint, adjoint_local, states, sums,
    out_whole, base,
):
    core, group = place_ref[0], place_ref[1]
    half = mine.shape[1]
    for i in range(mine.shape[0]):
        start = ((group + i // 2) % 4 * 2 + i % 2) * (2 * half)
        for block, turn in ((mine, core), (other, 1 - core)):
            rows = pl.ds(pl.multiple_of(start + turn * half, half), half)
            gate_whole[rows, :] = block[i, :, :1024]
            out_whole[rows, :] = block[i, :, 1024:]
    base[...] = jnp.ones_like(base)
    adjoint_local[...] = jnp.zeros_like(adjoint_local)
    sums[...] = jnp.zeros_like(sums)
    skip = widen(hp[2:3, :], spread[...])

    def body(c, carry):
        rows = rows_of(c)
        before = base[0:1, :]
        entering = before * state_in[...]
        states[rows, :] = states_local[rows, :] + entering
        logs = decay[rows, :]
        value_c = value[rows, :]
        activated = value_c * sigmoid(value_c)
        reach = select_dot(jnp.exp(logs), spread[...])
        out_c = out_map[rows, :]
        y_state = y_local[rows, :] + reach * dot3(out_c, entering)
        y = y_state + skip * activated
        gate = dot(act_low[rows, :], gate_whole[...])
        grad_mixed = dot(grad_out[rows, :], out_whole[...], NT)
        sig = sigmoid(gate)
        silu = gate * sig
        gated = y * silu
        gate_scale = lax.rsqrt(jnp.mean(gated * gated, axis=1, keepdims=True) + epsilon)
        gnorm = gated * gate_scale
        mixed[rows, :] = (gnorm * gains[1:2, :]).astype(LOW)
        along = grad_mixed * gnorm
        sums[0:1, :] = sums[0:1, :] + jnp.sum(along, axis=0, keepdims=True)
        grad_gnorm = grad_mixed * gains[1:2, :]
        mean = jnp.mean(grad_gnorm * gnorm, axis=1, keepdims=True)
        grad_gated = gate_scale * (grad_gnorm - gnorm * mean)
        grad_gate[rows, :] = (grad_gated * y * sig * (1.0 + gate * (1.0 - sig))).astype(LOW)
        grad_y = grad_gated * silu
        grad_ssd[rows, :] = grad_y
        sums[1:2, :] = sums[1:2, :] + jnp.sum(grad_y * activated, axis=0, keepdims=True)
        out_dot[rows, :] = select_dot(grad_y * y_state, spread[...], NT)
        adjoint_c = dot3(out_c.T, reach * grad_y)
        adjoint[rows, :] = adjoint_c
        adjoint_local[...] = adjoint_local[...] + before * adjoint_c
        base[0:1, :] = before * widen(jnp.exp(logs[Q - 1 : Q, :]), spread[...])
        return carry

    lax.fori_loop(0, act_low.shape[0] // Q, body, 0)


def inner_kernel(
    spread, value, in_map, out_map, step, decay, fresh, states, grad_ssd, adjoint,
    grad_scaled, grad_maps, crossings,
    held, scaled,
):
    held[...] = jnp.zeros_like(held)
    chunks = value.shape[0] // Q

    def body(i, carry):
        c = chunks - 1 - i
        rows = rows_of(c)
        logs = decay[rows, :]
        logs_t = logs.T
        last = logs[Q - 1 : Q, :]
        in_c = in_map[rows, :]
        out_c = out_map[rows, :]
        through = widen(jnp.exp(last), spread[...])
        state_end = through * states[rows, :] + fresh[rows, :]
        crossing = jnp.sum(held[...] * state_end, axis=0, keepdims=True)
        crossing = select_dot(jnp.broadcast_to(crossing, (8, 1024)), spread[...], NT)
        crossings[pl.ds(pl.multiple_of(8 * c, 8), 8), :] = crossing
        value_c = value[rows, :]
        scaled[...] = select_dot(step[rows, :], spread[...]) * (value_c * sigmoid(value_c))
        tail = select_dot(jnp.exp(last - logs), spread[...])
        grad_scaled[rows, :] = tail * dot3(in_c, held[...])
        grad_in = dot3(tail * scaled[...], held[...], NT)
        reach = select_dot(jnp.exp(logs), spread[...])
        grad_out_map = dot3(reach * grad_ssd[rows, :], states[rows, :], NT)
        scores = dot3(in_c, out_c, NT)
        grad_scores = jnp.zeros((Q, Q), F32)
        for pair in range(8):
            lanes = slice(128 * pair, 128 * pair + 128)
            one, two = pair_gaps(logs, logs_t, pair, True)
            grad_pair = by_head(grad_ssd[rows, lanes], 0)
            weighted = jnp.concatenate([one * scores, two * scores], axis=1)
            grad_scaled[rows, lanes] = grad_scaled[rows, lanes] + dot3(weighted, grad_pair)
            both = dot3(scaled[:, lanes], grad_pair, NT)
            grad_scores = grad_scores + one * both[:, :Q] + two * both[:, Q:]
        grad_maps[rows, 0:128] = grad_in + dot3(grad_scores, out_c)
        grad_maps[rows, 128:256] = grad_out_map + dot3(grad_scores.T, in_c)
        held[...] = adjoint[rows, :] + through * held[...]
        return carry

    lax.fori_loop(0, chunks, body, 0)


def grad_kernel(
    tok, row, scale, gains, hp, spread, wide, gate_whole, grad_gate, value, in_map,
    step_raw, step, decay, fresh, states, grad_ssd, out_dot, grad_inner, grad_maps, crossings,
    adjoint_out, sums_mix,
    grad_wide, tokens_grad, sums, heads,
    after,
):
    after[...] = jnp.ones_like(after)
    sums[...] = jnp.zeros_like(sums)
    heads[...] = jnp.zeros_like(heads)
    heads[2:3, :] = select_dot(sums_mix[...], spread[...], NT)[1:2, :]
    skip = widen(hp[2:3, :], spread[...])
    chunks = tok.shape[0] // Q
    ones_up = (iota(1) >= iota(0)).astype(F32).astype(LOW)

    def body(i, carry):
        c = chunks - 1 - i
        rows = rows_of(c)
        logs = decay[rows, :]
        last = logs[Q - 1 : Q, :]
        size = step[rows, :]
        through = widen(jnp.exp(last), spread[...])
        leaving = after[0:1, :] * adjoint_out[...]
        state_end = through * states[rows, :] + fresh[rows, :]
        crossing = jnp.sum(leaving * state_end, axis=0, keepdims=True)
        crossing = select_dot(jnp.broadcast_to(crossing, (8, 1024)), spread[...], NT)
        crossing = (crossing + crossings[pl.ds(pl.multiple_of(8 * c, 8), 8), :])[0:1, :]
        value_c = value[rows, :]
        sig = sigmoid(value_c)
        activated = value_c * sig
        size_wide = select_dot(size, spread[...])
        tail = select_dot(jnp.exp(last - logs), spread[...])
        grad_scaled = grad_inner[rows, :] + tail * dot3(in_map[rows, :], leaving)
        grad_in = grad_maps[rows, 0:128] + dot3(tail * (size_wide * activated), leaving, NT)
        per_step = select_dot(activated * grad_scaled, spread[...], NT)
        grad_logs = out_dot[rows, :] - size * per_step
        grad_rate = select_left(ones_up, grad_logs) + crossing
        speed = jnp.exp(hp[1:2, :])
        raw = step_raw[rows, :]
        grad_raw = jnp.where(iota(1) < 16, (per_step - speed * grad_rate) * sigmoid(raw), 0.0)
        heads[0:1, :] = heads[0:1, :] + jnp.sum(grad_raw, axis=0, keepdims=True)
        heads[1:2, :] = heads[1:2, :] - jnp.sum(
            grad_rate * (speed * size), axis=0, keepdims=True
        )
        grad_act_c = size_wide * grad_scaled + skip * grad_ssd[rows, :]
        grad_wide[rows, 0:1024] = (grad_act_c * sig * (1.0 + value_c * (1.0 - sig))).astype(LOW)
        grad_wide[rows, 1024:1152] = grad_in.astype(LOW)
        grad_wide[rows, 1152:1280] = grad_maps[rows, 128:256].astype(LOW)
        grad_wide[rows, 1280:1408] = grad_raw.astype(LOW)
        after[0:1, :] = after[0:1, :] * through
        grad_act = dot(grad_wide[rows, :], wide[...], NT) + dot(
            grad_gate[rows, :], gate_whole[...], NT
        )
        factor = scale[rows, 0:1]
        normed = (tok[rows, :].astype(F32) + row[0:1, :]) * factor
        sums[0:1, :] = sums[0:1, :] + jnp.sum(grad_act * normed, axis=0, keepdims=True)
        grad_normed = grad_act * gains[0:1, :]
        mean = jnp.mean(grad_normed * normed, axis=1, keepdims=True)
        grad_input = factor * (grad_normed - normed * mean)
        tokens_grad[rows, :] = grad_input.astype(LOW)
        sums[1:2, :] = sums[1:2, :] + jnp.sum(grad_input, axis=0, keepdims=True)
        return carry

    lax.fori_loop(0, chunks, body, 0)


def early_kernel(mine, other, packed):
    def body(j, carry):
        rows = pl.ds(pl.multiple_of(j * Q, Q), Q)
        both = mine[rows, :].astype(F32) + other[rows, :].astype(F32)
        packed[pl.ds(j * 16, 16)] = both.reshape(16, 8, -1).astype(LOW)
        return carry

    lax.fori_loop(0, mine.shape[0] // Q, body, 0)


def late_kernel(core_ref, term, other, sums, sums_mix, tile, packed, across, columns):
    across[...] = jnp.zeros_like(across)
    across[16:17, :] = sums[0:1, :]
    across[17:18, :] = sums_mix[0:1, :]
    across[24:25, :] = sums[1:2, :]
    columns[...] = across[...].T
    first = core_ref[0] == 0
    lane = iota(1)

    def body(j, carry):
        rows = pl.ds(pl.multiple_of(j * Q, Q), Q)
        mine = jnp.where(first, term[rows, 0:640], term[rows, 640:1280])
        both = mine.astype(LOW).astype(F32) + other[rows, :].astype(F32)
        packed[pl.ds(j * 16, 16), :, 0:640] = both.reshape(16, 8, 640).astype(LOW)
        extra = (term[rows, 1280:1408] + columns[rows, :]).reshape(16, 8, 128)
        extra = (extra + tile[...][None]).reshape(Q, 128)
        coarse = extra.astype(LOW).astype(F32)
        fine = pltpu.roll(extra - coarse, 64, 1)
        small = jnp.where(lane < 64, coarse, fine)
        packed[pl.ds(j * 16, 16), :, 640:768] = small.reshape(16, 8, 128).astype(LOW)
        return carry

    lax.fori_loop(0, term.shape[0] // Q, body, 0)


def sum_kernel(grad_scale, early, late, input_grad, output_grad, small, table):
    input_grad[...] = jnp.zeros_like(input_grad)
    output_grad[...] = jnp.zeros_like(output_grad)
    small[...] = jnp.zeros_like(small)
    table[...] = jnp.zeros_like(table)
    lane = lax.broadcasted_iota(jnp.int32, (8, 128), 1).astype(F32)

    def body(j, carry):
        input_grad[:, 0:1024] += early[2 * j].astype(F32)
        output_grad[...] += early[2 * j + 1].astype(F32)
        input_grad[:, 1024:1664] += late[2 * j, :, 0:640].astype(F32)
        input_grad[:, 1664:2304] += late[2 * j + 1, :, 0:640].astype(F32)
        for k in range(2):
            parts = late[2 * j + k, :, 640:768].astype(F32)
            parts = parts + pltpu.roll(parts, 64, 1)
            small[...] += parts
            table[...] += jnp.where(lane == parts[:, 25:26], parts[:, 24:25], 0.0)
        return carry

    lax.fori_loop(0, early.shape[0] // 2, body, 0, unroll=4)
    for out in (input_grad, output_grad, small, table):
        out[...] = out[...] * grad_scale


def at_origin(rank, *unused):
    return (0,) * rank


def run(kernel, args, outs, scratch=(), scalars=0):
    specs = [
        pl.BlockSpec(
            arg.shape, functools.partial(at_origin, arg.ndim), pipeline_mode=pl.Buffered(1)
        )
        for arg in args[scalars:]
    ]
    out_specs = [
        pl.BlockSpec(shape, functools.partial(at_origin, len(shape)), pipeline_mode=pl.Buffered(1))
        for shape, _ in outs
    ]
    return pl.pallas_call(
        kernel,
        name=getattr(kernel, "__name__", "sum_kernel"),
        out_shape=[jax.ShapeDtypeStruct(shape, dtype) for shape, dtype in outs],
        grid_spec=pltpu.PrefetchScalarGridSpec(
            num_scalar_prefetch=scalars,
            grid=(1,),
            in_specs=specs,
            out_specs=out_specs,
            scratch_shapes=[pltpu.VMEM(shape, dtype) for shape, dtype in scratch],
        ),
        compiler_params=pltpu.CompilerParams(vmem_limit_bytes=60 << 20),
    )(*args)


def core_partner(value):
    flips = [(i, i ^ 1) for i in range(lax.axis_size("dp") * lax.axis_size("ctx"))]
    return lax.ppermute(value, ALL, flips)


def on_first_core():
    return lax.axis_index("ctx") % 2 == 0


def gather_rows(shard):
    half = shard.shape[0] // 2
    count = lax.axis_size("dp")
    mine = jnp.where(on_first_core(), shard[:half], shard[half:])
    pieces = lax.all_to_all(jnp.broadcast_to(mine[None], (count,) + mine.shape), "dp", 0, 0)
    return pieces, core_partner(pieces)


def moved(value, to):
    count = lax.axis_size("dp") * lax.axis_size("ctx")
    return lax.ppermute(value, ALL, [(i, to(i) % count) for i in range(count)])


def ring_near(shard):
    half = shard.shape[0] // 2
    slots = lax.axis_size("ctx")
    mine = jnp.where(on_first_core(), shard[:half], shard[half:])
    return mine, moved(mine, lambda i: i ^ slots)


def ring_sides(mine, near):
    step = 2 * lax.axis_size("ctx")
    even = lax.axis_index("dp") % 2 == 0
    pair = jnp.stack([jnp.where(even, mine, near), jnp.where(even, near, mine)])
    return pair, moved(pair, lambda i: i + step), moved(pair, lambda i: i - step)


def ring_far(lower, upper):
    step = 2 * lax.axis_size("ctx")
    half = lower.shape[1] // 2
    far_low = moved(lower[:, :half], lambda i: i + step)
    far_high = moved(upper[:, half:], lambda i: i - step)
    return far_low, far_high


def column_dot(a, b):
    return lax.dot_general(a, b, (((0,), (0,)), ((), ())), preferred_element_type=F32)


def per_device(
    tokens,
    grad_output,
    session_ids,
    session_table,
    norm_gain,
    input_weight,
    step_weight,
    head_params,
    gate_gain,
    output_weight,
):
    tok, grad_out = tokens[0], grad_output[0]
    bins = tok.shape[0]
    devices = lax.axis_size("dp") * lax.axis_size("ctx")
    slots = lax.axis_size("ctx")
    sessions = session_table.shape[0]
    grad_scale = 1.0 / math.sqrt(bins * devices)
    core = (lax.axis_index("ctx") % 2).astype(jnp.int32)[None]
    first = on_first_core()
    row = lax.dynamic_slice(session_table, (session_ids[0], 0), (1, 1024)).astype(F32)
    row = jnp.broadcast_to(row, (8, 1024))
    params = jnp.pad(head_params, ((0, 5), (0, 112)))
    spread = (jnp.arange(1024)[None, :] // 64 == jnp.arange(128)[:, None]).astype(LOW)
    shard = jnp.concatenate(
        [
            input_weight[:, 1024:],
            step_weight,
            norm_gain[:, None],
            gate_gain[:, None],
            jnp.zeros((input_weight.shape[0], 110), LOW),
        ],
        axis=1,
    )
    mine, other = gather_rows(shard)
    mine, rest = lax.optimization_barrier(
        (mine, jnp.concatenate([input_weight[:, :1024], output_weight], axis=1))
    )
    rest_half, near = ring_near(rest)
    place = jnp.stack([core[0], lax.axis_index("dp").astype(jnp.int32) // 2])
    seq = (bins, 1024)
    lane = (bins, 128)
    prepared = run(
        prep_kernel,
        (core, tok, row, mine, other, params, spread),
        (
            ((1024, 1408), LOW), (seq, LOW), (lane, F32), (seq, F32), (lane, F32), (lane, F32),
            (lane, F32), (lane, F32), (lane, F32), (seq, F32), ((128, 1152), F32), ((8, 1024), F32),
        ),
        (((128, 1024), F32), ((8, 128), F32)),
        1,
    )
    wide, act_low, scale, value, in_map, out_map, step_raw, step, decay, fresh, packed, gains = (
        prepared
    )
    near, packed = lax.optimization_barrier((near, packed))
    pair, lower, upper = ring_sides(rest_half, near)
    pieces = lax.all_to_all(packed.reshape(slots, 8, 1152), "ctx", 0, 0)
    y_local, states_local = run(
        local_kernel,
        (value, in_map, out_map, step, decay, fresh, spread),
        ((seq, F32), (seq, F32)),
        (((Q, 1024), F32), ((Q, 1024), F32), ((128, 1024), F32)),
    )
    pieces, y_local, lower, upper = lax.optimization_barrier((pieces, y_local, lower, upper))
    far_low, far_high = ring_far(lower, upper)
    carried, decays = run(
        scan_forward, (pieces, spread), (((slots, 8, 1024), F32), ((slots, 1024), F32))
    )
    carried, far_low, far_high = lax.optimization_barrier((carried, far_low, far_high))
    far = jnp.concatenate([far_low, far_high], axis=1)
    rest_mine = jnp.concatenate([pair, upper, far, lower], axis=0)
    rest_other = core_partner(rest_mine)
    state_in = lax.all_to_all(carried, "ctx", 0, 0).reshape(128, 1024)
    gate_whole, mixed, grad_gate, grad_ssd, out_dot, adjoint, adjoint_local, states, sums_mix = run(
        mix_kernel,
        (
            place, act_low, rest_mine, rest_other, grad_out, value, out_map, decay, y_local,
            states_local, state_in, gains, params, spread,
        ),
        (
            ((1024, 1024), LOW), (seq, LOW), (seq, LOW), (seq, F32), (lane, F32), (seq, F32),
            ((128, 1024), F32), (seq, F32), ((8, 1024), F32),
        ),
        (((1024, 1024), LOW), ((8, 1024), F32)),
        1,
    )
    pieces = lax.all_to_all(adjoint_local.reshape(slots, 8, 1024), "ctx", 0, 0)
    term_output = column_dot(mixed, grad_out).astype(LOW)
    term_gates = column_dot(act_low, grad_gate).astype(LOW)
    received = core_partner(jnp.where(first, term_output, term_gates))
    (early,) = run(
        early_kernel,
        (jnp.where(first, term_gates, term_output), received),
        (((devices, 8, 1024), LOW),),
    )
    grad_inner, grad_maps, crossings = run(
        inner_kernel,
        (
            spread, value, in_map, out_map, step, decay, fresh, states, grad_ssd, adjoint,
        ),
        ((seq, F32), ((bins, 256), F32), ((bins // Q * 8, 128), F32)),
        (((128, 1024), F32), ((Q, 1024), F32)),
    )
    pieces, grad_inner = lax.optimization_barrier((pieces, grad_inner))
    (carried,) = run(scan_backward, (pieces, decays), (((slots, 8, 1024), F32),))
    adjoint_out = lax.all_to_all(carried, "ctx", 0, 0).reshape(128, 1024)
    adjoint_out, early = lax.optimization_barrier((adjoint_out, early))
    early_got = lax.all_to_all(early, ALL, 0, 0)
    grad_wide, tokens_grad, sums, heads = run(
        grad_kernel,
        (
            tok, row, scale, gains, params, spread, wide, gate_whole, grad_gate, value, in_map,
            step_raw, step, decay, fresh, states, grad_ssd, out_dot, grad_inner, grad_maps,
            crossings, adjoint_out, sums_mix,
        ),
        (((bins, 1408), LOW), (seq, LOW), ((8, 1024), F32), ((8, 128), F32)),
        (((8, 1024), F32),),
    )
    term_wide = column_dot(act_low, grad_wide)
    received = core_partner(
        jnp.where(first, term_wide[:, 640:1280], term_wide[:, :640]).astype(LOW)
    )
    tile = jnp.concatenate(
        [
            jnp.zeros((8, 18), F32),
            heads[:3, :16].reshape(8, 6),
            jnp.zeros((8, 1), F32),
            jnp.broadcast_to(session_ids.astype(F32)[:, None], (8, 1)),
            jnp.zeros((8, 102), F32),
        ],
        axis=1,
    )
    (late,) = run(
        late_kernel,
        (core, term_wide, received, sums, sums_mix, tile),
        (((devices, 8, 768), LOW),),
        (((128, 1024), F32), ((1024, 128), F32)),
        1,
    )
    late_got = lax.all_to_all(late, ALL, 0, 0)
    input_grad, output_grad, totals, table = run(
        functools.partial(sum_kernel, grad_scale),
        (early_got, late_got),
        (((8, 2304), F32), ((8, 1024), F32), ((8, 128), F32), ((8, 128), F32)),
    )
    return (
        tokens_grad[None],
        totals[:, 16],
        input_grad,
        totals[:, :16],
        totals[:, 18:24].reshape(3, 16),
        totals[:, 17],
        output_grad,
        table[:, :sessions].T,
    )


def solution(mesh):
    placed = (
        P("dp", "ctx", None),
        P("dp", "ctx", None),
        P("dp"),
        P(),
        P("dp"),
        P("dp", None),
        P("dp", None),
        P(),
        P("dp"),
        P("dp", None),
    )
    return jax.shard_map(
        per_device,
        mesh=mesh,
        in_specs=placed,
        out_specs=(
            P("dp", "ctx", None),
            P(("dp", "ctx")),
            P(("dp", "ctx"), None),
            P(("dp", "ctx"), None),
            P(),
            P(("dp", "ctx")),
            P(("dp", "ctx"), None),
            P(None, ("dp", "ctx")),
        ),
        check_vma=False,
    )
```

time: 1940 us -> 267 us (0.14)
  waiting for transfers between devices: 1520 us -> 23.7 us
  matrix products: 133 us -> 9.22 us
  Pallas kernels: 0 us -> 105 us
  blocking collectives: 159 us -> 59.5 us
  other arithmetic: 69.8 us -> 7.98 us
  starting transfers between devices: 0.28 us -> 39.8 us
    reduce_scatter x2 -> x0, waiting for transfers between devices: 1310 us -> none  [the longest x1 656 us: per_device(): lax.psum_scatter(term_input, ('dp', 'ctx'), scatter_dimension=0, tiled=True)]
    all_gather x4 -> x0, waiting for transfers between devices: 142 us -> none  [the longest x2 96.1 us: carried_in(): pieces = jax.tree.map(lambda part: lax.all_gather(part, axis), value)]
    dot_general x23 -> x3, matrix products: 133 us -> 9.22 us  [column_dot(): lax.dot_general(a, b, (((0,), (0,)), ((), ())), preferred_element_type=F32)]
    pallas_call x0 -> x10, Pallas kernels: none -> 105 us  [run(): pl.pallas_call(kernel, name=getattr(kernel, '__name__', 'sum_kernel'), ou...]
    all_gather x4 -> x0, blocking collectives: 93.4 us -> none  [the longest x1 31.4 us: per_device(): lax.all_gather(step_weight, 'dp', axis=0, tiled=True)]
    unnamed x8 -> x0, waiting for transfers between devices: 66.5 us -> none
    unnamed x1 -> x0, blocking collectives: 65.7 us -> none
    all_to_all x0 -> x2, blocking collectives: none -> 59.5 us  [the longest x1 34.1 us: per_device(): late_got = lax.all_to_all(late, ALL, 0, 0)]
  transfers between devices with their start and end apart: 7 -> 14, of which waited for: 7 -> 6; matrix products, arithmetic and copies ran while one was open for 4% -> 5% of each run, Pallas kernels for 0% -> 30%
where the time goes in v1:
time: 267 us; the launch traced here: 266 us
  Pallas kernels  105 us (39%)
  blocking collectives  59.5 us (22%)
  starting transfers between devices  39.8 us (15%)
  waiting for transfers between devices  23.7 us (9%)
  local copies, waits for them, and re-layouts  19.3 us (7%)
  matrix products  9.22 us (3%)
  other arithmetic  7.98 us (3%)
    pallas_call x10, Pallas kernels, run(): pl.pallas_call(kernel, name=getattr(kernel, '__name__', 'sum_kernel'), ou...  105 us
    all_to_all x1, blocking collectives, per_device(): late_got = lax.all_to_all(late, ALL, 0, 0)  34.1 us
    all_to_all x1, blocking collectives, gather_rows(): lax.all_to_all(jnp.broadcast_to(mine[None], (count,) + mine.shape), 'dp',...  25.4 us
    all_to_all x1, waiting for transfers between devices, per_device(): state_in = lax.all_to_all(carried, 'ctx', 0, 0).reshape(128, 1024)  11.7 us
    dot_general x3, matrix products, column_dot(): lax.dot_general(a, b, (((0,), (0,)), ((), ())), preferred_element_type=F32)  9.22 us
    ppermute x5, starting transfers between devices, moved(): return lax.ppermute(value, ALL, [(i, to(i) % count) for i in range(count)])  7.65 us
    all_to_all x1, starting transfers between devices, per_device(): pieces = lax.all_to_all(packed.reshape(slots, 8, 1152), 'ctx', 0, 0)  7.59 us
    unnamed x28, local copies, waits for them, and re-layouts  7.28 us
  transfers between devices with their start and end apart: 14, of which 6 were waited for; matrix products, arithmetic and copies ran while one was open for 5% of the time, Pallas kernels for 30%

profile of v1, /device:TPU:0, one launch (start us, length us, event | category | flops | bytes accessed | tf_op | source)
XLA Modules:
  0.0 266.1 jit_solution(6769572008025795498)
XLA Ops:
  4.3 25.4 %all_to_all.35.mine = bf16[8,64,1408]{2,1,0:T(8,128)(2,1)S(1)} all-to-all(bf16[8,64,1408]{2,1,0:T(8,128)(2,1)S(1)} %broadcast_in_dim.54), channel_id=1, replica_groups=mesh['dp'=8,'ctx'=16] {'dp'}, dimensions={0} | all-to-all | bytes 2883584 | tf_op jit(solution)/shard_map/all_to_all | solution.py:465
  29.8 1.8 slice.51
  38.3 12.2 %prep_kernel.1 = (bf16[1024,1408]{1,0:T(8,128)(2,1)}, bf16[512,1024]{1,0:T(8,128)(2,1)}, f32[512,128]{1,0:T(8,128)}, f32[512,1024]{1,0:T(8,128)}, f32[512,128]{1...) custom-call(s32[1]{0:T(128)} %bitcast.3.core_ref, ...), custom_call_target="tpu_custom_call" | custom-call | tf_op jit(solution)/shard_map/prep_kernel/pallas_call | solution.py:437
  50.7 1.8 constant_dynamic-update-slice_fusion.2
  52.4 7.6 %all-to-all-start.1 = ((f32[16,8,1152]{2,1,0:T(8,128)}), f32[16,8,1152]{2,1,0:T(8,128)S(1)}, u32[]{:S(2)}, u32[]{:S(2)}) async-start(f32[16,8,1152]{2,1,0:T(8,128)} %bitcast.39), calls=%async_computation.1 | async-start | bytes 1179648 | tf_op jit(solution)/shard_map/all_to_all | solution.py:557
  61.7 2.6 collective-permute-start.3
  64.3 11.0 %local_kernel.1 = (f32[512,1024]{1,0:T(8,128)}, f32[512,1024]{1,0:T(8,128)}) custom-call(f32[512,1024]{1,0:T(8,128)} %get-tuple-element.68.value, f32[512,128]{1,0:T(8,128)} %get-tuple-element.69.in_map, f32[512,128]{1,0:T(8,128)} %get-tuple-element.70.out_map, f32[512,128]{1,0:T(8,128)} %get-tuple-element.71.step, f32[512,128]{1,0:T(8,128)} %get-tuple-element.72.decay, ...), custom_call_target="tpu_custom_call" | custom-call | tf_op jit(solution)/shard_map/local_kernel/pallas_call | solution.py:437
  77.7 3.2 %collective-permute-start.5 = (bf16[2,32,2048]{2,1,0:T(8,128)(2,1)S(1)}, bf16[2,32,2048]{2,1,0:T(8,128)(2,1)}, u32[]{:S(2)}, u32[]{:S(2)}) collective-permute-start(bf16[2,32,2048]{2,1,0:T(8,128)(2,1)S(1)} %slice.55), channel_id=1, source_target_pairs={{0,96},{1,97},{2,98},{3,99},{4,100},{5,101},{6,102},{7,103},{8,104... | collective-permute-start | bytes 786440 | tf_op jit(solution)/shard_map/ppermute | solution.py:471
  80.9 2.2 scan_forward.1
  84.2 1.4 collective-permute-done.4
  87.1 6.7 %all-to-all-start.2 = ((f32[16,8,1024]{2,1,0:T(8,128)}), f32[16,8,1024]{2,1,0:T(8,128)S(1)}, u32[]{:S(2)}, u32[]{:S(2)}) async-start(f32[16,8,1024]{2,1,0:T(8,128)} %get-tuple-element.83), calls=%async_computation.2 | async-start | bytes 1048576 | tf_op jit(solution)/shard_map/all_to_all | solution.py:573
  94.4 11.7 %all-to-all-done.2 = f32[16,8,1024]{2,1,0:T(8,128)S(1)} async-done(((f32[16,8,1024]{2,1,0:T(8,128)}), f32[16,8,1024]{2,1,0:T(8,128)S(1)}, u32[]{:S(2)}, u32[]{:S(2)}) %all-to-all-start.2) | async-done | bytes 524320 | tf_op jit(solution)/shard_map/all_to_all | solution.py:573
  107.0 19.5 %mix_kernel.1 = (bf16[1024,1024]{1,0:T(8,128)(2,1)}, bf16[512,1024]{1,0:T(8,128)(2,1)}, bf16[512,1024]{1,0:T(8,128)(2,1)}, f32[512,1024]{1,0:T(8,128)}, f32[512,...) custom-call(s32[2]{0:T(128)} %pad_add_fusion.place_ref, ...), custom_call_target="tpu_custom_call" | custom-call | tf_op jit(solution)/shard_map/mix_kernel/pallas_call | solution.py:437
  126.4 2.7 convolution_convert_fusion.1
  129.1 3.4 %broadcast_select_fusion = (bf16[1024,1024]{1,0:T(8,128)(2,1)}, bf16[1024,1024]{1,0:T(8,128)(2,1)}) fusion(bf16[1024,1024]{1,0:T(8,128)(2,1)S(1)} %convolution_convert_fusion.1, pred[]{:T(512)S(6)} %eq.57, bf16[512,1024]{1,0:T(8,128)(2,1)S(1)} %copy-done.12, bf16[1,512,1024]{2,1,0:T(8,128)(2,1)S(1)} %copy-done.9), kind=kOutput, calls=%fused_computation.2 | convolution fusion | flops 1076887552 | bytes 8388609 | tf_op jit(solution)/shard_map/dot_general | solution.py:497
  132.5 4.2 %all-to-all-start.3 = ((f32[16,8,1024]{2,1,0:T(8,128)}), f32[16,8,1024]{2,1,0:T(8,128)}, u32[]{:S(2)}, u32[]{:S(2)}) async-start(f32[16,8,1024]{2,1,0:T(8,128)} %bitcast.40), calls=%async_computation.3 | async-start | bytes 1048576 | tf_op jit(solution)/shard_map/all_to_all | solution.py:587
  136.7 18.1 %inner_kernel.1 = (f32[512,1024]{1,0:T(8,128)}, f32[512,256]{1,0:T(8,128)}, f32[32,128]{1,0:T(8,128)}) custom-call(bf16[128,1024]{1,0:T(8,128)(2,1)} %fusion.1.spread, f32[512,1024]{1,0:T(8,128)} %get-tuple-element.68.value, f32[512,128]{1,0:T(8,128)} %get-tuple-element.69.in_map, f32[512,128]{1,0:T(8,128)} %get-tuple-element.70.out_map, ...), custom_call_target="tpu_custom_call" | custom-call | tf_op jit(solution)/shard_map/inner_kernel/pallas_call | solution.py:437
  154.8 1.9 scan_backward.1
  156.7 7.2 %all-to-all-start.4 = ((f32[16,8,1024]{2,1,0:T(8,128)}), f32[16,8,1024]{2,1,0:T(8,128)}, u32[]{:S(2)}, u32[]{:S(2)}) async-start(f32[16,8,1024]{2,1,0:T(8,128)} %scan_backward.1), calls=%async_computation.4 | async-start | bytes 1048576 | tf_op jit(solution)/shard_map/all_to_all | solution.py:606
  163.9 1.3 copy-done.6
  165.2 4.0 %early_kernel.1 = bf16[128,8,1024]{2,1,0:T(8,128)(2,1)} custom-call(bf16[1024,1024]{1,0:T(8,128)(2,1)} %get-tuple-element.117.mine, bf16[1024,1024]{1,0:T(8,128)(2,1)} %copy-done.6), custom_call_target="tpu_custom_call" | custom-call | tf_op jit(solution)/shard_map/early_kernel/pallas_call | solution.py:437
  169.2 7.0 %all-to-all-done.4 = f32[16,8,1024]{2,1,0:T(8,128)} async-done(((f32[16,8,1024]{2,1,0:T(8,128)}), f32[16,8,1024]{2,1,0:T(8,128)}, u32[]{:S(2)}, u32[]{:S(2)}) %all-to-all-start.4) | async-done | bytes 524320 | tf_op jit(solution)/shard_map/all_to_all | solution.py:606
  176.3 6.3 %all-to-all-start.5 = ((bf16[128,8,1024]{2,1,0:T(8,128)(2,1)}), bf16[128,8,1024]{2,1,0:T(8,128)(2,1)S(1)}, u32[]{:S(2)}, u32[]{:S(2)}) async-start(bf16[128,8,1024]{2,1,0:T(8,128)(2,1)} %early_kernel.1), calls=%async_computation.5 | async-start | bytes 4194304 | tf_op jit(solution)/shard_map/all_to_all | solution.py:608
  182.5 24.2 %grad_kernel.1 = (bf16[512,1408]{1,0:T(8,128)(2,1)}, bf16[512,1024]{1,0:T(8,128)(2,1)}, f32[8,1024]{1,0:T(8,128)}, f32[8,128]{1,0:T(8,128)}) custom-call(bf16[512,1024]{1,0:T(8,128)(2,1)} %bitcast.36, f32[8,1024]{1,0:T(8,128)} %broadcast_in_dim.49.row, f32[512,128]{1,0:T(8,128)} %get-tuple-element.60.scale, f32[8,1024]{1,0:T(8,128)} %get-tuple-element.61.gains, ...), custom_call_target="tpu_custom_call" | custom-call | tf_op jit(solution)/shard_map/grad_kernel/pallas_call | solution.py:437
  206.8 3.2 %fusion.6.term = f32[1024,1408]{1,0:T(8,128)S(1)} fusion(bf16[512,1024]{1,0:T(8,128)(2,1)S(1)} %copy-done.3, bf16[512,1408]{1,0:T(8,128)(2,1)} %get-tuple-element.103), kind=kOutput, calls=%fused_computation.32 | convolution fusion | flops 1476395008 | bytes 8257536 | tf_op jit(solution)/shard_map/dot_general | solution.py:497
  210.0 2.5 copy-done
  213.9 2.0 collective-permute-done.8.other
  216.0 5.8 %late_kernel.1 = bf16[128,8,768]{2,1,0:T(8,128)(2,1)} custom-call(s32[1]{0:T(128)} %bitcast.3.core_ref, f32[1024,1408]{1,0:T(8,128)} %copy-done, bf16[1024,640]{1,0:T(8,128)(2,1)} %collective-permute-done.8.other, f32[8,1024]{1,0:T(8,128)} %get-tuple-element.104.sums, f32[8,1024]{1,0:T(8,128)} %get-tuple-element.100.sums_mix, f32[8,128]{1,0:T(8,128)} %concatenate.20.tile), custom_call_target="tpu_custom_call" | custom-call | tf_op jit(solution)/shard_map/late_kernel/pallas_call | solution.py:437
  221.8 34.1 %all_to_all.36.late = bf16[128,8,768]{2,1,0:T(8,128)(2,1)} all-to-all(bf16[128,8,768]{2,1,0:T(8,128)(2,1)} %late_kernel.1), channel_id=1, replica_groups=mesh['dp'=8,'ctx'=16] {'dp','ctx'}, dimensions={0} | all-to-all | bytes 3145728 | tf_op jit(solution)/shard_map/all_to_all | solution.py:640
  255.9 6.1 %sum_kernel.1 = (f32[8,2304]{1,0:T(8,128)}, f32[8,1024]{1,0:T(8,128)}, f32[8,128]{1,0:T(8,128)}, f32[8,128]{1,0:T(8,128)}) custom-call(bf16[128,8,1024]{2,1,0:T(8,128)(2,1)} %copy-done.1, bf16[128,8,768]{2,1,0:T(8,128)(2,1)} %all_to_all.36.late), custom_call_target="tpu_custom_call" | custom-call | tf_op jit(solution)/shard_map/sum_kernel/pallas_call | solution.py:437
  262.7 1.5 slice_reduce_fusion
  264.9 1.3 slice_bitcast_fusion
  (74 shorter events, 20.7 us)
Async XLA Ops:
  4.3 31.5 %copy-start.10 = (f32[3,16]{1,0:T(4,128)S(1)}, f32[3,16]{1,0:T(4,128)}, u32[]{:S(2)}) copy-start(f32[3,16]{1,0:T(4,128)} %param.17) | copy-start | bytes 580
  29.7 8.1 %copy-start.2 = (bf16[8,64,1408]{2,1,0:T(8,128)(2,1)}, bf16[8,64,1408]{2,1,0:T(8,128)(2,1)S(1)}, u32[]{:S(2)}) copy-start(bf16[8,64,1408]{2,1,0:T(8,128)(2,1)S(1)} %all_to_all.35.mine) | copy-start | bytes 4325380
  29.7 7.5 %collective-permute-start = (bf16[8,64,1408]{2,1,0:T(8,128)(2,1)S(1)}, bf16[8,64,1408]{2,1,0:T(8,128)(2,1)S(1)}, u32[]{:S(2)}, u32[]{:S(2)}) collective-permute-start(bf16[8,64,1408]{2,1,0:T(8,128)(2,1)S(1)} %all_to_all.35.mine), channel_id=1, source_target_pairs={{0,1},{1,0},{2,3},{3,2},{4,5},{5,4},{6,7},{7,6},{8,9},{9,8},{10,11... | collective-permute-start | bytes 4325384 | tf_op jit(solution)/shard_map/ppermute | solution.py:454
  34.0 16.5 %collective-permute-start.1 = (bf16[64,2048]{1,0:T(8,128)(2,1)}, bf16[64,2048]{1,0:T(8,128)(2,1)}, u32[]{:S(2)}, u32[]{:S(2)}) collective-permute-start(bf16[64,2048]{1,0:T(8,128)(2,1)} %slice_select_fusion.1), channel_id=1, source_target_pairs={{0,16},{1,17},{2,18},{3,19},{4,20},{5,21},{6,22},{7,23},{8,24},{9,... | collective-permute-start | bytes 786440 | tf_op jit(solution)/shard_map/ppermute | solution.py:471
  37.2 1.1 copy-start.8
  52.4 24.1 %all-to-all-start.1 = ((f32[16,8,1152]{2,1,0:T(8,128)}), f32[16,8,1152]{2,1,0:T(8,128)S(1)}, u32[]{:S(2)}, u32[]{:S(2)}) async-start(f32[16,8,1152]{2,1,0:T(8,128)} %bitcast.39), calls=%async_computation.1 | async-start | bytes 1179648 | tf_op jit(solution)/shard_map/all_to_all | solution.py:557
  61.0 15.5 %collective-permute-start.2 = (bf16[2,64,2048]{2,1,0:T(8,128)(2,1)S(1)}, bf16[2,64,2048]{2,1,0:T(8,128)(2,1)S(1)}, u32[]{:S(2)}, u32[]{:S(2)}) collective-permute-start(bf16[2,64,2048]{2,1,0:T(8,128)(2,1)S(1)} %pad_maximum_fusion.1), channel_id=1, source_target_pairs={{0,32},{1,33},{2,34},{3,35},{4,36},{5,37},{6,38},{7,39},{8,40},{9,... | collective-permute-start | bytes 1572872 | tf_op jit(solution)/shard_map/ppermute | solution.py:471
  61.7 14.8 %collective-permute-start.3 = (bf16[2,64,2048]{2,1,0:T(8,128)(2,1)S(1)}, bf16[2,64,2048]{2,1,0:T(8,128)(2,1)}, u32[]{:S(2)}, u32[]{:S(2)}) collective-permute-start(bf16[2,64,2048]{2,1,0:T(8,128)(2,1)S(1)} %pad_maximum_fusion.1), channel_id=1, source_target_pairs={{0,96},{1,97},{2,98},{3,99},{4,100},{5,101},{6,102},{7,103},{8,104... | collective-permute-start | bytes 1572872 | tf_op jit(solution)/shard_map/ppermute | solution.py:471
  76.5 4.4 %copy-start.5 = (f32[16,8,1152]{2,1,0:T(8,128)}, f32[16,8,1152]{2,1,0:T(8,128)S(1)}, u32[]{:S(2)}) copy-start(f32[16,8,1152]{2,1,0:T(8,128)S(1)} %all-to-all-done.1.pieces) | copy-start | bytes 1769476
  76.6 9.0 %collective-permute-start.4 = (bf16[2,32,2048]{2,1,0:T(8,128)(2,1)S(1)}, bf16[2,32,2048]{2,1,0:T(8,128)(2,1)S(1)}, u32[]{:S(2)}, u32[]{:S(2)}) collective-permute-start(bf16[2,32,2048]{2,1,0:T(8,128)(2,1)S(1)} %slice.54), channel_id=1, source_target_pairs={{0,32},{1,33},{2,34},{3,35},{4,36},{5,37},{6,38},{7,39},{8,40},{9,... | collective-permute-start | bytes 786440 | tf_op jit(solution)/shard_map/ppermute | solution.py:471
  77.7 8.2 %collective-permute-start.5 = (bf16[2,32,2048]{2,1,0:T(8,128)(2,1)S(1)}, bf16[2,32,2048]{2,1,0:T(8,128)(2,1)}, u32[]{:S(2)}, u32[]{:S(2)}) collective-permute-start(bf16[2,32,2048]{2,1,0:T(8,128)(2,1)S(1)} %slice.55), channel_id=1, source_target_pairs={{0,96},{1,97},{2,98},{3,99},{4,100},{5,101},{6,102},{7,103},{8,104... | collective-permute-start | bytes 786440 | tf_op jit(solution)/shard_map/ppermute | solution.py:471
  87.0 19.2 %copy-start.4 = (bf16[8,64,2048]{2,1,0:T(8,128)(2,1)}, bf16[8,64,2048]{2,1,0:T(8,128)(2,1)S(1)}, u32[]{:S(2)}) copy-start(bf16[8,64,2048]{2,1,0:T(8,128)(2,1)S(1)} %constant_dynamic-update-slice_fusion.mine) | copy-start | bytes 6291460
  87.0 19.2 %collective-permute-start.6 = (bf16[8,64,2048]{2,1,0:T(8,128)(2,1)S(1)}, bf16[8,64,2048]{2,1,0:T(8,128)(2,1)}, u32[]{:S(2)}, u32[]{:S(2)}) collective-permute-start(bf16[8,64,2048]{2,1,0:T(8,128)(2,1)S(1)} %constant_dynamic-update-slice_fusion.mine), channel_id=1, source_target_pairs={{0,1},{1,0},{2,3},{3,2},{4,5},{5,4},{6,7},{7,6},{8,9},{9,8},{10,11... | collective-permute-start | bytes 6291464 | tf_op jit(solution)/shard_map/ppermute | solution.py:454
  87.1 19.1 %all-to-all-start.2 = ((f32[16,8,1024]{2,1,0:T(8,128)}), f32[16,8,1024]{2,1,0:T(8,128)S(1)}, u32[]{:S(2)}, u32[]{:S(2)}) async-start(f32[16,8,1024]{2,1,0:T(8,128)} %get-tuple-element.83), calls=%async_computation.2 | async-start | bytes 1048576 | tf_op jit(solution)/shard_map/all_to_all | solution.py:573
  106.1 0.8 copy-start.7
  107.0 19.5 %copy-start.3 = (bf16[512,1024]{1,0:T(8,128)(2,1)S(1)}, bf16[512,1024]{1,0:T(8,128)(2,1)}, u32[]{:S(2)}) copy-start(bf16[512,1024]{1,0:T(8,128)(2,1)} %get-tuple-element.63.act_low) | copy-start | bytes 3145732
  126.4 2.7 %copy-start.9 = (bf16[1,512,1024]{2,1,0:T(8,128)(2,1)S(1)}, bf16[1,512,1024]{2,1,0:T(8,128)(2,1)}, u32[]{:S(2)}) copy-start(bf16[1,512,1024]{2,1,0:T(8,128)(2,1)} %param.11) | copy-start | bytes 3145732
  126.4 2.7 %copy-start.12 = (bf16[512,1024]{1,0:T(8,128)(2,1)S(1)}, bf16[512,1024]{1,0:T(8,128)(2,1)}, u32[]{:S(2)}) copy-start(bf16[512,1024]{1,0:T(8,128)(2,1)} %get-tuple-element.98) | copy-start | bytes 3145732
  132.5 31.4 %collective-permute-start.7 = (bf16[1024,1024]{1,0:T(8,128)(2,1)}, bf16[1024,1024]{1,0:T(8,128)(2,1)S(1)}, u32[]{:S(2)}, u32[]{:S(2)}) collective-permute-start(bf16[1024,1024]{1,0:T(8,128)(2,1)} %get-tuple-element.116), channel_id=1, source_target_pairs={{0,1},{1,0},{2,3},{3,2},{4,5},{5,4},{6,7},{7,6},{8,9},{9,8},{10,11... | collective-permute-start | bytes 6291464 | tf_op jit(solution)/shard_map/ppermute | solution.py:454
  132.5 22.3 %all-to-all-start.3 = ((f32[16,8,1024]{2,1,0:T(8,128)}), f32[16,8,1024]{2,1,0:T(8,128)}, u32[]{:S(2)}, u32[]{:S(2)}) async-start(f32[16,8,1024]{2,1,0:T(8,128)} %bitcast.40), calls=%async_computation.3 | async-start | bytes 1048576 | tf_op jit(solution)/shard_map/all_to_all | solution.py:587
  156.7 19.5 %all-to-all-start.4 = ((f32[16,8,1024]{2,1,0:T(8,128)}), f32[16,8,1024]{2,1,0:T(8,128)}, u32[]{:S(2)}, u32[]{:S(2)}) async-start(f32[16,8,1024]{2,1,0:T(8,128)} %scan_backward.1), calls=%async_computation.4 | async-start | bytes 1048576 | tf_op jit(solution)/shard_map/all_to_all | solution.py:606
  163.9 1.3 copy-start.6
  176.3 45.5 %all-to-all-start.5 = ((bf16[128,8,1024]{2,1,0:T(8,128)(2,1)}), bf16[128,8,1024]{2,1,0:T(8,128)(2,1)S(1)}, u32[]{:S(2)}, u32[]{:S(2)}) async-start(bf16[128,8,1024]{2,1,0:T(8,128)(2,1)} %early_kernel.1), calls=%async_computation.5 | async-start | bytes 4194304 | tf_op jit(solution)/shard_map/all_to_all | solution.py:608
  210.0 2.5 copy-start
  212.5 0.7 copy-start.11
  212.7 3.2 %collective-permute-start.8 = (bf16[1024,640]{1,0:T(8,128)(2,1)S(1)}, bf16[1024,640]{1,0:T(8,128)(2,1)}, u32[]{:S(2)}, u32[]{:S(2)}) collective-permute-start(bf16[1024,640]{1,0:T(8,128)(2,1)S(1)} %fusion), channel_id=1, source_target_pairs={{0,1},{1,0},{2,3},{3,2},{4,5},{5,4},{6,7},{7,6},{8,9},{9,8},{10,11... | collective-permute-start | bytes 3932168 | tf_op jit(solution)/shard_map/ppermute | solution.py:454
  221.8 34.1 %copy-start.1 = (bf16[128,8,1024]{2,1,0:T(8,128)(2,1)}, bf16[128,8,1024]{2,1,0:T(8,128)(2,1)S(1)}, u32[]{:S(2)}) copy-start(bf16[128,8,1024]{2,1,0:T(8,128)(2,1)S(1)} %all-to-all-done.5.early) | copy-start | bytes 6291460

commit v2 on v1

--- a/solution.py
+++ b/solution.py
@@ -38,9 +38,21 @@
     return high, mid, (rest - mid.astype(F32)).astype(LOW)
 
 
-def select_dot(x, chosen, dims=NN):
-    high, mid, low = thirds(x)
-    return dot(high, chosen, dims) + dot(mid, chosen, dims) + dot(low, chosen, dims)
+def expand(x, spread):
+    high = x.astype(LOW).astype(F32)
+    rest = x - high
+    mid = rest.astype(LOW).astype(F32)
+    parts = high + pltpu.roll(mid, 16, 1) + pltpu.roll(rest - mid, 32, 1)
+    return dot(parts.astype(LOW), spread)
+
+
+def by_heads(x, spread):
+    high, low = split(x)
+    return dot(high, spread, NT) + dot(low, spread, NT)
+
+
+def of_heads(x):
+    return jnp.where(iota(1, x.shape) < 16, x, 0.0)
 
 
 def select_left(chosen, x):
@@ -79,7 +91,8 @@
 def prep_kernel(
     core_ref, tok, row, mine, other, hp, spread,
     wide, act_low, scale, value, in_map, out_map, step_raw, step, decay, fresh, packed, gains,
-    state, total,
+    through,
+    state, total, rest,
 ):
     assemble(core_ref[0], mine, other, wide)
     small = wide[:, 1280:1408].astype(F32).T
@@ -88,38 +101,44 @@
     state[...] = jnp.zeros_like(state)
     total[...] = jnp.zeros_like(total)
     ones_low = (iota(0) >= iota(1)).astype(F32).astype(LOW)
-    used = iota(1) < 16
-
-    def body(c, carry):
+    chunks = tok.shape[0] // Q
+
+    def norm(c, carry):
         rows = rows_of(c)
         x = tok[rows, :].astype(F32) + row[0:1, :]
         factor = lax.rsqrt(jnp.mean(x * x, axis=1, keepdims=True) + epsilon)
-        low = (x * factor * gains[0:1, :]).astype(LOW)
-        act_low[rows, :] = low
+        act_low[rows, :] = (x * factor * gains[0:1, :]).astype(LOW)
         scale[rows, :] = jnp.broadcast_to(factor, (Q, 128))
-        value_c = dot(low, wide[:, :1024])
-        value[rows, :] = value_c
-        rest = dot(low, wide[:, 1024:1408])
-        in_c = rest[:, 0:128]
+        return carry
+
+    lax.fori_loop(0, chunks, norm, 0)
+    value[...] = dot(act_low[...], wide[:, :1024])
+    rest[...] = dot(act_low[...], wide[:, 1024:1408])
+
+    def body(c, carry):
+        rows = rows_of(c)
+        value_c = value[rows, :]
+        in_c = rest[rows, 0:128]
         in_map[rows, :] = in_c
-        out_map[rows, :] = rest[:, 128:256]
-        raw = jnp.where(used, rest[:, 256:384] + hp[0:1, :], 0.0)
+        out_map[rows, :] = rest[rows, 128:256]
+        raw = of_heads(rest[rows, 256:384] + hp[0:1, :])
         step_raw[rows, :] = raw
-        size = jnp.where(used, softplus(raw), 0.0)
+        size = of_heads(softplus(raw))
         step[rows, :] = size
         logs = select_left(ones_low, -jnp.exp(hp[1:2, :]) * size)
         decay[rows, :] = logs
         last = logs[Q - 1 : Q, :]
-        weight = select_dot(jnp.exp(last - logs) * size, spread[...])
+        weight = expand(jnp.exp(last - logs) * size, spread[...])
         activated = value_c * sigmoid(value_c)
         fresh_c = dot3(in_c.T, weight * activated)
         fresh[rows, :] = fresh_c
-        through = select_dot(jnp.broadcast_to(jnp.exp(last), (8, 128)), spread[...])[0:1, :]
-        state[...] = through * state[...] + fresh_c
+        kept = expand(of_heads(jnp.broadcast_to(jnp.exp(last), (8, 128))), spread[...])
+        through[eight(c), :] = kept
+        state[...] = kept[0:1, :] * state[...] + fresh_c
         total[...] = total[...] + last
         return carry
 
-    lax.fori_loop(0, tok.shape[0] // Q, body, 0)
+    lax.fori_loop(0, chunks, body, 0)
     packed[:, :1024] = state[...]
     packed[:, 1024:1152] = jnp.broadcast_to(jnp.exp(total[0:1, :]), (128, 128))
 
@@ -127,7 +146,7 @@
 def scan_forward(pieces, spread, carried, decays):
     count = pieces.shape[0]
     rates = jnp.concatenate([pieces[j, 0:1, 1024:1152] for j in range(count)], axis=0)
-    decays[...] = select_dot(rates, spread[...])
+    decays[...] = expand(of_heads(rates), spread[...])
     held = jnp.zeros((8, 1024), F32)
     for j in range(count):
         carried[j] = held
@@ -161,10 +180,14 @@
 
 
 def widen(row, spread):
-    return select_dot(jnp.broadcast_to(row, (8, 128)), spread)[0:1, :]
-
-
-def local_kernel(value, in_map, out_map, step, decay, fresh, spread, y_local, states, ssd, scaled, held):
+    return expand(jnp.broadcast_to(row, (8, 128)), spread)[0:1, :]
+
+
+def eight(c):
+    return pl.ds(pl.multiple_of(8 * c, 8), 8)
+
+
+def local_kernel(value, in_map, out_map, step, decay, fresh, through, spread, y_local, states, ssd, scaled, held):
     held[...] = jnp.zeros_like(held)
 
     def body(c, carry):
@@ -173,8 +196,8 @@
         logs = decay[rows, :]
         logs_t = logs.T
         value_c = value[rows, :]
-        scaled[...] = select_dot(step[rows, :], spread[...]) * (value_c * sigmoid(value_c))
-        reach = select_dot(jnp.exp(logs), spread[...])
+        scaled[...] = expand(step[rows, :], spread[...]) * (value_c * sigmoid(value_c))
+        reach = expand(of_heads(jnp.exp(logs)), spread[...])
         out_c = out_map[rows, :]
         scores = dot3(out_c, in_map[rows, :], NT)
         for pair in range(8):
@@ -183,18 +206,14 @@
             weighted = jnp.concatenate([one * scores, two * scores], axis=1)
             ssd[:, lanes] = dot3(weighted, by_head(scaled[:, lanes], 0))
         y_local[rows, :] = ssd[...] + reach * dot3(out_c, held[...])
-        through = widen(jnp.exp(logs[Q - 1 : Q, :]), spread[...])
-        held[...] = through * held[...] + fresh[rows, :]
+        held[...] = through[eight(c), :][0:1, :] * held[...] + fresh[rows, :]
         return carry
 
     lax.fori_loop(0, value.shape[0] // Q, body, 0)
 
 
-def mix_kernel(
-    place_ref, act_low, mine, other, grad_out, value, out_map, decay, y_local,
-    states_local, state_in, gains, hp, spread,
-    gate_whole, mixed, grad_gate, grad_ssd, out_dot, adjoint, adjoint_local, states, sums,
-    out_whole, base,
+def gate_kernel(
+    place_ref, act_low, mine, other, grad_out, gate_whole, gate, grad_mixed, out_whole
 ):
     core, group = place_ref[0], place_ref[1]
     half = mine.shape[1]
@@ -204,6 +223,16 @@
             rows = pl.ds(pl.multiple_of(start + turn * half, half), half)
             gate_whole[rows, :] = block[i, :, :1024]
             out_whole[rows, :] = block[i, :, 1024:]
+    gate[...] = dot(act_low[...], gate_whole[...])
+    grad_mixed[...] = dot(grad_out[...], out_whole[...], NT)
+
+
+def mix_kernel(
+    gate_all, grad_mixed_all, value, out_map, decay, y_local, states_local, state_in, gains, hp,
+    through, spread,
+    mixed, grad_gate, grad_ssd, out_dot, adjoint, adjoint_local, states, sums,
+    base,
+):
     base[...] = jnp.ones_like(base)
     adjoint_local[...] = jnp.zeros_like(adjoint_local)
     sums[...] = jnp.zeros_like(sums)
@@ -217,12 +246,12 @@
         logs = decay[rows, :]
         value_c = value[rows, :]
         activated = value_c * sigmoid(value_c)
-        reach = select_dot(jnp.exp(logs), spread[...])
+        reach = expand(of_heads(jnp.exp(logs)), spread[...])
         out_c = out_map[rows, :]
         y_state = y_local[rows, :] + reach * dot3(out_c, entering)
         y = y_state + skip * activated
-        gate = dot(act_low[rows, :], gate_whole[...])
-        grad_mixed = dot(grad_out[rows, :], out_whole[...], NT)
+        gate = gate_all[rows, :]
+        grad_mixed = grad_mixed_all[rows, :]
         sig = sigmoid(gate)
         silu = gate * sig
         gated = y * silu
@@ -238,18 +267,18 @@
         grad_y = grad_gated * silu
         grad_ssd[rows, :] = grad_y
         sums[1:2, :] = sums[1:2, :] + jnp.sum(grad_y * activated, axis=0, keepdims=True)
-        out_dot[rows, :] = select_dot(grad_y * y_state, spread[...], NT)
+        out_dot[rows, :] = by_heads(grad_y * y_state, spread[...])
         adjoint_c = dot3(out_c.T, reach * grad_y)
         adjoint[rows, :] = adjoint_c
         adjoint_local[...] = adjoint_local[...] + before * adjoint_c
-        base[0:1, :] = before * widen(jnp.exp(logs[Q - 1 : Q, :]), spread[...])
-        return carry
-
-    lax.fori_loop(0, act_low.shape[0] // Q, body, 0)
+        base[0:1, :] = before * through[eight(c), :][0:1, :]
+        return carry
+
+    lax.fori_loop(0, value.shape[0] // Q, body, 0)
 
 
 def inner_kernel(
-    spread, value, in_map, out_map, step, decay, fresh, states, grad_ssd, adjoint,
+    spread, value, in_map, out_map, step, decay, fresh, through_all, states, grad_ssd, adjoint,
     grad_scaled, grad_maps, crossings,
     held, scaled,
 ):
@@ -264,17 +293,17 @@
         last = logs[Q - 1 : Q, :]
         in_c = in_map[rows, :]
         out_c = out_map[rows, :]
-        through = widen(jnp.exp(last), spread[...])
+        through = through_all[eight(c), :][0:1, :]
         state_end = through * states[rows, :] + fresh[rows, :]
         crossing = jnp.sum(held[...] * state_end, axis=0, keepdims=True)
-        crossing = select_dot(jnp.broadcast_to(crossing, (8, 1024)), spread[...], NT)
-        crossings[pl.ds(pl.multiple_of(8 * c, 8), 8), :] = crossing
+        crossing = by_heads(jnp.broadcast_to(crossing, (8, 1024)), spread[...])
+        crossings[eight(c), :] = crossing
         value_c = value[rows, :]
-        scaled[...] = select_dot(step[rows, :], spread[...]) * (value_c * sigmoid(value_c))
-        tail = select_dot(jnp.exp(last - logs), spread[...])
+        scaled[...] = expand(step[rows, :], spread[...]) * (value_c * sigmoid(value_c))
+        tail = expand(of_heads(jnp.exp(last - logs)), spread[...])
         grad_scaled[rows, :] = tail * dot3(in_c, held[...])
         grad_in = dot3(tail * scaled[...], held[...], NT)
-        reach = select_dot(jnp.exp(logs), spread[...])
+        reach = expand(of_heads(jnp.exp(logs)), spread[...])
         grad_out_map = dot3(reach * grad_ssd[rows, :], states[rows, :], NT)
         scores = dot3(in_c, out_c, NT)
         grad_scores = jnp.zeros((Q, Q), F32)
@@ -296,15 +325,15 @@
 
 def grad_kernel(
     tok, row, scale, gains, hp, spread, wide, gate_whole, grad_gate, value, in_map,
-    step_raw, step, decay, fresh, states, grad_ssd, out_dot, grad_inner, grad_maps, crossings,
-    adjoint_out, sums_mix,
-    grad_wide, tokens_grad, sums, heads,
-    after,
+    step_raw, step, decay, fresh, through_all, states, grad_ssd, out_dot, grad_inner, grad_maps,
+    crossings, adjoint_out, sums_mix,
+    grad_wide, grad_steps, tokens_grad, sums, heads,
+    after, grad_act_all,
 ):
     after[...] = jnp.ones_like(after)
     sums[...] = jnp.zeros_like(sums)
     heads[...] = jnp.zeros_like(heads)
-    heads[2:3, :] = select_dot(sums_mix[...], spread[...], NT)[1:2, :]
+    heads[2:3, :] = by_heads(sums_mix[...], spread[...])[1:2, :]
     skip = widen(hp[2:3, :], spread[...])
     chunks = tok.shape[0] // Q
     ones_up = (iota(1) >= iota(0)).astype(F32).astype(LOW)
@@ -315,20 +344,20 @@
         logs = decay[rows, :]
         last = logs[Q - 1 : Q, :]
         size = step[rows, :]
-        through = widen(jnp.exp(last), spread[...])
+        through = through_all[eight(c), :][0:1, :]
         leaving = after[0:1, :] * adjoint_out[...]
         state_end = through * states[rows, :] + fresh[rows, :]
         crossing = jnp.sum(leaving * state_end, axis=0, keepdims=True)
-        crossing = select_dot(jnp.broadcast_to(crossing, (8, 1024)), spread[...], NT)
-        crossing = (crossing + crossings[pl.ds(pl.multiple_of(8 * c, 8), 8), :])[0:1, :]
+        crossing = by_heads(jnp.broadcast_to(crossing, (8, 1024)), spread[...])
+        crossing = (crossing + crossings[eight(c), :])[0:1, :]
         value_c = value[rows, :]
         sig = sigmoid(value_c)
         activated = value_c * sig
-        size_wide = select_dot(size, spread[...])
-        tail = select_dot(jnp.exp(last - logs), spread[...])
+        size_wide = expand(size, spread[...])
+        tail = expand(of_heads(jnp.exp(last - logs)), spread[...])
         grad_scaled = grad_inner[rows, :] + tail * dot3(in_map[rows, :], leaving)
         grad_in = grad_maps[rows, 0:128] + dot3(tail * (size_wide * activated), leaving, NT)
-        per_step = select_dot(activated * grad_scaled, spread[...], NT)
+        per_step = by_heads(activated * grad_scaled, spread[...])
         grad_logs = out_dot[rows, :] - size * per_step
         grad_rate = select_left(ones_up, grad_logs) + crossing
         speed = jnp.exp(hp[1:2, :])
@@ -342,11 +371,20 @@
         grad_wide[rows, 0:1024] = (grad_act_c * sig * (1.0 + value_c * (1.0 - sig))).astype(LOW)
         grad_wide[rows, 1024:1152] = grad_in.astype(LOW)
         grad_wide[rows, 1152:1280] = grad_maps[rows, 128:256].astype(LOW)
-        grad_wide[rows, 1280:1408] = grad_raw.astype(LOW)
+        grad_steps[rows, :] = grad_raw.astype(LOW)
         after[0:1, :] = after[0:1, :] * through
-        grad_act = dot(grad_wide[rows, :], wide[...], NT) + dot(
-            grad_gate[rows, :], gate_whole[...], NT
-        )
+        return carry
+
+    lax.fori_loop(0, chunks, body, 0)
+    grad_act_all[...] = (
+        dot(grad_wide[...], wide[:, :1280], NT)
+        + dot(grad_steps[...], wide[:, 1280:1408], NT)
+        + dot(grad_gate[...], gate_whole[...], NT)
+    )
+
+    def finish(c, carry):
+        rows = rows_of(c)
+        grad_act = grad_act_all[rows, :]
         factor = scale[rows, 0:1]
         normed = (tok[rows, :].astype(F32) + row[0:1, :]) * factor
         sums[0:1, :] = sums[0:1, :] + jnp.sum(grad_act * normed, axis=0, keepdims=True)
@@ -357,7 +395,7 @@
         sums[1:2, :] = sums[1:2, :] + jnp.sum(grad_input, axis=0, keepdims=True)
         return carry
 
-    lax.fori_loop(0, chunks, body, 0)
+    lax.fori_loop(0, chunks, finish, 0)
 
 
 def early_kernel(mine, other, packed):
@@ -370,7 +408,7 @@
     lax.fori_loop(0, mine.shape[0] // Q, body, 0)
 
 
-def late_kernel(core_ref, term, other, sums, sums_mix, tile, packed, across, columns):
+def late_kernel(core_ref, term, steps, other, sums, sums_mix, tile, packed, across, columns):
     across[...] = jnp.zeros_like(across)
     across[16:17, :] = sums[0:1, :]
     across[17:18, :] = sums_mix[0:1, :]
@@ -381,10 +419,11 @@
 
     def body(j, carry):
         rows = pl.ds(pl.multiple_of(j * Q, Q), Q)
-        mine = jnp.where(first, term[rows, 0:640], term[rows, 640:1280])
-        both = mine.astype(LOW).astype(F32) + other[rows, :].astype(F32)
+        low, high = term[rows, 0:640].astype(F32), term[rows, 640:1280].astype(F32)
+        mine = jnp.where(first, low, high)
+        both = mine.astype(F32) + other[rows, :].astype(F32)
         packed[pl.ds(j * 16, 16), :, 0:640] = both.reshape(16, 8, 640).astype(LOW)
-        extra = (term[rows, 1280:1408] + columns[rows, :]).reshape(16, 8, 128)
+        extra = (steps[rows, :] + columns[rows, :]).reshape(16, 8, 128)
         extra = (extra + tile[...][None]).reshape(Q, 128)
         coarse = extra.astype(LOW).astype(F32)
         fine = pltpu.roll(extra - coarse, 64, 1)
@@ -395,16 +434,27 @@
     lax.fori_loop(0, term.shape[0] // Q, body, 0)
 
 
-def sum_kernel(grad_scale, early, late, input_grad, output_grad, small, table):
+def early_sum(early, gates, outs):
+    gates[...] = jnp.zeros_like(gates)
+    outs[...] = jnp.zeros_like(outs)
+
+    def body(j, carry):
+        gates[...] += early[2 * j].astype(F32)
+        outs[...] += early[2 * j + 1].astype(F32)
+        return carry
+
+    lax.fori_loop(0, early.shape[0] // 2, body, 0, unroll=4)
+
+
+def late_sum(grad_scale, late, gates, outs, input_grad, output_grad, small, table):
     input_grad[...] = jnp.zeros_like(input_grad)
-    output_grad[...] = jnp.zeros_like(output_grad)
     small[...] = jnp.zeros_like(small)
     table[...] = jnp.zeros_like(table)
-    lane = lax.broadcasted_iota(jnp.int32, (8, 128), 1).astype(F32)
+    input_grad[:, 0:1024] = gates[...] * grad_scale
+    output_grad[...] = outs[...] * grad_scale
+    lane = iota(1, (8, 128)).astype(F32)
 
     def body(j, carry):
-        input_grad[:, 0:1024] += early[2 * j].astype(F32)
-        output_grad[...] += early[2 * j + 1].astype(F32)
         input_grad[:, 1024:1664] += late[2 * j, :, 0:640].astype(F32)
         input_grad[:, 1664:2304] += late[2 * j + 1, :, 0:640].astype(F32)
         for k in range(2):
@@ -414,9 +464,10 @@
             table[...] += jnp.where(lane == parts[:, 25:26], parts[:, 24:25], 0.0)
         return carry
 
-    lax.fori_loop(0, early.shape[0] // 2, body, 0, unroll=4)
-    for out in (input_grad, output_grad, small, table):
-        out[...] = out[...] * grad_scale
+    lax.fori_loop(0, late.shape[0] // 2, body, 0, unroll=4)
+    input_grad[:, 1024:2304] = input_grad[:, 1024:2304] * grad_scale
+    small[...] = small[...] * grad_scale
+    table[...] = table[...] * grad_scale
 
 
 def at_origin(rank, *unused):
@@ -436,7 +487,7 @@
     ]
     return pl.pallas_call(
         kernel,
-        name=getattr(kernel, "__name__", "sum_kernel"),
+        name=getattr(kernel, "__name__", "late_sum"),
         out_shape=[jax.ShapeDtypeStruct(shape, dtype) for shape, dtype in outs],
         grid_spec=pltpu.PrefetchScalarGridSpec(
             num_scalar_prefetch=scalars,
@@ -471,11 +522,9 @@
     return lax.ppermute(value, ALL, [(i, to(i) % count) for i in range(count)])
 
 
-def ring_near(shard):
-    half = shard.shape[0] // 2
+def ring_near(mine):
     slots = lax.axis_size("ctx")
-    mine = jnp.where(on_first_core(), shard[:half], shard[half:])
-    return mine, moved(mine, lambda i: i ^ slots)
+    return moved(mine, lambda i: i ^ slots)
 
 
 def ring_sides(mine, near):
@@ -520,7 +569,8 @@
     row = lax.dynamic_slice(session_table, (session_ids[0], 0), (1, 1024)).astype(F32)
     row = jnp.broadcast_to(row, (8, 1024))
     params = jnp.pad(head_params, ((0, 5), (0, 112)))
-    spread = (jnp.arange(1024)[None, :] // 64 == jnp.arange(128)[:, None]).astype(LOW)
+    copies = jnp.arange(128)[:, None]
+    spread = ((jnp.arange(1024)[None, :] // 64 == copies % 16) & (copies < 48)).astype(LOW)
     shard = jnp.concatenate(
         [
             input_weight[:, 1024:],
@@ -532,10 +582,10 @@
         axis=1,
     )
     mine, other = gather_rows(shard)
-    mine, rest = lax.optimization_barrier(
-        (mine, jnp.concatenate([input_weight[:, :1024], output_weight], axis=1))
-    )
-    rest_half, near = ring_near(rest)
+    rest = jnp.concatenate([input_weight[:, :1024], output_weight], axis=1)
+    rest_half = jnp.where(first, rest[:64], rest[64:])
+    mine, rest_half = lax.optimization_barrier((mine, rest_half))
+    near = ring_near(rest_half)
     place = jnp.stack([core[0], lax.axis_index("dp").astype(jnp.int32) // 2])
     seq = (bins, 1024)
     lane = (bins, 128)
@@ -545,19 +595,19 @@
         (
             ((1024, 1408), LOW), (seq, LOW), (lane, F32), (seq, F32), (lane, F32), (lane, F32),
             (lane, F32), (lane, F32), (lane, F32), (seq, F32), ((128, 1152), F32), ((8, 1024), F32),
+            ((bins // Q * 8, 1024), F32),
         ),
-        (((128, 1024), F32), ((8, 128), F32)),
+        (((128, 1024), F32), ((8, 128), F32), ((bins, 384), F32)),
         1,
     )
-    wide, act_low, scale, value, in_map, out_map, step_raw, step, decay, fresh, packed, gains = (
-        prepared
-    )
+    wide, act_low, scale, value, in_map, out_map, step_raw, step = prepared[:8]
+    decay, fresh, packed, gains, through = prepared[8:]
     near, packed = lax.optimization_barrier((near, packed))
     pair, lower, upper = ring_sides(rest_half, near)
     pieces = lax.all_to_all(packed.reshape(slots, 8, 1152), "ctx", 0, 0)
     y_local, states_local = run(
         local_kernel,
-        (value, in_map, out_map, step, decay, fresh, spread),
+        (value, in_map, out_map, step, decay, fresh, through, spread),
         ((seq, F32), (seq, F32)),
         (((Q, 1024), F32), ((Q, 1024), F32), ((128, 1024), F32)),
     )
@@ -571,55 +621,64 @@
     rest_mine = jnp.concatenate([pair, upper, far, lower], axis=0)
     rest_other = core_partner(rest_mine)
     state_in = lax.all_to_all(carried, "ctx", 0, 0).reshape(128, 1024)
-    gate_whole, mixed, grad_gate, grad_ssd, out_dot, adjoint, adjoint_local, states, sums_mix = run(
+    gate_whole, gate, grad_mixed = run(
+        gate_kernel,
+        (place, act_low, rest_mine, rest_other, grad_out),
+        (((1024, 1024), LOW), (seq, F32), (seq, F32)),
+        (((1024, 1024), LOW),),
+        1,
+    )
+    mixed, grad_gate, grad_ssd, out_dot, adjoint, adjoint_local, states, sums_mix = run(
         mix_kernel,
         (
-            place, act_low, rest_mine, rest_other, grad_out, value, out_map, decay, y_local,
-            states_local, state_in, gains, params, spread,
+            gate, grad_mixed, value, out_map, decay, y_local, states_local, state_in, gains,
+            params, through, spread,
         ),
         (
-            ((1024, 1024), LOW), (seq, LOW), (seq, LOW), (seq, F32), (lane, F32), (seq, F32),
-            ((128, 1024), F32), (seq, F32), ((8, 1024), F32),
+            (seq, LOW), (seq, LOW), (seq, F32), (lane, F32), (seq, F32), ((128, 1024), F32),
+            (seq, F32), ((8, 1024), F32),
         ),
-        (((1024, 1024), LOW), ((8, 1024), F32)),
-        1,
+        (((8, 1024), F32),),
     )
     pieces = lax.all_to_all(adjoint_local.reshape(slots, 8, 1024), "ctx", 0, 0)
+    grad_inner, grad_maps, crossings = run(
+        inner_kernel,
+        (
+            spread, value, in_map, out_map, step, decay, fresh, through, states, grad_ssd,
+            adjoint,
+        ),
+        ((seq, F32), ((bins, 256), F32), ((bins // Q * 8, 128), F32)),
+        (((128, 1024), F32), ((Q, 1024), F32)),
+    )
+    pieces, grad_inner = lax.optimization_barrier((pieces, grad_inner))
+    (carried,) = run(scan_backward, (pieces, decays), (((slots, 8, 1024), F32),))
+    carried, mixed, early_gate = lax.optimization_barrier((carried, mixed, grad_gate))
     term_output = column_dot(mixed, grad_out).astype(LOW)
-    term_gates = column_dot(act_low, grad_gate).astype(LOW)
+    term_gates = column_dot(act_low, early_gate).astype(LOW)
     received = core_partner(jnp.where(first, term_output, term_gates))
     (early,) = run(
         early_kernel,
         (jnp.where(first, term_gates, term_output), received),
         (((devices, 8, 1024), LOW),),
     )
-    grad_inner, grad_maps, crossings = run(
-        inner_kernel,
-        (
-            spread, value, in_map, out_map, step, decay, fresh, states, grad_ssd, adjoint,
-        ),
-        ((seq, F32), ((bins, 256), F32), ((bins // Q * 8, 128), F32)),
-        (((128, 1024), F32), ((Q, 1024), F32)),
-    )
-    pieces, grad_inner = lax.optimization_barrier((pieces, grad_inner))
-    (carried,) = run(scan_backward, (pieces, decays), (((slots, 8, 1024), F32),))
     adjoint_out = lax.all_to_all(carried, "ctx", 0, 0).reshape(128, 1024)
     adjoint_out, early = lax.optimization_barrier((adjoint_out, early))
     early_got = lax.all_to_all(early, ALL, 0, 0)
-    grad_wide, tokens_grad, sums, heads = run(
+    grad_wide, grad_steps, tokens_grad, sums, heads = run(
         grad_kernel,
         (
             tok, row, scale, gains, params, spread, wide, gate_whole, grad_gate, value, in_map,
-            step_raw, step, decay, fresh, states, grad_ssd, out_dot, grad_inner, grad_maps,
-            crossings, adjoint_out, sums_mix,
+            step_raw, step, decay, fresh, through, states, grad_ssd, out_dot, grad_inner,
+            grad_maps, crossings, adjoint_out, sums_mix,
         ),
-        (((bins, 1408), LOW), (seq, LOW), ((8, 1024), F32), ((8, 128), F32)),
-        (((8, 1024), F32),),
-    )
-    term_wide = column_dot(act_low, grad_wide)
-    received = core_partner(
-        jnp.where(first, term_wide[:, 640:1280], term_wide[:, :640]).astype(LOW)
-    )
+        (
+            ((bins, 1280), LOW), (lane, LOW), (seq, LOW), ((8, 1024), F32), ((8, 128), F32),
+        ),
+        (((8, 1024), F32), (seq, F32)),
+    )
+    term_low = column_dot(act_low, grad_wide).astype(LOW)
+    term_steps = column_dot(act_low, grad_steps)
+    received = core_partner(jnp.where(first, term_low[:, 640:], term_low[:, :640]))
     tile = jnp.concatenate(
         [
             jnp.zeros((8, 18), F32),
@@ -632,15 +691,16 @@
     )
     (late,) = run(
         late_kernel,
-        (core, term_wide, received, sums, sums_mix, tile),
+        (core, term_low, term_steps, received, sums, sums_mix, tile),
         (((devices, 8, 768), LOW),),
         (((128, 1024), F32), ((1024, 128), F32)),
         1,
     )
     late_got = lax.all_to_all(late, ALL, 0, 0)
+    gates, outs = run(early_sum, (early_got,), (((8, 1024), F32), ((8, 1024), F32)))
     input_grad, output_grad, totals, table = run(
-        functools.partial(sum_kernel, grad_scale),
-        (early_got, late_got),
+        functools.partial(late_sum, grad_scale),
+        (late_got, gates, outs),
         (((8, 2304), F32), ((8, 1024), F32), ((8, 128), F32), ((8, 128), F32)),
     )
     return (

time: 267 us -> 246 us (0.921)
  blocking collectives: 59.5 us -> 25.6 us
  waiting for transfers between devices: 23.7 us -> 37.1 us
  starting transfers between devices: 39.8 us -> 49.3 us
  Pallas kernels: 105 us -> 98.9 us
  other arithmetic: 7.98 us -> 4.68 us
    all_to_all x1 -> x0, blocking collectives: 34.1 us -> none  [per_device(): late_got = lax.all_to_all(late, ALL, 0, 0)]
    all_to_all x0 -> x1, waiting for transfers between devices: none -> 21.8 us  [per_device(): late_got = lax.all_to_all(late, ALL, 0, 0)]
    all_to_all x0 -> x1, starting transfers between devices: none -> 9.72 us  [per_device(): late_got = lax.all_to_all(late, ALL, 0, 0)]
    all_to_all x1, waiting for transfers between devices: 11.7 us -> 4.39 us  [per_device(): state_in = lax.all_to_all(carried, 'ctx', 0, 0).reshape(128, 1024)]
    pallas_call x10 -> x12, Pallas kernels: 105 us -> 98.9 us  [run(): pl.pallas_call(kernel, name=getattr(kernel, '__name__', 'late_sum'), out_...]
    dot_general x3 -> x4, matrix products: 9.22 us -> 10.4 us  [column_dot(): lax.dot_general(a, b, (((0,), (0,)), ((), ())), preferred_element_type=F32)]
    unnamed x28 -> x36, local copies, waits for them, and re-layouts: 7.28 us -> 7.09 us
  transfers between devices with their start and end apart: 14 -> 15, of which waited for: 6 -> 7; matrix products, arithmetic and copies ran while one was open for 5% -> 5% of each run, Pallas kernels for 30% -> 32%
where the time goes in v2:
time: 246 us; the launch traced here: 245 us
  Pallas kernels  98.9 us (40%)
  starting transfers between devices  49.3 us (20%)
  waiting for transfers between devices  37.1 us (15%)
  blocking collectives  25.6 us (10%)
  local copies, waits for them, and re-layouts  17.2 us (7%)
  matrix products  10.4 us (4%)
  other arithmetic  4.68 us (2%)
    pallas_call x12, Pallas kernels, run(): pl.pallas_call(kernel, name=getattr(kernel, '__name__', 'late_sum'), out_...  98.9 us
    all_to_all x1, blocking collectives, gather_rows(): lax.all_to_all(jnp.broadcast_to(mine[None], (count,) + mine.shape), 'dp',...  25.6 us
    all_to_all x1, waiting for transfers between devices, per_device(): late_got = lax.all_to_all(late, ALL, 0, 0)  21.8 us
    dot_general x4, matrix products, column_dot(): lax.dot_general(a, b, (((0,), (0,)), ((), ())), preferred_element_type=F32)  10.4 us
    all_to_all x1, starting transfers between devices, per_device(): late_got = lax.all_to_all(late, ALL, 0, 0)  9.72 us
    ppermute x5, starting transfers between devices, moved(): return lax.ppermute(value, ALL, [(i, to(i) % count) for i in range(count)])  7.73 us
    all_to_all x1, starting transfers between devices, per_device(): pieces = lax.all_to_all(packed.reshape(slots, 8, 1152), 'ctx', 0, 0)  7.61 us
    unnamed x36, local copies, waits for them, and re-layouts  7.09 us
  transfers between devices with their start and end apart: 15, of which 7 were waited for; matrix products, arithmetic and copies ran while one was open for 5% of the time, Pallas kernels for 32%

profile of v2, /device:TPU:0, one launch (start us, length us, event | category | flops | bytes accessed | tf_op | source)
XLA Modules:
  0.0 244.8 jit_solution(12712028311181515523)
XLA Ops:
  4.4 25.6 %all_to_all.35.mine = bf16[8,64,1408]{2,1,0:T(8,128)(2,1)S(1)} all-to-all(bf16[8,64,1408]{2,1,0:T(8,128)(2,1)S(1)} %broadcast_in_dim.54), channel_id=1, replica_groups=mesh['dp'=8,'ctx'=16] {'dp'}, dimensions={0} | all-to-all | bytes 2883584 | tf_op jit(solution)/shard_map/all_to_all | solution.py:516
  34.7 12.0 %prep_kernel.1 = (bf16[1024,1408]{1,0:T(8,128)(2,1)}, bf16[512,1024]{1,0:T(8,128)(2,1)}, f32[512,128]{1,0:T(8,128)}, f32[512,1024]{1,0:T(8,128)}, f32[512,128]{1...) custom-call(s32[1]{0:T(128)} %bitcast.3.core_ref, ...), custom_call_target="tpu_custom_call" | custom-call | tf_op jit(solution)/shard_map/prep_kernel/pallas_call | solution.py:488
  46.9 7.6 %all-to-all-start.1 = ((f32[16,8,1152]{2,1,0:T(8,128)}), f32[16,8,1152]{2,1,0:T(8,128)S(1)}, u32[]{:S(2)}, u32[]{:S(2)}) async-start(f32[16,8,1152]{2,1,0:T(8,128)} %bitcast.40), calls=%async_computation.1 | async-start | bytes 1179648 | tf_op jit(solution)/shard_map/all_to_all | solution.py:607
  55.2 2.6 %collective-permute-start.3 = (bf16[2,64,2048]{2,1,0:T(8,128)(2,1)S(1)}, bf16[2,64,2048]{2,1,0:T(8,128)(2,1)}, u32[]{:S(2)}, u32[]{:S(2)}) collective-permute-start(bf16[2,64,2048]{2,1,0:T(8,128)(2,1)S(1)} %pad_maximum_fusion), channel_id=1, source_target_pairs={{0,96},{1,97},{2,98},{3,99},{4,100},{5,101},{6,102},{7,103},{8,104... | collective-permute-start | bytes 1572872 | tf_op jit(solution)/shard_map/ppermute | solution.py:522
  57.8 10.1 %local_kernel.1 = (f32[512,1024]{1,0:T(8,128)}, f32[512,1024]{1,0:T(8,128)}) custom-call(f32[512,1024]{1,0:T(8,128)} %get-tuple-element.77.value, f32[512,128]{1,0:T(8,128)} %get-tuple-element.78.in_map, f32[512,128]{1,0:T(8,128)} %get-tuple-element.79.out_map, f32[512,128]{1,0:T(8,128)} %get-tuple-element.80.step, f32[512,128]{1,0:T(8,128)} %get-tuple-element.81.decay, ...), custom_call_target="tpu_custom_call" | custom-call | tf_op jit(solution)/shard_map/local_kernel/pallas_call | solution.py:488
  67.9 2.2 collective-permute-done.2
  71.2 3.2 %collective-permute-start.5 = (bf16[2,32,2048]{2,1,0:T(8,128)(2,1)S(1)}, bf16[2,32,2048]{2,1,0:T(8,128)(2,1)}, u32[]{:S(2)}, u32[]{:S(2)}) collective-permute-start(bf16[2,32,2048]{2,1,0:T(8,128)(2,1)S(1)} %slice.55), channel_id=1, source_target_pairs={{0,96},{1,97},{2,98},{3,99},{4,100},{5,101},{6,102},{7,103},{8,104... | collective-permute-start | bytes 786440 | tf_op jit(solution)/shard_map/ppermute | solution.py:522
  74.4 2.2 scan_forward.1
  77.8 1.4 collective-permute-done.4
  80.6 6.7 %all-to-all-start.2 = ((f32[16,8,1024]{2,1,0:T(8,128)}), f32[16,8,1024]{2,1,0:T(8,128)S(1)}, u32[]{:S(2)}, u32[]{:S(2)}) async-start(f32[16,8,1024]{2,1,0:T(8,128)} %get-tuple-element.96), calls=%async_computation.2 | async-start | bytes 1048576 | tf_op jit(solution)/shard_map/all_to_all | solution.py:623
  87.9 7.3 %gate_kernel.1 = (bf16[1024,1024]{1,0:T(8,128)(2,1)}, f32[512,1024]{1,0:T(8,128)}, f32[512,1024]{1,0:T(8,128)}) custom-call(s32[2]{0:T(128)} %pad_add_fusion.place_ref, bf16[512,1024]{1,0:T(8,128)(2,1)} %get-tuple-element.72.act_low, bf16[8,64,2048]{2,1,0:T(8,128)(2,1)} %copy-done.4, bf16[8,64,2048]{2,1,0:T(8,128)(2,1)} %collective-permute-done.6.other, ...), custom_call_target="tpu_custom_call" | custom-call | tf_op jit(solution)/shard_map/gate_kernel/pallas_call | solution.py:488
  95.2 4.4 %all-to-all-done.2 = f32[16,8,1024]{2,1,0:T(8,128)S(1)} async-done(((f32[16,8,1024]{2,1,0:T(8,128)}), f32[16,8,1024]{2,1,0:T(8,128)S(1)}, u32[]{:S(2)}, u32[]{:S(2)}) %all-to-all-start.2) | async-done | bytes 524320 | tf_op jit(solution)/shard_map/all_to_all | solution.py:623
  100.5 13.9 %mix_kernel.1 = (bf16[512,1024]{1,0:T(8,128)(2,1)}, bf16[512,1024]{1,0:T(8,128)(2,1)}, f32[512,1024]{1,0:T(8,128)}, f32[512,128]{1,0:T(8,128)}, f32[512,1024]{1,...) custom-call(f32[512,1024]{1,0:T(8,128)} %get-tuple-element.92.gate_all, ...), custom_call_target="tpu_custom_call" | custom-call | tf_op jit(solution)/shard_map/mix_kernel/pallas_call | solution.py:488
  114.4 3.8 %all-to-all-start.3 = ((f32[16,8,1024]{2,1,0:T(8,128)}), f32[16,8,1024]{2,1,0:T(8,128)S(1)}, u32[]{:S(2)}, u32[]{:S(2)}) async-start(f32[16,8,1024]{2,1,0:T(8,128)} %bitcast.41), calls=%async_computation.3 | async-start | bytes 1048576 | tf_op jit(solution)/shard_map/all_to_all | solution.py:643
  118.1 15.8 %inner_kernel.1 = (f32[512,1024]{1,0:T(8,128)}, f32[512,256]{1,0:T(8,128)}, f32[32,128]{1,0:T(8,128)}) custom-call(bf16[128,1024]{1,0:T(8,128)(2,1)} %and_convert_fusion.spread, f32[512,1024]{1,0:T(8,128)} %get-tuple-element.77.value, f32[512,128]{1,0:T(8,128)} %get-tuple-element.78.in_map, f32[512,128]{1,0:T(8,128)} %get-tuple-element.79.out_map, ...), custom_call_target="tpu_custom_call" | custom-call | tf_op jit(solution)/shard_map/inner_kernel/pallas_call | solution.py:488
  134.7 1.9 scan_backward.1
  136.6 1.3 convolution_convert_fusion.1
  138.2 3.4 %broadcast_select_fusion = (bf16[1024,1024]{1,0:T(8,128)(2,1)}, bf16[1024,1024]{1,0:T(8,128)(2,1)}) fusion(bf16[1024,1024]{1,0:T(8,128)(2,1)S(1)} %convolution_convert_fusion.1, pred[]{:T(512)S(6)} %eq.57, bf16[512,1024]{1,0:T(8,128)(2,1)S(1)} %copy-done.3, bf16[512,1024]{1,0:T(8,128)(2,1)S(1)} %copy-done.11), kind=kOutput, calls=%fused_computation.1 | convolution fusion | flops 1076887552 | bytes 8388609 | tf_op jit(solution)/shard_map/dot_general | solution.py:546
  141.7 7.0 %all-to-all-start.4 = ((f32[16,8,1024]{2,1,0:T(8,128)}), f32[16,8,1024]{2,1,0:T(8,128)S(1)}, u32[]{:S(2)}, u32[]{:S(2)}) async-start(f32[16,8,1024]{2,1,0:T(8,128)} %scan_backward.1), calls=%async_computation.4 | async-start | bytes 1048576 | tf_op jit(solution)/shard_map/all_to_all | solution.py:664
  148.7 1.3 copy-done.6
  150.0 4.1 %early_kernel.1 = bf16[128,8,1024]{2,1,0:T(8,128)(2,1)} custom-call(bf16[1024,1024]{1,0:T(8,128)(2,1)} %get-tuple-element.135.mine, bf16[1024,1024]{1,0:T(8,128)(2,1)} %copy-done.6), custom_call_target="tpu_custom_call" | custom-call | tf_op jit(solution)/shard_map/early_kernel/pallas_call | solution.py:488
  154.1 6.9 %all-to-all-done.4 = f32[16,8,1024]{2,1,0:T(8,128)S(1)} async-done(((f32[16,8,1024]{2,1,0:T(8,128)}), f32[16,8,1024]{2,1,0:T(8,128)S(1)}, u32[]{:S(2)}, u32[]{:S(2)}) %all-to-all-start.4) | async-done | bytes 524320 | tf_op jit(solution)/shard_map/all_to_all | solution.py:664
  161.8 6.6 %all-to-all-start.6 = ((bf16[128,8,1024]{2,1,0:T(8,128)(2,1)}), bf16[128,8,1024]{2,1,0:T(8,128)(2,1)}, u32[]{:S(2)}, u32[]{:S(2)}) async-start(bf16[128,8,1024]{2,1,0:T(8,128)(2,1)} %early_kernel.1), calls=%async_computation.6 | async-start | bytes 4194304 | tf_op jit(solution)/shard_map/all_to_all | solution.py:666
  168.4 18.5 %grad_kernel.1 = (bf16[512,1280]{1,0:T(8,128)(2,1)}, bf16[512,128]{1,0:T(8,128)(2,1)}, bf16[512,1024]{1,0:T(8,128)(2,1)}, f32[8,1024]{1,0:T(8,128)}, f32[8,128]{1,0:T(8,128)}) custom-call(bf16[512,1024]{1,0:T(8,128)(2,1)} %bitcast.36, f32[8,1024]{1,0:T(8,128)} %broadcast_in_dim.49.row, f32[512,128]{1,0:T(8,128)} %get-tuple-element.69.scale, ...), custom_call_target="tpu_custom_call" | custom-call | tf_op jit(solution)/shard_map/grad_kernel/pallas_call | solution.py:488
  187.0 3.2 %convolution_convert_fusion.term = bf16[1024,1280]{1,0:T(8,128)(2,1)S(1)} fusion(bf16[512,1024]{1,0:T(8,128)(2,1)} %get-tuple-element.72.act_low, bf16[512,1280]{1,0:T(8,128)(2,1)} %get-tuple-element.117), kind=kOutput, calls=%fused_computation | convolution fusion | flops 1343488000 | bytes 4980736 | tf_op jit(solution)/shard_map/dot_general | solution.py:546
  192.2 2.5 %fusion.6.steps = f32[1024,128]{1,0:T(8,128)} fusion(bf16[512,1024]{1,0:T(8,128)(2,1)} %get-tuple-element.72.act_low, bf16[512,128]{1,0:T(8,128)(2,1)S(1)} %copy-done.13), kind=kOutput, calls=%fused_computation.36 | convolution fusion | flops 134217728 | bytes 1703936 | tf_op jit(solution)/shard_map/dot_general | solution.py:546
  194.8 5.0 %late_kernel.1 = bf16[128,8,768]{2,1,0:T(8,128)(2,1)} custom-call(s32[1]{0:T(128)} %bitcast.3.core_ref, bf16[1024,1280]{1,0:T(8,128)(2,1)} %copy-done, f32[1024,128]{1,0:T(8,128)} %fusion.6.steps, bf16[1024,640]{1,0:T(8,128)(2,1)} %collective-permute-done.8.other, f32[8,1024]{1,0:T(8,128)} %get-tuple-element.119.sums, ...), custom_call_target="tpu_custom_call" | custom-call | tf_op jit(solution)/shard_map/late_kernel/pallas_call | solution.py:488
  199.8 9.7 %all-to-all-start.5 = ((bf16[128,8,768]{2,1,0:T(8,128)(2,1)}), bf16[128,8,768]{2,1,0:T(8,128)(2,1)S(1)}, u32[]{:S(2)}, u32[]{:S(2)}) async-start(bf16[128,8,768]{2,1,0:T(8,128)(2,1)} %late_kernel.1), calls=%async_computation.5 | async-start | bytes 3145728 | tf_op jit(solution)/shard_map/all_to_all | solution.py:699
  209.6 2.6 %early_sum.1 = (f32[8,1024]{1,0:T(8,128)}, f32[8,1024]{1,0:T(8,128)}) custom-call(bf16[128,8,1024]{2,1,0:T(8,128)(2,1)} %all-to-all-done.6.early), custom_call_target="tpu_custom_call" | custom-call | tf_op jit(solution)/shard_map/early_sum/pallas_call | solution.py:488
  212.2 21.8 %all-to-all-done.5.late = bf16[128,8,768]{2,1,0:T(8,128)(2,1)S(1)} async-done(((bf16[128,8,768]{2,1,0:T(8,128)(2,1)}), bf16[128,8,768]{2,1,0:T(8,128)(2,1)S(1)}, u32[]{:S(2)}, u32[]{:S(2)}) %all-to-all-start.5) | async-done | bytes 1572896 | tf_op jit(solution)/shard_map/all_to_all | solution.py:699
  235.2 5.5 %late_sum.1 = (f32[8,2304]{1,0:T(8,128)}, f32[8,1024]{1,0:T(8,128)}, f32[8,128]{1,0:T(8,128)}, f32[8,128]{1,0:T(8,128)}) custom-call(bf16[128,8,768]{2,1,0:T(8,128)(2,1)} %copy-done.1, f32[8,1024]{1,0:T(8,128)} %get-tuple-element.122.gates, f32[8,1024]{1,0:T(8,128)} %get-tuple-element.123.outs), custom_call_target="tpu_custom_call" | custom-call | tf_op jit(solution)/shard_map/late_sum/pallas_call | solution.py:488
  240.7 1.5 slice_reduce_fusion
  (88 shorter events, 21.6 us)
Async XLA Ops:
  4.3 27.0 %slice-start = ((bf16[128,2304]{1,0:T(8,128)(2,1)}), bf16[128,1024]{1,0:T(8,128)(2,1)S(1)}, s32[]{:S(2)}) async-start(bf16[128,2304]{1,0:T(8,128)(2,1)} %param.15), calls=%async_computation.7 | async-start | bytes 524288 | tf_op jit(solution)/shard_map/slice | solution.py:585
  4.3 27.0 %copy-start.12 = (bf16[128,1024]{1,0:T(8,128)(2,1)S(1)}, bf16[128,1024]{1,0:T(8,128)(2,1)}, u32[]{:S(2)}) copy-start(bf16[128,1024]{1,0:T(8,128)(2,1)} %param.19) | copy-start | bytes 786436
  4.3 28.2 %copy-start.14 = (f32[3,16]{1,0:T(4,128)S(1)}, f32[3,16]{1,0:T(4,128)}, u32[]{:S(2)}) copy-start(f32[3,16]{1,0:T(4,128)} %param.17) | copy-start | bytes 580
  29.9 4.8 %copy-start.2 = (bf16[8,64,1408]{2,1,0:T(8,128)(2,1)}, bf16[8,64,1408]{2,1,0:T(8,128)(2,1)S(1)}, u32[]{:S(2)}) copy-start(bf16[8,64,1408]{2,1,0:T(8,128)(2,1)S(1)} %all_to_all.35.mine) | copy-start | bytes 4325380
  29.9 4.1 %collective-permute-start = (bf16[8,64,1408]{2,1,0:T(8,128)(2,1)S(1)}, bf16[8,64,1408]{2,1,0:T(8,128)(2,1)}, u32[]{:S(2)}, u32[]{:S(2)}) collective-permute-start(bf16[8,64,1408]{2,1,0:T(8,128)(2,1)S(1)} %all_to_all.35.mine), channel_id=1, source_target_pairs={{0,1},{1,0},{2,3},{3,2},{4,5},{5,4},{6,7},{7,6},{8,9},{9,8},{10,11... | collective-permute-start | bytes 4325384 | tf_op jit(solution)/shard_map/ppermute | solution.py:505
  31.4 15.3 %collective-permute-start.1 = (bf16[64,2048]{1,0:T(8,128)(2,1)S(1)}, bf16[64,2048]{1,0:T(8,128)(2,1)S(1)}, u32[]{:S(2)}, u32[]{:S(2)}) collective-permute-start(bf16[64,2048]{1,0:T(8,128)(2,1)S(1)} %fusion.1), channel_id=1, source_target_pairs={{0,16},{1,17},{2,18},{3,19},{4,20},{5,21},{6,22},{7,23},{8,24},{9,... | collective-permute-start | bytes 786440 | tf_op jit(solution)/shard_map/ppermute | solution.py:522
  46.9 23.2 %all-to-all-start.1 = ((f32[16,8,1152]{2,1,0:T(8,128)}), f32[16,8,1152]{2,1,0:T(8,128)S(1)}, u32[]{:S(2)}, u32[]{:S(2)}) async-start(f32[16,8,1152]{2,1,0:T(8,128)} %bitcast.40), calls=%async_computation.1 | async-start | bytes 1179648 | tf_op jit(solution)/shard_map/all_to_all | solution.py:607
  54.5 15.5 %collective-permute-start.2 = (bf16[2,64,2048]{2,1,0:T(8,128)(2,1)S(1)}, bf16[2,64,2048]{2,1,0:T(8,128)(2,1)S(1)}, u32[]{:S(2)}, u32[]{:S(2)}) collective-permute-start(bf16[2,64,2048]{2,1,0:T(8,128)(2,1)S(1)} %pad_maximum_fusion), channel_id=1, source_target_pairs={{0,32},{1,33},{2,34},{3,35},{4,36},{5,37},{6,38},{7,39},{8,40},{9,... | collective-permute-start | bytes 1572872 | tf_op jit(solution)/shard_map/ppermute | solution.py:522
  55.2 14.8 %collective-permute-start.3 = (bf16[2,64,2048]{2,1,0:T(8,128)(2,1)S(1)}, bf16[2,64,2048]{2,1,0:T(8,128)(2,1)}, u32[]{:S(2)}, u32[]{:S(2)}) collective-permute-start(bf16[2,64,2048]{2,1,0:T(8,128)(2,1)S(1)} %pad_maximum_fusion), channel_id=1, source_target_pairs={{0,96},{1,97},{2,98},{3,99},{4,100},{5,101},{6,102},{7,103},{8,104... | collective-permute-start | bytes 1572872 | tf_op jit(solution)/shard_map/ppermute | solution.py:522
  70.0 4.4 %copy-start.5 = (f32[16,8,1152]{2,1,0:T(8,128)}, f32[16,8,1152]{2,1,0:T(8,128)S(1)}, u32[]{:S(2)}) copy-start(f32[16,8,1152]{2,1,0:T(8,128)S(1)} %all-to-all-done.1.pieces) | copy-start | bytes 1769476
  70.1 9.0 %collective-permute-start.4 = (bf16[2,32,2048]{2,1,0:T(8,128)(2,1)S(1)}, bf16[2,32,2048]{2,1,0:T(8,128)(2,1)S(1)}, u32[]{:S(2)}, u32[]{:S(2)}) collective-permute-start(bf16[2,32,2048]{2,1,0:T(8,128)(2,1)S(1)} %slice.54), channel_id=1, source_target_pairs={{0,32},{1,33},{2,34},{3,35},{4,36},{5,37},{6,38},{7,39},{8,40},{9,... | collective-permute-start | bytes 786440 | tf_op jit(solution)/shard_map/ppermute | solution.py:522
  71.2 8.2 %collective-permute-start.5 = (bf16[2,32,2048]{2,1,0:T(8,128)(2,1)S(1)}, bf16[2,32,2048]{2,1,0:T(8,128)(2,1)}, u32[]{:S(2)}, u32[]{:S(2)}) collective-permute-start(bf16[2,32,2048]{2,1,0:T(8,128)(2,1)S(1)} %slice.55), channel_id=1, source_target_pairs={{0,96},{1,97},{2,98},{3,99},{4,100},{5,101},{6,102},{7,103},{8,104... | collective-permute-start | bytes 786440 | tf_op jit(solution)/shard_map/ppermute | solution.py:522
  80.5 7.5 %copy-start.4 = (bf16[8,64,2048]{2,1,0:T(8,128)(2,1)}, bf16[8,64,2048]{2,1,0:T(8,128)(2,1)S(1)}, u32[]{:S(2)}) copy-start(bf16[8,64,2048]{2,1,0:T(8,128)(2,1)S(1)} %constant_dynamic-update-slice_fusion.mine) | copy-start | bytes 6291460
  80.5 7.4 %collective-permute-start.6 = (bf16[8,64,2048]{2,1,0:T(8,128)(2,1)S(1)}, bf16[8,64,2048]{2,1,0:T(8,128)(2,1)}, u32[]{:S(2)}, u32[]{:S(2)}) collective-permute-start(bf16[8,64,2048]{2,1,0:T(8,128)(2,1)S(1)} %constant_dynamic-update-slice_fusion.mine), channel_id=1, source_target_pairs={{0,1},{1,0},{2,3},{3,2},{4,5},{5,4},{6,7},{7,6},{8,9},{9,8},{10,11... | collective-permute-start | bytes 6291464 | tf_op jit(solution)/shard_map/ppermute | solution.py:505
  80.6 19.1 %all-to-all-start.2 = ((f32[16,8,1024]{2,1,0:T(8,128)}), f32[16,8,1024]{2,1,0:T(8,128)S(1)}, u32[]{:S(2)}, u32[]{:S(2)}) async-start(f32[16,8,1024]{2,1,0:T(8,128)} %get-tuple-element.96), calls=%async_computation.2 | async-start | bytes 1048576 | tf_op jit(solution)/shard_map/all_to_all | solution.py:623
  99.6 0.8 copy-start.7
  114.4 19.6 %all-to-all-start.3 = ((f32[16,8,1024]{2,1,0:T(8,128)}), f32[16,8,1024]{2,1,0:T(8,128)S(1)}, u32[]{:S(2)}, u32[]{:S(2)}) async-start(f32[16,8,1024]{2,1,0:T(8,128)} %bitcast.41), calls=%async_computation.3 | async-start | bytes 1048576 | tf_op jit(solution)/shard_map/all_to_all | solution.py:643
  118.1 18.5 %copy-start.10 = (bf16[1,512,1024]{2,1,0:T(8,128)(2,1)S(1)}, bf16[1,512,1024]{2,1,0:T(8,128)(2,1)}, u32[]{:S(2)}) copy-start(bf16[1,512,1024]{2,1,0:T(8,128)(2,1)} %param.11) | copy-start | bytes 3145732
  118.1 18.5 %copy-start.16 = (bf16[512,1024]{1,0:T(8,128)(2,1)S(1)}, bf16[512,1024]{1,0:T(8,128)(2,1)}, u32[]{:S(2)}) copy-start(bf16[512,1024]{1,0:T(8,128)(2,1)} %get-tuple-element.113) | copy-start | bytes 3145732
  136.6 1.3 copy-start.3
  136.6 1.5 copy-start.11
  141.6 7.1 %collective-permute-start.7 = (bf16[1024,1024]{1,0:T(8,128)(2,1)}, bf16[1024,1024]{1,0:T(8,128)(2,1)S(1)}, u32[]{:S(2)}, u32[]{:S(2)}) collective-permute-start(bf16[1024,1024]{1,0:T(8,128)(2,1)} %get-tuple-element.134), channel_id=1, source_target_pairs={{0,1},{1,0},{2,3},{3,2},{4,5},{5,4},{6,7},{7,6},{8,9},{9,8},{10,11... | collective-permute-start | bytes 6291464 | tf_op jit(solution)/shard_map/ppermute | solution.py:505
  141.7 19.3 %all-to-all-start.4 = ((f32[16,8,1024]{2,1,0:T(8,128)}), f32[16,8,1024]{2,1,0:T(8,128)S(1)}, u32[]{:S(2)}, u32[]{:S(2)}) async-start(f32[16,8,1024]{2,1,0:T(8,128)} %scan_backward.1), calls=%async_computation.4 | async-start | bytes 1048576 | tf_op jit(solution)/shard_map/all_to_all | solution.py:664
  148.7 1.3 copy-start.6
  161.0 0.8 copy-start.8
  161.8 38.0 %all-to-all-start.6 = ((bf16[128,8,1024]{2,1,0:T(8,128)(2,1)}), bf16[128,8,1024]{2,1,0:T(8,128)(2,1)}, u32[]{:S(2)}, u32[]{:S(2)}) async-start(bf16[128,8,1024]{2,1,0:T(8,128)(2,1)} %early_kernel.1), calls=%async_computation.6 | async-start | bytes 4194304 | tf_op jit(solution)/shard_map/all_to_all | solution.py:666
  190.2 4.5 %copy-start = (bf16[1024,1280]{1,0:T(8,128)(2,1)}, bf16[1024,1280]{1,0:T(8,128)(2,1)S(1)}, u32[]{:S(2)}) copy-start(bf16[1024,1280]{1,0:T(8,128)(2,1)S(1)} %convolution_convert_fusion.term) | copy-start | bytes 7864324
  190.2 1.2 copy-start.15
  190.2 2.0 copy-start.13
  191.4 3.4 %collective-permute-start.8 = (bf16[1024,640]{1,0:T(8,128)(2,1)}, bf16[1024,640]{1,0:T(8,128)(2,1)}, u32[]{:S(2)}, u32[]{:S(2)}) collective-permute-start(bf16[1024,640]{1,0:T(8,128)(2,1)} %slice_select_fusion), channel_id=1, source_target_pairs={{0,1},{1,0},{2,3},{3,2},{4,5},{5,4},{6,7},{7,6},{8,9},{9,8},{10,11... | collective-permute-start | bytes 3932168 | tf_op jit(solution)/shard_map/ppermute | solution.py:505
  199.8 34.2 %all-to-all-start.5 = ((bf16[128,8,768]{2,1,0:T(8,128)(2,1)}), bf16[128,8,768]{2,1,0:T(8,128)(2,1)S(1)}, u32[]{:S(2)}, u32[]{:S(2)}) async-start(bf16[128,8,768]{2,1,0:T(8,128)(2,1)} %late_kernel.1), calls=%async_computation.5 | async-start | bytes 3145728 | tf_op jit(solution)/shard_map/all_to_all | solution.py:699
  234.0 1.2 copy-start.1
  (1 other events, 0.8 us)

commit v3 on v2

--- a/solution.py
+++ b/solution.py
@@ -188,10 +188,12 @@
 
 
 def local_kernel(value, in_map, out_map, step, decay, fresh, through, spread, y_local, states, ssd, scaled, held):
-    held[...] = jnp.zeros_like(held)
+    @pl.when(pl.program_id(0) == 0)
+    def start():
+        held[...] = jnp.zeros_like(held)
 
     def body(c, carry):
-        rows = rows_of(c)
+        rows = slice(None)
         states[rows, :] = held[...]
         logs = decay[rows, :]
         logs_t = logs.T
@@ -209,7 +211,7 @@
         held[...] = through[eight(c), :][0:1, :] * held[...] + fresh[rows, :]
         return carry
 
-    lax.fori_loop(0, value.shape[0] // Q, body, 0)
+    body(pl.program_id(0), 0)
 
 
 def gate_kernel(
@@ -233,13 +235,16 @@
     mixed, grad_gate, grad_ssd, out_dot, adjoint, adjoint_local, states, sums,
     base,
 ):
-    base[...] = jnp.ones_like(base)
-    adjoint_local[...] = jnp.zeros_like(adjoint_local)
-    sums[...] = jnp.zeros_like(sums)
+    @pl.when(pl.program_id(0) == 0)
+    def start():
+        base[...] = jnp.ones_like(base)
+        adjoint_local[...] = jnp.zeros_like(adjoint_local)
+        sums[...] = jnp.zeros_like(sums)
+
     skip = widen(hp[2:3, :], spread[...])
 
     def body(c, carry):
-        rows = rows_of(c)
+        rows = slice(None)
         before = base[0:1, :]
         entering = before * state_in[...]
         states[rows, :] = states_local[rows, :] + entering
@@ -274,7 +279,7 @@
         base[0:1, :] = before * through[eight(c), :][0:1, :]
         return carry
 
-    lax.fori_loop(0, value.shape[0] // Q, body, 0)
+    body(pl.program_id(0), 0)
 
 
 def inner_kernel(
@@ -282,12 +287,15 @@
     grad_scaled, grad_maps, crossings,
     held, scaled,
 ):
-    held[...] = jnp.zeros_like(held)
-    chunks = value.shape[0] // Q
+    chunks = pl.num_programs(0)
+
+    @pl.when(pl.program_id(0) == 0)
+    def start():
+        held[...] = jnp.zeros_like(held)
 
     def body(i, carry):
         c = chunks - 1 - i
-        rows = rows_of(c)
+        rows = slice(None)
         logs = decay[rows, :]
         logs_t = logs.T
         last = logs[Q - 1 : Q, :]
@@ -320,27 +328,36 @@
         held[...] = adjoint[rows, :] + through * held[...]
         return carry
 
-    lax.fori_loop(0, chunks, body, 0)
+    body(pl.program_id(0), 0)
 
 
 def grad_kernel(
-    tok, row, scale, gains, hp, spread, wide, gate_whole, grad_gate, value, in_map,
+    tok_c, row, scale, gains, hp, spread, wide_c, gate_whole_c, grad_gate_c, value, in_map,
     step_raw, step, decay, fresh, through_all, states, grad_ssd, out_dot, grad_inner, grad_maps,
     crossings, adjoint_out, sums_mix,
     grad_wide, grad_steps, tokens_grad, sums, heads,
-    after, grad_act_all,
+    after, grad_act_all, tok, wide, gate_whole, grad_gate,
 ):
-    after[...] = jnp.ones_like(after)
-    sums[...] = jnp.zeros_like(sums)
-    heads[...] = jnp.zeros_like(heads)
-    heads[2:3, :] = by_heads(sums_mix[...], spread[...])[1:2, :]
+    @pl.when(pl.program_id(0) == 0)
+    def start():
+        after[...] = jnp.ones_like(after)
+        sums[...] = jnp.zeros_like(sums)
+        heads[...] = jnp.zeros_like(heads)
+        heads[2:3, :] = by_heads(sums_mix[...], spread[...])[1:2, :]
+
     skip = widen(hp[2:3, :], spread[...])
-    chunks = tok.shape[0] // Q
+    chunks = scale.shape[0] // Q
     ones_up = (iota(1) >= iota(0)).astype(F32).astype(LOW)
 
     def body(i, carry):
         c = chunks - 1 - i
-        rows = rows_of(c)
+        rows = slice(None)
+        place = rows_of(c)
+        part = pl.ds(pl.multiple_of(c * 256, 256), 256)
+        tok[place, :] = tok_c[...]
+        grad_gate[place, :] = grad_gate_c[...]
+        wide[part, :] = wide_c[...]
+        gate_whole[part, :] = gate_whole_c[...]
         logs = decay[rows, :]
         last = logs[Q - 1 : Q, :]
         size = step[rows, :]
@@ -368,34 +385,37 @@
             grad_rate * (speed * size), axis=0, keepdims=True
         )
         grad_act_c = size_wide * grad_scaled + skip * grad_ssd[rows, :]
-        grad_wide[rows, 0:1024] = (grad_act_c * sig * (1.0 + value_c * (1.0 - sig))).astype(LOW)
-        grad_wide[rows, 1024:1152] = grad_in.astype(LOW)
-        grad_wide[rows, 1152:1280] = grad_maps[rows, 128:256].astype(LOW)
-        grad_steps[rows, :] = grad_raw.astype(LOW)
+        grad_wide[place, 0:1024] = (grad_act_c * sig * (1.0 + value_c * (1.0 - sig))).astype(LOW)
+        grad_wide[place, 1024:1152] = grad_in.astype(LOW)
+        grad_wide[place, 1152:1280] = grad_maps[rows, 128:256].astype(LOW)
+        grad_steps[place, :] = grad_raw.astype(LOW)
         after[0:1, :] = after[0:1, :] * through
         return carry
 
-    lax.fori_loop(0, chunks, body, 0)
-    grad_act_all[...] = (
-        dot(grad_wide[...], wide[:, :1280], NT)
-        + dot(grad_steps[...], wide[:, 1280:1408], NT)
-        + dot(grad_gate[...], gate_whole[...], NT)
-    )
-
-    def finish(c, carry):
-        rows = rows_of(c)
-        grad_act = grad_act_all[rows, :]
-        factor = scale[rows, 0:1]
-        normed = (tok[rows, :].astype(F32) + row[0:1, :]) * factor
-        sums[0:1, :] = sums[0:1, :] + jnp.sum(grad_act * normed, axis=0, keepdims=True)
-        grad_normed = grad_act * gains[0:1, :]
-        mean = jnp.mean(grad_normed * normed, axis=1, keepdims=True)
-        grad_input = factor * (grad_normed - normed * mean)
-        tokens_grad[rows, :] = grad_input.astype(LOW)
-        sums[1:2, :] = sums[1:2, :] + jnp.sum(grad_input, axis=0, keepdims=True)
-        return carry
-
-    lax.fori_loop(0, chunks, finish, 0)
+    body(pl.program_id(0), 0)
+
+    @pl.when(pl.program_id(0) == chunks - 1)
+    def end():
+        grad_act_all[...] = (
+            dot(grad_wide[...], wide[:, :1280], NT)
+            + dot(grad_steps[...], wide[:, 1280:1408], NT)
+            + dot(grad_gate[...], gate_whole[...], NT)
+        )
+
+        def finish(c, carry):
+            rows = rows_of(c)
+            grad_act = grad_act_all[rows, :]
+            factor = scale[rows, 0:1]
+            normed = (tok[rows, :].astype(F32) + row[0:1, :]) * factor
+            sums[0:1, :] = sums[0:1, :] + jnp.sum(grad_act * normed, axis=0, keepdims=True)
+            grad_normed = grad_act * gains[0:1, :]
+            mean = jnp.mean(grad_normed * normed, axis=1, keepdims=True)
+            grad_input = factor * (grad_normed - normed * mean)
+            tokens_grad[rows, :] = grad_input.astype(LOW)
+            sums[1:2, :] = sums[1:2, :] + jnp.sum(grad_input, axis=0, keepdims=True)
+            return carry
+
+        lax.fori_loop(0, chunks, finish, 0)
 
 
 def early_kernel(mine, other, packed):
@@ -474,26 +494,26 @@
     return (0,) * rank
 
 
-def run(kernel, args, outs, scratch=(), scalars=0):
-    specs = [
-        pl.BlockSpec(
-            arg.shape, functools.partial(at_origin, arg.ndim), pipeline_mode=pl.Buffered(1)
-        )
-        for arg in args[scalars:]
-    ]
-    out_specs = [
-        pl.BlockSpec(shape, functools.partial(at_origin, len(shape)), pipeline_mode=pl.Buffered(1))
-        for shape, _ in outs
-    ]
+def run(kernel, args, outs, scratch=(), scalars=0, chunks=1, parts=(), out_parts=(), back=False):
+    def spec(shape, divided):
+        if not divided:
+            return pl.BlockSpec(
+                shape, functools.partial(at_origin, len(shape)), pipeline_mode=pl.Buffered(1)
+            )
+        block = (shape[0] // chunks,) + tuple(shape[1:])
+        if back:
+            return pl.BlockSpec(block, lambda i: (chunks - 1 - i, 0))
+        return pl.BlockSpec(block, lambda i: (i, 0))
+
     return pl.pallas_call(
         kernel,
         name=getattr(kernel, "__name__", "late_sum"),
         out_shape=[jax.ShapeDtypeStruct(shape, dtype) for shape, dtype in outs],
         grid_spec=pltpu.PrefetchScalarGridSpec(
             num_scalar_prefetch=scalars,
-            grid=(1,),
-            in_specs=specs,
-            out_specs=out_specs,
+            grid=(chunks,),
+            in_specs=[spec(arg.shape, i in parts) for i, arg in enumerate(args[scalars:])],
+            out_specs=[spec(shape, i in out_parts) for i, (shape, _) in enumerate(outs)],
             scratch_shapes=[pltpu.VMEM(shape, dtype) for shape, dtype in scratch],
         ),
         compiler_params=pltpu.CompilerParams(vmem_limit_bytes=60 << 20),
@@ -610,6 +630,9 @@
         (value, in_map, out_map, step, decay, fresh, through, spread),
         ((seq, F32), (seq, F32)),
         (((Q, 1024), F32), ((Q, 1024), F32), ((128, 1024), F32)),
+        chunks=bins // Q,
+        parts=range(6),
+        out_parts=range(2),
     )
     pieces, y_local, lower, upper = lax.optimization_barrier((pieces, y_local, lower, upper))
     far_low, far_high = ring_far(lower, upper)
@@ -639,6 +662,9 @@
             (seq, F32), ((8, 1024), F32),
         ),
         (((8, 1024), F32),),
+        chunks=bins // Q,
+        parts=range(7),
+        out_parts=(0, 1, 2, 3, 4, 6),
     )
     pieces = lax.all_to_all(adjoint_local.reshape(slots, 8, 1024), "ctx", 0, 0)
     grad_inner, grad_maps, crossings = run(
@@ -649,6 +675,10 @@
         ),
         ((seq, F32), ((bins, 256), F32), ((bins // Q * 8, 128), F32)),
         (((128, 1024), F32), ((Q, 1024), F32)),
+        chunks=bins // Q,
+        parts=(1, 2, 3, 4, 5, 6, 8, 9, 10),
+        out_parts=range(2),
+        back=True,
     )
     pieces, grad_inner = lax.optimization_barrier((pieces, grad_inner))
     (carried,) = run(scan_backward, (pieces, decays), (((slots, 8, 1024), F32),))
@@ -674,7 +704,13 @@
         (
             ((bins, 1280), LOW), (lane, LOW), (seq, LOW), ((8, 1024), F32), ((8, 128), F32),
         ),
-        (((8, 1024), F32), (seq, F32)),
+        (
+            ((8, 1024), F32), (seq, F32), (seq, LOW), ((1024, 1408), LOW), ((1024, 1024), LOW),
+            (seq, LOW),
+        ),
+        chunks=bins // Q,
+        parts=(0, 6, 7, 8, 9, 10, 11, 12, 13, 14, 16, 17, 18, 19, 20),
+        back=True,
     )
     term_low = column_dot(act_low, grad_wide).astype(LOW)
     term_steps = column_dot(act_low, grad_steps)

time: 246 us -> 238 us (0.967)
  Pallas kernels: 98.9 us -> 88.7 us
  waiting for transfers between devices: 37.1 us -> 40 us
    pallas_call x12, Pallas kernels: 98.9 us -> 88.7 us  [run(): pl.pallas_call(kernel, name=getattr(kernel, '__name__', 'late_sum'), out_...]
  transfers between devices with their start and end apart: 15 -> 15, of which waited for: 7 -> 8; matrix products, arithmetic and copies ran while one was open for 5% -> 6% of each run, Pallas kernels for 32% -> 30%
where the time goes in v3:
time: 238 us; the launch traced here: 236 us
  Pallas kernels  88.7 us (37%)
  starting transfers between devices  48.1 us (20%)
  waiting for transfers between devices  40 us (17%)
  blocking collectives  25.6 us (11%)
  local copies, waits for them, and re-layouts  17.2 us (7%)
  matrix products  10.4 us (4%)
  other arithmetic  4.68 us (2%)
    pallas_call x12, Pallas kernels, run(): pl.pallas_call(kernel, name=getattr(kernel, '__name__', 'late_sum'), out_...  88.7 us
    all_to_all x1, blocking collectives, gather_rows(): lax.all_to_all(jnp.broadcast_to(mine[None], (count,) + mine.shape), 'dp',...  25.6 us
    all_to_all x1, waiting for transfers between devices, per_device(): late_got = lax.all_to_all(late, ALL, 0, 0)  21.8 us
    dot_general x4, matrix products, column_dot(): lax.dot_general(a, b, (((0,), (0,)), ((), ())), preferred_element_type=F32)  10.4 us
    all_to_all x1, starting transfers between devices, per_device(): late_got = lax.all_to_all(late, ALL, 0, 0)  8.51 us
    ppermute x5, starting transfers between devices, moved(): return lax.ppermute(value, ALL, [(i, to(i) % count) for i in range(count)])  7.73 us
    all_to_all x1, starting transfers between devices, per_device(): pieces = lax.all_to_all(packed.reshape(slots, 8, 1152), 'ctx', 0, 0)  7.61 us
    unnamed x36, local copies, waits for them, and re-layouts  7.08 us
  transfers between devices with their start and end apart: 15, of which 8 were waited for; matrix products, arithmetic and copies ran while one was open for 6% of the time, Pallas kernels for 30%

profile of v3, /device:TPU:0, one launch (start us, length us, event | category | flops | bytes accessed | tf_op | source)
XLA Modules:
  0.0 236.4 jit_solution(283079936088782806)
XLA Ops:
  4.4 25.6 %all_to_all.35.mine = bf16[8,64,1408]{2,1,0:T(8,128)(2,1)S(1)} all-to-all(bf16[8,64,1408]{2,1,0:T(8,128)(2,1)S(1)} %broadcast_in_dim.54), channel_id=1, replica_groups=mesh['dp'=8,'ctx'=16] {'dp'}, dimensions={0} | all-to-all | bytes 2883584 | tf_op jit(solution)/shard_map/all_to_all | solution.py:536
  34.7 12.0 %prep_kernel.1 = (bf16[1024,1408]{1,0:T(8,128)(2,1)}, bf16[512,1024]{1,0:T(8,128)(2,1)}, f32[512,128]{1,0:T(8,128)}, f32[512,1024]{1,0:T(8,128)}, f32[512,128]{1...) custom-call(s32[1]{0:T(128)} %bitcast.3.core_ref, ...), custom_call_target="tpu_custom_call" | custom-call | tf_op jit(solution)/shard_map/prep_kernel/pallas_call | solution.py:508
  46.9 7.6 %all-to-all-start.1 = ((f32[16,8,1152]{2,1,0:T(8,128)}), f32[16,8,1152]{2,1,0:T(8,128)S(1)}, u32[]{:S(2)}, u32[]{:S(2)}) async-start(f32[16,8,1152]{2,1,0:T(8,128)} %bitcast.40), calls=%async_computation.1 | async-start | bytes 1179648 | tf_op jit(solution)/shard_map/all_to_all | solution.py:627
  55.2 2.6 %collective-permute-start.3 = (bf16[2,64,2048]{2,1,0:T(8,128)(2,1)S(1)}, bf16[2,64,2048]{2,1,0:T(8,128)(2,1)}, u32[]{:S(2)}, u32[]{:S(2)}) collective-permute-start(bf16[2,64,2048]{2,1,0:T(8,128)(2,1)S(1)} %pad_maximum_fusion), channel_id=1, source_target_pairs={{0,96},{1,97},{2,98},{3,99},{4,100},{5,101},{6,102},{7,103},{8,104... | collective-permute-start | bytes 1572872 | tf_op jit(solution)/shard_map/ppermute | solution.py:542
  57.8 8.3 %local_kernel.1 = (f32[512,1024]{1,0:T(8,128)}, f32[512,1024]{1,0:T(8,128)}) custom-call(f32[512,1024]{1,0:T(8,128)} %get-tuple-element.77.value, f32[512,128]{1,0:T(8,128)} %get-tuple-element.78.in_map, f32[512,128]{1,0:T(8,128)} %get-tuple-element.79.out_map, f32[512,128]{1,0:T(8,128)} %get-tuple-element.80.step, f32[512,128]{1,0:T(8,128)} %get-tuple-element.81.decay, ...), custom_call_target="tpu_custom_call" | custom-call | tf_op jit(solution)/shard_map/local_kernel/pallas_call | solution.py:508
  66.2 3.9 %collective-permute-done.2 = bf16[2,64,2048]{2,1,0:T(8,128)(2,1)S(1)} collective-permute-done((bf16[2,64,2048]{2,1,0:T(8,128)(2,1)S(1)}, bf16[2,64,2048]{2,1,0:T(8,128)(2,1)S(1)}, u32[]{:S(2)}, u32[]{:S(2)}) %collective-permute-start.2) | collective-permute-done | bytes 524320 | tf_op jit(solution)/shard_map/ppermute | solution.py:542
  71.2 3.2 %collective-permute-start.5 = (bf16[2,32,2048]{2,1,0:T(8,128)(2,1)S(1)}, bf16[2,32,2048]{2,1,0:T(8,128)(2,1)}, u32[]{:S(2)}, u32[]{:S(2)}) collective-permute-start(bf16[2,32,2048]{2,1,0:T(8,128)(2,1)S(1)} %slice.55), channel_id=1, source_target_pairs={{0,96},{1,97},{2,98},{3,99},{4,100},{5,101},{6,102},{7,103},{8,104... | collective-permute-start | bytes 786440 | tf_op jit(solution)/shard_map/ppermute | solution.py:542
  74.4 2.2 scan_forward.1
  77.8 1.4 collective-permute-done.4
  80.6 6.7 %all-to-all-start.2 = ((f32[16,8,1024]{2,1,0:T(8,128)}), f32[16,8,1024]{2,1,0:T(8,128)S(1)}, u32[]{:S(2)}, u32[]{:S(2)}) async-start(f32[16,8,1024]{2,1,0:T(8,128)} %get-tuple-element.96), calls=%async_computation.2 | async-start | bytes 1048576 | tf_op jit(solution)/shard_map/all_to_all | solution.py:646
  87.9 7.3 %gate_kernel.1 = (bf16[1024,1024]{1,0:T(8,128)(2,1)}, f32[512,1024]{1,0:T(8,128)}, f32[512,1024]{1,0:T(8,128)}) custom-call(s32[2]{0:T(128)} %pad_add_fusion.place_ref, bf16[512,1024]{1,0:T(8,128)(2,1)} %get-tuple-element.72.act_low, bf16[8,64,2048]{2,1,0:T(8,128)(2,1)} %copy-done.4, bf16[8,64,2048]{2,1,0:T(8,128)(2,1)} %collective-permute-done.6.other, ...), custom_call_target="tpu_custom_call" | custom-call | tf_op jit(solution)/shard_map/gate_kernel/pallas_call | solution.py:508
  95.2 4.4 %all-to-all-done.2 = f32[16,8,1024]{2,1,0:T(8,128)S(1)} async-done(((f32[16,8,1024]{2,1,0:T(8,128)}), f32[16,8,1024]{2,1,0:T(8,128)S(1)}, u32[]{:S(2)}, u32[]{:S(2)}) %all-to-all-start.2) | async-done | bytes 524320 | tf_op jit(solution)/shard_map/all_to_all | solution.py:646
  100.5 10.9 %mix_kernel.1 = (bf16[512,1024]{1,0:T(8,128)(2,1)}, bf16[512,1024]{1,0:T(8,128)(2,1)}, f32[512,1024]{1,0:T(8,128)}, f32[512,128]{1,0:T(8,128)}, f32[512,1024]{1,...) custom-call(f32[512,1024]{1,0:T(8,128)} %get-tuple-element.92.gate_all, ...), custom_call_target="tpu_custom_call" | custom-call | tf_op jit(solution)/shard_map/mix_kernel/pallas_call | solution.py:508
  111.4 3.8 %all-to-all-start.3 = ((f32[16,8,1024]{2,1,0:T(8,128)}), f32[16,8,1024]{2,1,0:T(8,128)S(1)}, u32[]{:S(2)}, u32[]{:S(2)}) async-start(f32[16,8,1024]{2,1,0:T(8,128)} %bitcast.41), calls=%async_computation.3 | async-start | bytes 1048576 | tf_op jit(solution)/shard_map/all_to_all | solution.py:669
  115.2 13.2 %inner_kernel.1 = (f32[512,1024]{1,0:T(8,128)}, f32[512,256]{1,0:T(8,128)}, f32[32,128]{1,0:T(8,128)}) custom-call(bf16[128,1024]{1,0:T(8,128)(2,1)} %and_convert_fusion.spread, f32[512,1024]{1,0:T(8,128)} %get-tuple-element.77.value, f32[512,128]{1,0:T(8,128)} %get-tuple-element.78.in_map, f32[512,128]{1,0:T(8,128)} %get-tuple-element.79.out_map, ...), custom_call_target="tpu_custom_call" | custom-call | tf_op jit(solution)/shard_map/inner_kernel/pallas_call | solution.py:508
  129.1 1.9 scan_backward.1
  131.1 1.3 convolution_convert_fusion.1
  132.6 3.4 %broadcast_select_fusion = (bf16[1024,1024]{1,0:T(8,128)(2,1)}, bf16[1024,1024]{1,0:T(8,128)(2,1)}) fusion(bf16[1024,1024]{1,0:T(8,128)(2,1)S(1)} %convolution_convert_fusion.1, pred[]{:T(512)S(6)} %eq.57, bf16[512,1024]{1,0:T(8,128)(2,1)S(1)} %copy-done.3, bf16[512,1024]{1,0:T(8,128)(2,1)S(1)} %copy-done.11), kind=kOutput, calls=%fused_computation.1 | convolution fusion | flops 1076887552 | bytes 8388609 | tf_op jit(solution)/shard_map/dot_general | solution.py:566
  136.1 7.0 %all-to-all-start.4 = ((f32[16,8,1024]{2,1,0:T(8,128)}), f32[16,8,1024]{2,1,0:T(8,128)S(1)}, u32[]{:S(2)}, u32[]{:S(2)}) async-start(f32[16,8,1024]{2,1,0:T(8,128)} %scan_backward.1), calls=%async_computation.4 | async-start | bytes 1048576 | tf_op jit(solution)/shard_map/all_to_all | solution.py:694
  143.1 1.3 copy-done.6
  144.4 4.1 %early_kernel.1 = bf16[128,8,1024]{2,1,0:T(8,128)(2,1)} custom-call(bf16[1024,1024]{1,0:T(8,128)(2,1)} %get-tuple-element.135.mine, bf16[1024,1024]{1,0:T(8,128)(2,1)} %copy-done.6), custom_call_target="tpu_custom_call" | custom-call | tf_op jit(solution)/shard_map/early_kernel/pallas_call | solution.py:508
  148.5 6.9 %all-to-all-done.4 = f32[16,8,1024]{2,1,0:T(8,128)S(1)} async-done(((f32[16,8,1024]{2,1,0:T(8,128)}), f32[16,8,1024]{2,1,0:T(8,128)S(1)}, u32[]{:S(2)}, u32[]{:S(2)}) %all-to-all-start.4) | async-done | bytes 524320 | tf_op jit(solution)/shard_map/all_to_all | solution.py:694
  156.3 6.6 %all-to-all-start.6 = ((bf16[128,8,1024]{2,1,0:T(8,128)(2,1)}), bf16[128,8,1024]{2,1,0:T(8,128)(2,1)}, u32[]{:S(2)}, u32[]{:S(2)}) async-start(bf16[128,8,1024]{2,1,0:T(8,128)(2,1)} %early_kernel.1), calls=%async_computation.6 | async-start | bytes 4194304 | tf_op jit(solution)/shard_map/all_to_all | solution.py:696
  162.9 15.7 %grad_kernel.1 = (bf16[512,1280]{1,0:T(8,128)(2,1)}, bf16[512,128]{1,0:T(8,128)(2,1)}, bf16[512,1024]{1,0:T(8,128)(2,1)}, f32[8,1024]{1,0:T(8,128)}, f32[8,128]{1,0:T(8,128)}) custom-call(bf16[512,1024]{1,0:T(8,128)(2,1)} %bitcast.36, f32[8,1024]{1,0:T(8,128)} %broadcast_in_dim.49.row, f32[512,128]{1,0:T(8,128)} %get-tuple-element.69.scale, ...), custom_call_target="tpu_custom_call" | custom-call | tf_op jit(solution)/shard_map/grad_kernel/pallas_call | solution.py:508
  178.5 3.2 %convolution_convert_fusion.term = bf16[1024,1280]{1,0:T(8,128)(2,1)S(1)} fusion(bf16[512,1024]{1,0:T(8,128)(2,1)} %get-tuple-element.72.act_low, bf16[512,1280]{1,0:T(8,128)(2,1)} %get-tuple-element.117), kind=kOutput, calls=%fused_computation | convolution fusion | flops 1343488000 | bytes 4980736 | tf_op jit(solution)/shard_map/dot_general | solution.py:566
  183.8 2.5 %fusion.6.steps = f32[1024,128]{1,0:T(8,128)} fusion(bf16[512,1024]{1,0:T(8,128)(2,1)} %get-tuple-element.72.act_low, bf16[512,128]{1,0:T(8,128)(2,1)S(1)} %copy-done.13), kind=kOutput, calls=%fused_computation.36 | convolution fusion | flops 134217728 | bytes 1703936 | tf_op jit(solution)/shard_map/dot_general | solution.py:566
  186.4 5.0 %late_kernel.1 = bf16[128,8,768]{2,1,0:T(8,128)(2,1)} custom-call(s32[1]{0:T(128)} %bitcast.3.core_ref, bf16[1024,1280]{1,0:T(8,128)(2,1)} %copy-done, f32[1024,128]{1,0:T(8,128)} %fusion.6.steps, bf16[1024,640]{1,0:T(8,128)(2,1)} %collective-permute-done.8.other, f32[8,1024]{1,0:T(8,128)} %get-tuple-element.119.sums, ...), custom_call_target="tpu_custom_call" | custom-call | tf_op jit(solution)/shard_map/late_kernel/pallas_call | solution.py:508
  192.6 8.5 %all-to-all-start.5 = ((bf16[128,8,768]{2,1,0:T(8,128)(2,1)}), bf16[128,8,768]{2,1,0:T(8,128)(2,1)S(1)}, u32[]{:S(2)}, u32[]{:S(2)}) async-start(bf16[128,8,768]{2,1,0:T(8,128)(2,1)} %late_kernel.1), calls=%async_computation.5 | async-start | bytes 3145728 | tf_op jit(solution)/shard_map/all_to_all | solution.py:735
  201.1 2.6 %early_sum.1 = (f32[8,1024]{1,0:T(8,128)}, f32[8,1024]{1,0:T(8,128)}) custom-call(bf16[128,8,1024]{2,1,0:T(8,128)(2,1)} %all-to-all-done.6.early), custom_call_target="tpu_custom_call" | custom-call | tf_op jit(solution)/shard_map/early_sum/pallas_call | solution.py:508
  203.7 21.8 %all-to-all-done.5.late = bf16[128,8,768]{2,1,0:T(8,128)(2,1)S(1)} async-done(((bf16[128,8,768]{2,1,0:T(8,128)(2,1)}), bf16[128,8,768]{2,1,0:T(8,128)(2,1)S(1)}, u32[]{:S(2)}, u32[]{:S(2)}) %all-to-all-start.5) | async-done | bytes 1572896 | tf_op jit(solution)/shard_map/all_to_all | solution.py:735
  226.8 5.5 %late_sum.1 = (f32[8,2304]{1,0:T(8,128)}, f32[8,1024]{1,0:T(8,128)}, f32[8,128]{1,0:T(8,128)}, f32[8,128]{1,0:T(8,128)}) custom-call(bf16[128,8,768]{2,1,0:T(8,128)(2,1)} %copy-done.1, f32[8,1024]{1,0:T(8,128)} %get-tuple-element.122.gates, f32[8,1024]{1,0:T(8,128)} %get-tuple-element.123.outs), custom_call_target="tpu_custom_call" | custom-call | tf_op jit(solution)/shard_map/late_sum/pallas_call | solution.py:508
  232.2 1.5 slice_reduce_fusion
  (88 shorter events, 22.8 us)
Async XLA Ops:
  4.3 27.0 %slice-start = ((bf16[128,2304]{1,0:T(8,128)(2,1)}), bf16[128,1024]{1,0:T(8,128)(2,1)S(1)}, s32[]{:S(2)}) async-start(bf16[128,2304]{1,0:T(8,128)(2,1)} %param.15), calls=%async_computation.7 | async-start | bytes 524288 | tf_op jit(solution)/shard_map/slice | solution.py:605
  4.3 27.0 %copy-start.12 = (bf16[128,1024]{1,0:T(8,128)(2,1)S(1)}, bf16[128,1024]{1,0:T(8,128)(2,1)}, u32[]{:S(2)}) copy-start(bf16[128,1024]{1,0:T(8,128)(2,1)} %param.19) | copy-start | bytes 786436
  4.3 28.2 %copy-start.14 = (f32[3,16]{1,0:T(4,128)S(1)}, f32[3,16]{1,0:T(4,128)}, u32[]{:S(2)}) copy-start(f32[3,16]{1,0:T(4,128)} %param.17) | copy-start | bytes 580
  29.9 4.8 %copy-start.2 = (bf16[8,64,1408]{2,1,0:T(8,128)(2,1)}, bf16[8,64,1408]{2,1,0:T(8,128)(2,1)S(1)}, u32[]{:S(2)}) copy-start(bf16[8,64,1408]{2,1,0:T(8,128)(2,1)S(1)} %all_to_all.35.mine) | copy-start | bytes 4325380
  29.9 4.1 %collective-permute-start = (bf16[8,64,1408]{2,1,0:T(8,128)(2,1)S(1)}, bf16[8,64,1408]{2,1,0:T(8,128)(2,1)}, u32[]{:S(2)}, u32[]{:S(2)}) collective-permute-start(bf16[8,64,1408]{2,1,0:T(8,128)(2,1)S(1)} %all_to_all.35.mine), channel_id=1, source_target_pairs={{0,1},{1,0},{2,3},{3,2},{4,5},{5,4},{6,7},{7,6},{8,9},{9,8},{10,11... | collective-permute-start | bytes 4325384 | tf_op jit(solution)/shard_map/ppermute | solution.py:525
  31.4 15.3 %collective-permute-start.1 = (bf16[64,2048]{1,0:T(8,128)(2,1)S(1)}, bf16[64,2048]{1,0:T(8,128)(2,1)S(1)}, u32[]{:S(2)}, u32[]{:S(2)}) collective-permute-start(bf16[64,2048]{1,0:T(8,128)(2,1)S(1)} %fusion.1), channel_id=1, source_target_pairs={{0,16},{1,17},{2,18},{3,19},{4,20},{5,21},{6,22},{7,23},{8,24},{9,... | collective-permute-start | bytes 786440 | tf_op jit(solution)/shard_map/ppermute | solution.py:542
  46.9 23.2 %all-to-all-start.1 = ((f32[16,8,1152]{2,1,0:T(8,128)}), f32[16,8,1152]{2,1,0:T(8,128)S(1)}, u32[]{:S(2)}, u32[]{:S(2)}) async-start(f32[16,8,1152]{2,1,0:T(8,128)} %bitcast.40), calls=%async_computation.1 | async-start | bytes 1179648 | tf_op jit(solution)/shard_map/all_to_all | solution.py:627
  54.5 15.5 %collective-permute-start.2 = (bf16[2,64,2048]{2,1,0:T(8,128)(2,1)S(1)}, bf16[2,64,2048]{2,1,0:T(8,128)(2,1)S(1)}, u32[]{:S(2)}, u32[]{:S(2)}) collective-permute-start(bf16[2,64,2048]{2,1,0:T(8,128)(2,1)S(1)} %pad_maximum_fusion), channel_id=1, source_target_pairs={{0,32},{1,33},{2,34},{3,35},{4,36},{5,37},{6,38},{7,39},{8,40},{9,... | collective-permute-start | bytes 1572872 | tf_op jit(solution)/shard_map/ppermute | solution.py:542
  55.2 14.8 %collective-permute-start.3 = (bf16[2,64,2048]{2,1,0:T(8,128)(2,1)S(1)}, bf16[2,64,2048]{2,1,0:T(8,128)(2,1)}, u32[]{:S(2)}, u32[]{:S(2)}) collective-permute-start(bf16[2,64,2048]{2,1,0:T(8,128)(2,1)S(1)} %pad_maximum_fusion), channel_id=1, source_target_pairs={{0,96},{1,97},{2,98},{3,99},{4,100},{5,101},{6,102},{7,103},{8,104... | collective-permute-start | bytes 1572872 | tf_op jit(solution)/shard_map/ppermute | solution.py:542
  70.0 4.4 %copy-start.5 = (f32[16,8,1152]{2,1,0:T(8,128)}, f32[16,8,1152]{2,1,0:T(8,128)S(1)}, u32[]{:S(2)}) copy-start(f32[16,8,1152]{2,1,0:T(8,128)S(1)} %all-to-all-done.1.pieces) | copy-start | bytes 1769476
  70.1 9.0 %collective-permute-start.4 = (bf16[2,32,2048]{2,1,0:T(8,128)(2,1)S(1)}, bf16[2,32,2048]{2,1,0:T(8,128)(2,1)S(1)}, u32[]{:S(2)}, u32[]{:S(2)}) collective-permute-start(bf16[2,32,2048]{2,1,0:T(8,128)(2,1)S(1)} %slice.54), channel_id=1, source_target_pairs={{0,32},{1,33},{2,34},{3,35},{4,36},{5,37},{6,38},{7,39},{8,40},{9,... | collective-permute-start | bytes 786440 | tf_op jit(solution)/shard_map/ppermute | solution.py:542
  71.2 8.2 %collective-permute-start.5 = (bf16[2,32,2048]{2,1,0:T(8,128)(2,1)S(1)}, bf16[2,32,2048]{2,1,0:T(8,128)(2,1)}, u32[]{:S(2)}, u32[]{:S(2)}) collective-permute-start(bf16[2,32,2048]{2,1,0:T(8,128)(2,1)S(1)} %slice.55), channel_id=1, source_target_pairs={{0,96},{1,97},{2,98},{3,99},{4,100},{5,101},{6,102},{7,103},{8,104... | collective-permute-start | bytes 786440 | tf_op jit(solution)/shard_map/ppermute | solution.py:542
  80.5 7.5 %copy-start.4 = (bf16[8,64,2048]{2,1,0:T(8,128)(2,1)}, bf16[8,64,2048]{2,1,0:T(8,128)(2,1)S(1)}, u32[]{:S(2)}) copy-start(bf16[8,64,2048]{2,1,0:T(8,128)(2,1)S(1)} %constant_dynamic-update-slice_fusion.mine) | copy-start | bytes 6291460
  80.5 7.4 %collective-permute-start.6 = (bf16[8,64,2048]{2,1,0:T(8,128)(2,1)S(1)}, bf16[8,64,2048]{2,1,0:T(8,128)(2,1)}, u32[]{:S(2)}, u32[]{:S(2)}) collective-permute-start(bf16[8,64,2048]{2,1,0:T(8,128)(2,1)S(1)} %constant_dynamic-update-slice_fusion.mine), channel_id=1, source_target_pairs={{0,1},{1,0},{2,3},{3,2},{4,5},{5,4},{6,7},{7,6},{8,9},{9,8},{10,11... | collective-permute-start | bytes 6291464 | tf_op jit(solution)/shard_map/ppermute | solution.py:525
  80.6 19.1 %all-to-all-start.2 = ((f32[16,8,1024]{2,1,0:T(8,128)}), f32[16,8,1024]{2,1,0:T(8,128)S(1)}, u32[]{:S(2)}, u32[]{:S(2)}) async-start(f32[16,8,1024]{2,1,0:T(8,128)} %get-tuple-element.96), calls=%async_computation.2 | async-start | bytes 1048576 | tf_op jit(solution)/shard_map/all_to_all | solution.py:646
  99.6 0.8 copy-start.7
  111.4 17.0 %all-to-all-start.3 = ((f32[16,8,1024]{2,1,0:T(8,128)}), f32[16,8,1024]{2,1,0:T(8,128)S(1)}, u32[]{:S(2)}, u32[]{:S(2)}) async-start(f32[16,8,1024]{2,1,0:T(8,128)} %bitcast.41), calls=%async_computation.3 | async-start | bytes 1048576 | tf_op jit(solution)/shard_map/all_to_all | solution.py:669
  115.1 15.9 %copy-start.10 = (bf16[1,512,1024]{2,1,0:T(8,128)(2,1)S(1)}, bf16[1,512,1024]{2,1,0:T(8,128)(2,1)}, u32[]{:S(2)}) copy-start(bf16[1,512,1024]{2,1,0:T(8,128)(2,1)} %param.11) | copy-start | bytes 3145732
  115.2 15.9 %copy-start.16 = (bf16[512,1024]{1,0:T(8,128)(2,1)S(1)}, bf16[512,1024]{1,0:T(8,128)(2,1)}, u32[]{:S(2)}) copy-start(bf16[512,1024]{1,0:T(8,128)(2,1)} %get-tuple-element.113) | copy-start | bytes 3145732
  131.0 1.3 copy-start.3
  131.1 1.5 copy-start.11
  136.0 7.1 %collective-permute-start.7 = (bf16[1024,1024]{1,0:T(8,128)(2,1)}, bf16[1024,1024]{1,0:T(8,128)(2,1)S(1)}, u32[]{:S(2)}, u32[]{:S(2)}) collective-permute-start(bf16[1024,1024]{1,0:T(8,128)(2,1)} %get-tuple-element.134), channel_id=1, source_target_pairs={{0,1},{1,0},{2,3},{3,2},{4,5},{5,4},{6,7},{7,6},{8,9},{9,8},{10,11... | collective-permute-start | bytes 6291464 | tf_op jit(solution)/shard_map/ppermute | solution.py:525
  136.1 19.3 %all-to-all-start.4 = ((f32[16,8,1024]{2,1,0:T(8,128)}), f32[16,8,1024]{2,1,0:T(8,128)S(1)}, u32[]{:S(2)}, u32[]{:S(2)}) async-start(f32[16,8,1024]{2,1,0:T(8,128)} %scan_backward.1), calls=%async_computation.4 | async-start | bytes 1048576 | tf_op jit(solution)/shard_map/all_to_all | solution.py:694
  143.1 1.3 copy-start.6
  155.4 0.8 copy-start.8
  156.3 36.4 %all-to-all-start.6 = ((bf16[128,8,1024]{2,1,0:T(8,128)(2,1)}), bf16[128,8,1024]{2,1,0:T(8,128)(2,1)}, u32[]{:S(2)}, u32[]{:S(2)}) async-start(bf16[128,8,1024]{2,1,0:T(8,128)(2,1)} %early_kernel.1), calls=%async_computation.6 | async-start | bytes 4194304 | tf_op jit(solution)/shard_map/all_to_all | solution.py:696
  181.7 4.5 %copy-start = (bf16[1024,1280]{1,0:T(8,128)(2,1)}, bf16[1024,1280]{1,0:T(8,128)(2,1)S(1)}, u32[]{:S(2)}) copy-start(bf16[1024,1280]{1,0:T(8,128)(2,1)S(1)} %convolution_convert_fusion.term) | copy-start | bytes 7864324
  181.7 1.2 copy-start.15
  181.8 2.0 copy-start.13
  183.0 3.4 %collective-permute-start.8 = (bf16[1024,640]{1,0:T(8,128)(2,1)}, bf16[1024,640]{1,0:T(8,128)(2,1)}, u32[]{:S(2)}, u32[]{:S(2)}) collective-permute-start(bf16[1024,640]{1,0:T(8,128)(2,1)} %slice_select_fusion), channel_id=1, source_target_pairs={{0,1},{1,0},{2,3},{3,2},{4,5},{5,4},{6,7},{7,6},{8,9},{9,8},{10,11... | collective-permute-start | bytes 3932168 | tf_op jit(solution)/shard_map/ppermute | solution.py:525
  192.6 32.9 %all-to-all-start.5 = ((bf16[128,8,768]{2,1,0:T(8,128)(2,1)}), bf16[128,8,768]{2,1,0:T(8,128)(2,1)S(1)}, u32[]{:S(2)}, u32[]{:S(2)}) async-start(bf16[128,8,768]{2,1,0:T(8,128)(2,1)} %late_kernel.1), calls=%async_computation.5 | async-start | bytes 3145728 | tf_op jit(solution)/shard_map/all_to_all | solution.py:735
  225.6 1.2 copy-start.1
  (1 other events, 0.8 us)

commit v4 on v3

--- a/solution.py
+++ b/solution.py
@@ -429,29 +429,24 @@
 
 
 def late_kernel(core_ref, term, steps, other, sums, sums_mix, tile, packed, across, columns):
-    across[...] = jnp.zeros_like(across)
-    across[16:17, :] = sums[0:1, :]
-    across[17:18, :] = sums_mix[0:1, :]
-    across[24:25, :] = sums[1:2, :]
-    columns[...] = across[...].T
+    @pl.when(pl.program_id(0) == 0)
+    def start():
+        across[...] = jnp.zeros_like(across)
+        across[16:17, :] = sums[0:1, :]
+        across[17:18, :] = sums_mix[0:1, :]
+        across[24:25, :] = sums[1:2, :]
+        columns[...] = across[...].T
+
     first = core_ref[0] == 0
-    lane = iota(1)
-
-    def body(j, carry):
-        rows = pl.ds(pl.multiple_of(j * Q, Q), Q)
-        low, high = term[rows, 0:640].astype(F32), term[rows, 640:1280].astype(F32)
-        mine = jnp.where(first, low, high)
-        both = mine.astype(F32) + other[rows, :].astype(F32)
-        packed[pl.ds(j * 16, 16), :, 0:640] = both.reshape(16, 8, 640).astype(LOW)
-        extra = (steps[rows, :] + columns[rows, :]).reshape(16, 8, 128)
-        extra = (extra + tile[...][None]).reshape(Q, 128)
-        coarse = extra.astype(LOW).astype(F32)
-        fine = pltpu.roll(extra - coarse, 64, 1)
-        small = jnp.where(lane < 64, coarse, fine)
-        packed[pl.ds(j * 16, 16), :, 640:768] = small.reshape(16, 8, 128).astype(LOW)
-        return carry
-
-    lax.fori_loop(0, term.shape[0] // Q, body, 0)
+    low, high = term[:, 0:640].astype(F32), term[:, 640:1280].astype(F32)
+    both = jnp.where(first, low, high) + other[...].astype(F32)
+    packed[:, :, 0:640] = both.reshape(16, 8, 640).astype(LOW)
+    extra = (steps[...] + columns[rows_of(pl.program_id(0)), :]).reshape(16, 8, 128)
+    extra = (extra + tile[...][None]).reshape(Q, 128)
+    coarse = extra.astype(LOW).astype(F32)
+    fine = pltpu.roll(extra - coarse, 64, 1)
+    small = jnp.where(iota(1) < 64, coarse, fine)
+    packed[:, :, 640:768] = small.reshape(16, 8, 128).astype(LOW)
 
 
 def early_sum(early, gates, outs):
@@ -473,18 +468,26 @@
     input_grad[:, 0:1024] = gates[...] * grad_scale
     output_grad[...] = outs[...] * grad_scale
     lane = iota(1, (8, 128)).astype(F32)
-
-    def body(j, carry):
-        input_grad[:, 1024:1664] += late[2 * j, :, 0:640].astype(F32)
-        input_grad[:, 1664:2304] += late[2 * j + 1, :, 0:640].astype(F32)
-        for k in range(2):
-            parts = late[2 * j + k, :, 640:768].astype(F32)
-            parts = parts + pltpu.roll(parts, 64, 1)
-            small[...] += parts
-            table[...] += jnp.where(lane == parts[:, 25:26], parts[:, 24:25], 0.0)
-        return carry
-
-    lax.fori_loop(0, late.shape[0] // 2, body, 0, unroll=4)
+    across = late.shape[0] // 8
+
+    def body(d, carry):
+        parts = jnp.zeros((8, 128), F32)
+        low = jnp.zeros((8, 640), F32)
+        high = jnp.zeros((8, 640), F32)
+        for k in range(0, across, 2):
+            even, odd = late[across * d + k], late[across * d + k + 1]
+            low = low + even[:, 0:640].astype(F32)
+            high = high + odd[:, 0:640].astype(F32)
+            parts = parts + even[:, 640:768].astype(F32) + odd[:, 640:768].astype(F32)
+        input_grad[:, 1024:1664] += low
+        input_grad[:, 1664:2304] += high
+        parts = parts + pltpu.roll(parts, 64, 1)
+        small[...] += parts
+        session = parts[:, 25:26] * (1.0 / across)
+        table[...] += jnp.where(lane == session, parts[:, 24:25], 0.0)
+        return carry
+
+    lax.fori_loop(0, 8, body, 0)
     input_grad[:, 1024:2304] = input_grad[:, 1024:2304] * grad_scale
     small[...] = small[...] * grad_scale
     table[...] = table[...] * grad_scale
@@ -501,9 +504,10 @@
                 shape, functools.partial(at_origin, len(shape)), pipeline_mode=pl.Buffered(1)
             )
         block = (shape[0] // chunks,) + tuple(shape[1:])
+        last = (0,) * (len(shape) - 1)
         if back:
-            return pl.BlockSpec(block, lambda i: (chunks - 1 - i, 0))
-        return pl.BlockSpec(block, lambda i: (i, 0))
+            return pl.BlockSpec(block, lambda i, *unused: (chunks - 1 - i,) + last)
+        return pl.BlockSpec(block, lambda i, *unused: (i,) + last)
 
     return pl.pallas_call(
         kernel,
@@ -731,6 +735,9 @@
         (((devices, 8, 768), LOW),),
         (((128, 1024), F32), ((1024, 128), F32)),
         1,
+        chunks=1024 // Q,
+        parts=range(3),
+        out_parts=(0,),
     )
     late_got = lax.all_to_all(late, ALL, 0, 0)
     gates, outs = run(early_sum, (early_got,), (((8, 1024), F32), ((8, 1024), F32)))

time: 238 us -> 237 us (level)
  transfers between devices with their start and end apart: 15 -> 15, of which waited for: 8 -> 7; matrix products, arithmetic and copies ran while one was open for 6% -> 6% of each run, Pallas kernels for 30% -> 31%
where the time goes in v4:
time: 237 us; the launch traced here: 236 us
  Pallas kernels  88 us (37%)
  starting transfers between devices  49.4 us (21%)
  waiting for transfers between devices  38.8 us (16%)
  blocking collectives  25.6 us (11%)
  local copies, waits for them, and re-layouts  17.2 us (7%)
  matrix products  10.4 us (4%)
  other arithmetic  4.68 us (2%)
    pallas_call x12, Pallas kernels, run(): pl.pallas_call(kernel, name=getattr(kernel, '__name__', 'late_sum'), out_...  88 us
    all_to_all x1, blocking collectives, gather_rows(): lax.all_to_all(jnp.broadcast_to(mine[None], (count,) + mine.shape), 'dp',...  25.6 us
    all_to_all x1, waiting for transfers between devices, per_device(): late_got = lax.all_to_all(late, ALL, 0, 0)  21.8 us
    dot_general x4, matrix products, column_dot(): lax.dot_general(a, b, (((0,), (0,)), ((), ())), preferred_element_type=F32)  10.4 us
    all_to_all x1, starting transfers between devices, per_device(): late_got = lax.all_to_all(late, ALL, 0, 0)  9.74 us
    ppermute x5, starting transfers between devices, moved(): return lax.ppermute(value, ALL, [(i, to(i) % count) for i in range(count)])  7.73 us
    all_to_all x1, starting transfers between devices, per_device(): pieces = lax.all_to_all(packed.reshape(slots, 8, 1152), 'ctx', 0, 0)  7.61 us
    unnamed x36, local copies, waits for them, and re-layouts  7.08 us
  transfers between devices with their start and end apart: 15, of which 7 were waited for; matrix products, arithmetic and copies ran while one was open for 6% of the time, Pallas kernels for 31%

profile of v4, /device:TPU:0, one launch (start us, length us, event | category | flops | bytes accessed | tf_op | source)
XLA Modules:
  0.0 235.7 jit_solution(9927813650162709482)
XLA Ops:
  4.4 25.6 %all_to_all.35.mine = bf16[8,64,1408]{2,1,0:T(8,128)(2,1)S(1)} all-to-all(bf16[8,64,1408]{2,1,0:T(8,128)(2,1)S(1)} %broadcast_in_dim.54), channel_id=1, replica_groups=mesh['dp'=8,'ctx'=16] {'dp'}, dimensions={0} | all-to-all | bytes 2883584 | tf_op jit(solution)/shard_map/all_to_all | solution.py:540
  34.7 12.0 %prep_kernel.1 = (bf16[1024,1408]{1,0:T(8,128)(2,1)}, bf16[512,1024]{1,0:T(8,128)(2,1)}, f32[512,128]{1,0:T(8,128)}, f32[512,1024]{1,0:T(8,128)}, f32[512,128]{1...) custom-call(s32[1]{0:T(128)} %bitcast.3.core_ref, ...), custom_call_target="tpu_custom_call" | custom-call | tf_op jit(solution)/shard_map/prep_kernel/pallas_call | solution.py:512
  46.9 7.6 %all-to-all-start.1 = ((f32[16,8,1152]{2,1,0:T(8,128)}), f32[16,8,1152]{2,1,0:T(8,128)S(1)}, u32[]{:S(2)}, u32[]{:S(2)}) async-start(f32[16,8,1152]{2,1,0:T(8,128)} %bitcast.40), calls=%async_computation.1 | async-start | bytes 1179648 | tf_op jit(solution)/shard_map/all_to_all | solution.py:631
  55.2 2.6 %collective-permute-start.3 = (bf16[2,64,2048]{2,1,0:T(8,128)(2,1)S(1)}, bf16[2,64,2048]{2,1,0:T(8,128)(2,1)}, u32[]{:S(2)}, u32[]{:S(2)}) collective-permute-start(bf16[2,64,2048]{2,1,0:T(8,128)(2,1)S(1)} %pad_maximum_fusion), channel_id=1, source_target_pairs={{0,96},{1,97},{2,98},{3,99},{4,100},{5,101},{6,102},{7,103},{8,104... | collective-permute-start | bytes 1572872 | tf_op jit(solution)/shard_map/ppermute | solution.py:546
  57.8 8.3 %local_kernel.1 = (f32[512,1024]{1,0:T(8,128)}, f32[512,1024]{1,0:T(8,128)}) custom-call(f32[512,1024]{1,0:T(8,128)} %get-tuple-element.77.value, f32[512,128]{1,0:T(8,128)} %get-tuple-element.78.in_map, f32[512,128]{1,0:T(8,128)} %get-tuple-element.79.out_map, f32[512,128]{1,0:T(8,128)} %get-tuple-element.80.step, f32[512,128]{1,0:T(8,128)} %get-tuple-element.81.decay, ...), custom_call_target="tpu_custom_call" | custom-call | tf_op jit(solution)/shard_map/local_kernel/pallas_call | solution.py:512
  66.2 3.9 %collective-permute-done.2 = bf16[2,64,2048]{2,1,0:T(8,128)(2,1)S(1)} collective-permute-done((bf16[2,64,2048]{2,1,0:T(8,128)(2,1)S(1)}, bf16[2,64,2048]{2,1,0:T(8,128)(2,1)S(1)}, u32[]{:S(2)}, u32[]{:S(2)}) %collective-permute-start.2) | collective-permute-done | bytes 524320 | tf_op jit(solution)/shard_map/ppermute | solution.py:546
  71.2 3.2 %collective-permute-start.5 = (bf16[2,32,2048]{2,1,0:T(8,128)(2,1)S(1)}, bf16[2,32,2048]{2,1,0:T(8,128)(2,1)}, u32[]{:S(2)}, u32[]{:S(2)}) collective-permute-start(bf16[2,32,2048]{2,1,0:T(8,128)(2,1)S(1)} %slice.55), channel_id=1, source_target_pairs={{0,96},{1,97},{2,98},{3,99},{4,100},{5,101},{6,102},{7,103},{8,104... | collective-permute-start | bytes 786440 | tf_op jit(solution)/shard_map/ppermute | solution.py:546
  74.4 2.2 scan_forward.1
  77.8 1.4 collective-permute-done.4
  80.6 6.7 %all-to-all-start.2 = ((f32[16,8,1024]{2,1,0:T(8,128)}), f32[16,8,1024]{2,1,0:T(8,128)S(1)}, u32[]{:S(2)}, u32[]{:S(2)}) async-start(f32[16,8,1024]{2,1,0:T(8,128)} %get-tuple-element.96), calls=%async_computation.2 | async-start | bytes 1048576 | tf_op jit(solution)/shard_map/all_to_all | solution.py:650
  87.9 7.3 %gate_kernel.1 = (bf16[1024,1024]{1,0:T(8,128)(2,1)}, f32[512,1024]{1,0:T(8,128)}, f32[512,1024]{1,0:T(8,128)}) custom-call(s32[2]{0:T(128)} %pad_add_fusion.place_ref, bf16[512,1024]{1,0:T(8,128)(2,1)} %get-tuple-element.72.act_low, bf16[8,64,2048]{2,1,0:T(8,128)(2,1)} %copy-done.4, bf16[8,64,2048]{2,1,0:T(8,128)(2,1)} %collective-permute-done.6.other, ...), custom_call_target="tpu_custom_call" | custom-call | tf_op jit(solution)/shard_map/gate_kernel/pallas_call | solution.py:512
  95.2 4.4 %all-to-all-done.2 = f32[16,8,1024]{2,1,0:T(8,128)S(1)} async-done(((f32[16,8,1024]{2,1,0:T(8,128)}), f32[16,8,1024]{2,1,0:T(8,128)S(1)}, u32[]{:S(2)}, u32[]{:S(2)}) %all-to-all-start.2) | async-done | bytes 524320 | tf_op jit(solution)/shard_map/all_to_all | solution.py:650
  100.5 10.9 %mix_kernel.1 = (bf16[512,1024]{1,0:T(8,128)(2,1)}, bf16[512,1024]{1,0:T(8,128)(2,1)}, f32[512,1024]{1,0:T(8,128)}, f32[512,128]{1,0:T(8,128)}, f32[512,1024]{1,...) custom-call(f32[512,1024]{1,0:T(8,128)} %get-tuple-element.92.gate_all, ...), custom_call_target="tpu_custom_call" | custom-call | tf_op jit(solution)/shard_map/mix_kernel/pallas_call | solution.py:512
  111.4 3.8 %all-to-all-start.3 = ((f32[16,8,1024]{2,1,0:T(8,128)}), f32[16,8,1024]{2,1,0:T(8,128)S(1)}, u32[]{:S(2)}, u32[]{:S(2)}) async-start(f32[16,8,1024]{2,1,0:T(8,128)} %bitcast.41), calls=%async_computation.3 | async-start | bytes 1048576 | tf_op jit(solution)/shard_map/all_to_all | solution.py:673
  115.2 13.2 %inner_kernel.1 = (f32[512,1024]{1,0:T(8,128)}, f32[512,256]{1,0:T(8,128)}, f32[32,128]{1,0:T(8,128)}) custom-call(bf16[128,1024]{1,0:T(8,128)(2,1)} %and_convert_fusion.spread, f32[512,1024]{1,0:T(8,128)} %get-tuple-element.77.value, f32[512,128]{1,0:T(8,128)} %get-tuple-element.78.in_map, f32[512,128]{1,0:T(8,128)} %get-tuple-element.79.out_map, ...), custom_call_target="tpu_custom_call" | custom-call | tf_op jit(solution)/shard_map/inner_kernel/pallas_call | solution.py:512
  129.1 1.9 scan_backward.1
  131.1 1.3 convolution_convert_fusion.1
  132.6 3.4 %broadcast_select_fusion = (bf16[1024,1024]{1,0:T(8,128)(2,1)}, bf16[1024,1024]{1,0:T(8,128)(2,1)}) fusion(bf16[1024,1024]{1,0:T(8,128)(2,1)S(1)} %convolution_convert_fusion.1, pred[]{:T(512)S(6)} %eq.57, bf16[512,1024]{1,0:T(8,128)(2,1)S(1)} %copy-done.3, bf16[512,1024]{1,0:T(8,128)(2,1)S(1)} %copy-done.11), kind=kOutput, calls=%fused_computation.1 | convolution fusion | flops 1076887552 | bytes 8388609 | tf_op jit(solution)/shard_map/dot_general | solution.py:570
  136.1 7.0 %all-to-all-start.4 = ((f32[16,8,1024]{2,1,0:T(8,128)}), f32[16,8,1024]{2,1,0:T(8,128)S(1)}, u32[]{:S(2)}, u32[]{:S(2)}) async-start(f32[16,8,1024]{2,1,0:T(8,128)} %scan_backward.1), calls=%async_computation.4 | async-start | bytes 1048576 | tf_op jit(solution)/shard_map/all_to_all | solution.py:698
  143.1 1.3 copy-done.6
  144.4 4.1 %early_kernel.1 = bf16[128,8,1024]{2,1,0:T(8,128)(2,1)} custom-call(bf16[1024,1024]{1,0:T(8,128)(2,1)} %get-tuple-element.135.mine, bf16[1024,1024]{1,0:T(8,128)(2,1)} %copy-done.6), custom_call_target="tpu_custom_call" | custom-call | tf_op jit(solution)/shard_map/early_kernel/pallas_call | solution.py:512
  148.5 6.9 %all-to-all-done.4 = f32[16,8,1024]{2,1,0:T(8,128)S(1)} async-done(((f32[16,8,1024]{2,1,0:T(8,128)}), f32[16,8,1024]{2,1,0:T(8,128)S(1)}, u32[]{:S(2)}, u32[]{:S(2)}) %all-to-all-start.4) | async-done | bytes 524320 | tf_op jit(solution)/shard_map/all_to_all | solution.py:698
  156.3 6.6 %all-to-all-start.6 = ((bf16[128,8,1024]{2,1,0:T(8,128)(2,1)}), bf16[128,8,1024]{2,1,0:T(8,128)(2,1)}, u32[]{:S(2)}, u32[]{:S(2)}) async-start(bf16[128,8,1024]{2,1,0:T(8,128)(2,1)} %early_kernel.1), calls=%async_computation.6 | async-start | bytes 4194304 | tf_op jit(solution)/shard_map/all_to_all | solution.py:700
  162.9 15.7 %grad_kernel.1 = (bf16[512,1280]{1,0:T(8,128)(2,1)}, bf16[512,128]{1,0:T(8,128)(2,1)}, bf16[512,1024]{1,0:T(8,128)(2,1)}, f32[8,1024]{1,0:T(8,128)}, f32[8,128]{1,0:T(8,128)}) custom-call(bf16[512,1024]{1,0:T(8,128)(2,1)} %bitcast.36, f32[8,1024]{1,0:T(8,128)} %broadcast_in_dim.49.row, f32[512,128]{1,0:T(8,128)} %get-tuple-element.69.scale, ...), custom_call_target="tpu_custom_call" | custom-call | tf_op jit(solution)/shard_map/grad_kernel/pallas_call | solution.py:512
  178.5 3.2 %convolution_convert_fusion.term = bf16[1024,1280]{1,0:T(8,128)(2,1)S(1)} fusion(bf16[512,1024]{1,0:T(8,128)(2,1)} %get-tuple-element.72.act_low, bf16[512,1280]{1,0:T(8,128)(2,1)} %get-tuple-element.117), kind=kOutput, calls=%fused_computation | convolution fusion | flops 1343488000 | bytes 4980736 | tf_op jit(solution)/shard_map/dot_general | solution.py:570
  183.8 2.5 %fusion.6.steps = f32[1024,128]{1,0:T(8,128)} fusion(bf16[512,1024]{1,0:T(8,128)(2,1)} %get-tuple-element.72.act_low, bf16[512,128]{1,0:T(8,128)(2,1)S(1)} %copy-done.13), kind=kOutput, calls=%fused_computation.36 | convolution fusion | flops 134217728 | bytes 1703936 | tf_op jit(solution)/shard_map/dot_general | solution.py:570
  186.4 6.5 %late_kernel.1 = bf16[128,8,768]{2,1,0:T(8,128)(2,1)} custom-call(s32[1]{0:T(128)} %bitcast.3.core_ref, bf16[1024,1280]{1,0:T(8,128)(2,1)} %copy-done, f32[1024,128]{1,0:T(8,128)} %fusion.6.steps, bf16[1024,640]{1,0:T(8,128)(2,1)} %collective-permute-done.8.other, f32[8,1024]{1,0:T(8,128)} %get-tuple-element.119.sums, ...), custom_call_target="tpu_custom_call" | custom-call | tf_op jit(solution)/shard_map/late_kernel/pallas_call | solution.py:512
  192.9 9.7 %all-to-all-start.5 = ((bf16[128,8,768]{2,1,0:T(8,128)(2,1)}), bf16[128,8,768]{2,1,0:T(8,128)(2,1)S(1)}, u32[]{:S(2)}, u32[]{:S(2)}) async-start(bf16[128,8,768]{2,1,0:T(8,128)(2,1)} %late_kernel.1), calls=%async_computation.5 | async-start | bytes 3145728 | tf_op jit(solution)/shard_map/all_to_all | solution.py:742
  202.6 2.6 %early_sum.1 = (f32[8,1024]{1,0:T(8,128)}, f32[8,1024]{1,0:T(8,128)}) custom-call(bf16[128,8,1024]{2,1,0:T(8,128)(2,1)} %all-to-all-done.6.early), custom_call_target="tpu_custom_call" | custom-call | tf_op jit(solution)/shard_map/early_sum/pallas_call | solution.py:512
  205.2 21.8 %all-to-all-done.5.late = bf16[128,8,768]{2,1,0:T(8,128)(2,1)S(1)} async-done(((bf16[128,8,768]{2,1,0:T(8,128)(2,1)}), bf16[128,8,768]{2,1,0:T(8,128)(2,1)S(1)}, u32[]{:S(2)}, u32[]{:S(2)}) %all-to-all-start.5) | async-done | bytes 1572896 | tf_op jit(solution)/shard_map/all_to_all | solution.py:742
  228.2 3.3 %late_sum.1 = (f32[8,2304]{1,0:T(8,128)}, f32[8,1024]{1,0:T(8,128)}, f32[8,128]{1,0:T(8,128)}, f32[8,128]{1,0:T(8,128)}) custom-call(bf16[128,8,768]{2,1,0:T(8,128)(2,1)} %copy-done.1, f32[8,1024]{1,0:T(8,128)} %get-tuple-element.122.gates, f32[8,1024]{1,0:T(8,128)} %get-tuple-element.123.outs), custom_call_target="tpu_custom_call" | custom-call | tf_op jit(solution)/shard_map/late_sum/pallas_call | solution.py:512
  231.5 1.5 slice_reduce_fusion
  (88 shorter events, 21.6 us)
Async XLA Ops:
  4.3 27.0 %slice-start = ((bf16[128,2304]{1,0:T(8,128)(2,1)}), bf16[128,1024]{1,0:T(8,128)(2,1)S(1)}, s32[]{:S(2)}) async-start(bf16[128,2304]{1,0:T(8,128)(2,1)} %param.15), calls=%async_computation.7 | async-start | bytes 524288 | tf_op jit(solution)/shard_map/slice | solution.py:609
  4.3 27.0 %copy-start.12 = (bf16[128,1024]{1,0:T(8,128)(2,1)S(1)}, bf16[128,1024]{1,0:T(8,128)(2,1)}, u32[]{:S(2)}) copy-start(bf16[128,1024]{1,0:T(8,128)(2,1)} %param.19) | copy-start | bytes 786436
  4.3 28.2 %copy-start.14 = (f32[3,16]{1,0:T(4,128)S(1)}, f32[3,16]{1,0:T(4,128)}, u32[]{:S(2)}) copy-start(f32[3,16]{1,0:T(4,128)} %param.17) | copy-start | bytes 580
  29.9 4.8 %copy-start.2 = (bf16[8,64,1408]{2,1,0:T(8,128)(2,1)}, bf16[8,64,1408]{2,1,0:T(8,128)(2,1)S(1)}, u32[]{:S(2)}) copy-start(bf16[8,64,1408]{2,1,0:T(8,128)(2,1)S(1)} %all_to_all.35.mine) | copy-start | bytes 4325380
  29.9 4.1 %collective-permute-start = (bf16[8,64,1408]{2,1,0:T(8,128)(2,1)S(1)}, bf16[8,64,1408]{2,1,0:T(8,128)(2,1)}, u32[]{:S(2)}, u32[]{:S(2)}) collective-permute-start(bf16[8,64,1408]{2,1,0:T(8,128)(2,1)S(1)} %all_to_all.35.mine), channel_id=1, source_target_pairs={{0,1},{1,0},{2,3},{3,2},{4,5},{5,4},{6,7},{7,6},{8,9},{9,8},{10,11... | collective-permute-start | bytes 4325384 | tf_op jit(solution)/shard_map/ppermute | solution.py:529
  31.4 15.3 %collective-permute-start.1 = (bf16[64,2048]{1,0:T(8,128)(2,1)S(1)}, bf16[64,2048]{1,0:T(8,128)(2,1)S(1)}, u32[]{:S(2)}, u32[]{:S(2)}) collective-permute-start(bf16[64,2048]{1,0:T(8,128)(2,1)S(1)} %fusion.1), channel_id=1, source_target_pairs={{0,16},{1,17},{2,18},{3,19},{4,20},{5,21},{6,22},{7,23},{8,24},{9,... | collective-permute-start | bytes 786440 | tf_op jit(solution)/shard_map/ppermute | solution.py:546
  46.9 23.2 %all-to-all-start.1 = ((f32[16,8,1152]{2,1,0:T(8,128)}), f32[16,8,1152]{2,1,0:T(8,128)S(1)}, u32[]{:S(2)}, u32[]{:S(2)}) async-start(f32[16,8,1152]{2,1,0:T(8,128)} %bitcast.40), calls=%async_computation.1 | async-start | bytes 1179648 | tf_op jit(solution)/shard_map/all_to_all | solution.py:631
  54.5 15.5 %collective-permute-start.2 = (bf16[2,64,2048]{2,1,0:T(8,128)(2,1)S(1)}, bf16[2,64,2048]{2,1,0:T(8,128)(2,1)S(1)}, u32[]{:S(2)}, u32[]{:S(2)}) collective-permute-start(bf16[2,64,2048]{2,1,0:T(8,128)(2,1)S(1)} %pad_maximum_fusion), channel_id=1, source_target_pairs={{0,32},{1,33},{2,34},{3,35},{4,36},{5,37},{6,38},{7,39},{8,40},{9,... | collective-permute-start | bytes 1572872 | tf_op jit(solution)/shard_map/ppermute | solution.py:546
  55.2 14.8 %collective-permute-start.3 = (bf16[2,64,2048]{2,1,0:T(8,128)(2,1)S(1)}, bf16[2,64,2048]{2,1,0:T(8,128)(2,1)}, u32[]{:S(2)}, u32[]{:S(2)}) collective-permute-start(bf16[2,64,2048]{2,1,0:T(8,128)(2,1)S(1)} %pad_maximum_fusion), channel_id=1, source_target_pairs={{0,96},{1,97},{2,98},{3,99},{4,100},{5,101},{6,102},{7,103},{8,104... | collective-permute-start | bytes 1572872 | tf_op jit(solution)/shard_map/ppermute | solution.py:546
  70.0 4.4 %copy-start.5 = (f32[16,8,1152]{2,1,0:T(8,128)}, f32[16,8,1152]{2,1,0:T(8,128)S(1)}, u32[]{:S(2)}) copy-start(f32[16,8,1152]{2,1,0:T(8,128)S(1)} %all-to-all-done.1.pieces) | copy-start | bytes 1769476
  70.1 9.0 %collective-permute-start.4 = (bf16[2,32,2048]{2,1,0:T(8,128)(2,1)S(1)}, bf16[2,32,2048]{2,1,0:T(8,128)(2,1)S(1)}, u32[]{:S(2)}, u32[]{:S(2)}) collective-permute-start(bf16[2,32,2048]{2,1,0:T(8,128)(2,1)S(1)} %slice.54), channel_id=1, source_target_pairs={{0,32},{1,33},{2,34},{3,35},{4,36},{5,37},{6,38},{7,39},{8,40},{9,... | collective-permute-start | bytes 786440 | tf_op jit(solution)/shard_map/ppermute | solution.py:546
  71.2 8.2 %collective-permute-start.5 = (bf16[2,32,2048]{2,1,0:T(8,128)(2,1)S(1)}, bf16[2,32,2048]{2,1,0:T(8,128)(2,1)}, u32[]{:S(2)}, u32[]{:S(2)}) collective-permute-start(bf16[2,32,2048]{2,1,0:T(8,128)(2,1)S(1)} %slice.55), channel_id=1, source_target_pairs={{0,96},{1,97},{2,98},{3,99},{4,100},{5,101},{6,102},{7,103},{8,104... | collective-permute-start | bytes 786440 | tf_op jit(solution)/shard_map/ppermute | solution.py:546
  80.5 7.5 %copy-start.4 = (bf16[8,64,2048]{2,1,0:T(8,128)(2,1)}, bf16[8,64,2048]{2,1,0:T(8,128)(2,1)S(1)}, u32[]{:S(2)}) copy-start(bf16[8,64,2048]{2,1,0:T(8,128)(2,1)S(1)} %constant_dynamic-update-slice_fusion.mine) | copy-start | bytes 6291460
  80.5 7.4 %collective-permute-start.6 = (bf16[8,64,2048]{2,1,0:T(8,128)(2,1)S(1)}, bf16[8,64,2048]{2,1,0:T(8,128)(2,1)}, u32[]{:S(2)}, u32[]{:S(2)}) collective-permute-start(bf16[8,64,2048]{2,1,0:T(8,128)(2,1)S(1)} %constant_dynamic-update-slice_fusion.mine), channel_id=1, source_target_pairs={{0,1},{1,0},{2,3},{3,2},{4,5},{5,4},{6,7},{7,6},{8,9},{9,8},{10,11... | collective-permute-start | bytes 6291464 | tf_op jit(solution)/shard_map/ppermute | solution.py:529
  80.6 19.1 %all-to-all-start.2 = ((f32[16,8,1024]{2,1,0:T(8,128)}), f32[16,8,1024]{2,1,0:T(8,128)S(1)}, u32[]{:S(2)}, u32[]{:S(2)}) async-start(f32[16,8,1024]{2,1,0:T(8,128)} %get-tuple-element.96), calls=%async_computation.2 | async-start | bytes 1048576 | tf_op jit(solution)/shard_map/all_to_all | solution.py:650
  99.6 0.8 copy-start.7
  111.4 17.0 %all-to-all-start.3 = ((f32[16,8,1024]{2,1,0:T(8,128)}), f32[16,8,1024]{2,1,0:T(8,128)S(1)}, u32[]{:S(2)}, u32[]{:S(2)}) async-start(f32[16,8,1024]{2,1,0:T(8,128)} %bitcast.41), calls=%async_computation.3 | async-start | bytes 1048576 | tf_op jit(solution)/shard_map/all_to_all | solution.py:673
  115.1 15.9 %copy-start.10 = (bf16[1,512,1024]{2,1,0:T(8,128)(2,1)S(1)}, bf16[1,512,1024]{2,1,0:T(8,128)(2,1)}, u32[]{:S(2)}) copy-start(bf16[1,512,1024]{2,1,0:T(8,128)(2,1)} %param.11) | copy-start | bytes 3145732
  115.2 15.9 %copy-start.16 = (bf16[512,1024]{1,0:T(8,128)(2,1)S(1)}, bf16[512,1024]{1,0:T(8,128)(2,1)}, u32[]{:S(2)}) copy-start(bf16[512,1024]{1,0:T(8,128)(2,1)} %get-tuple-element.113) | copy-start | bytes 3145732
  131.0 1.3 copy-start.3
  131.1 1.5 copy-start.11
  136.0 7.1 %collective-permute-start.7 = (bf16[1024,1024]{1,0:T(8,128)(2,1)}, bf16[1024,1024]{1,0:T(8,128)(2,1)S(1)}, u32[]{:S(2)}, u32[]{:S(2)}) collective-permute-start(bf16[1024,1024]{1,0:T(8,128)(2,1)} %get-tuple-element.134), channel_id=1, source_target_pairs={{0,1},{1,0},{2,3},{3,2},{4,5},{5,4},{6,7},{7,6},{8,9},{9,8},{10,11... | collective-permute-start | bytes 6291464 | tf_op jit(solution)/shard_map/ppermute | solution.py:529
  136.1 19.3 %all-to-all-start.4 = ((f32[16,8,1024]{2,1,0:T(8,128)}), f32[16,8,1024]{2,1,0:T(8,128)S(1)}, u32[]{:S(2)}, u32[]{:S(2)}) async-start(f32[16,8,1024]{2,1,0:T(8,128)} %scan_backward.1), calls=%async_computation.4 | async-start | bytes 1048576 | tf_op jit(solution)/shard_map/all_to_all | solution.py:698
  143.1 1.3 copy-start.6
  155.4 0.8 copy-start.8
  156.3 36.6 %all-to-all-start.6 = ((bf16[128,8,1024]{2,1,0:T(8,128)(2,1)}), bf16[128,8,1024]{2,1,0:T(8,128)(2,1)}, u32[]{:S(2)}, u32[]{:S(2)}) async-start(bf16[128,8,1024]{2,1,0:T(8,128)(2,1)} %early_kernel.1), calls=%async_computation.6 | async-start | bytes 4194304 | tf_op jit(solution)/shard_map/all_to_all | solution.py:700
  181.7 4.5 %copy-start = (bf16[1024,1280]{1,0:T(8,128)(2,1)}, bf16[1024,1280]{1,0:T(8,128)(2,1)S(1)}, u32[]{:S(2)}) copy-start(bf16[1024,1280]{1,0:T(8,128)(2,1)S(1)} %convolution_convert_fusion.term) | copy-start | bytes 7864324
  181.7 1.2 copy-start.15
  181.8 2.0 copy-start.13
  183.0 3.4 %collective-permute-start.8 = (bf16[1024,640]{1,0:T(8,128)(2,1)}, bf16[1024,640]{1,0:T(8,128)(2,1)}, u32[]{:S(2)}, u32[]{:S(2)}) collective-permute-start(bf16[1024,640]{1,0:T(8,128)(2,1)} %slice_select_fusion), channel_id=1, source_target_pairs={{0,1},{1,0},{2,3},{3,2},{4,5},{5,4},{6,7},{7,6},{8,9},{9,8},{10,11... | collective-permute-start | bytes 3932168 | tf_op jit(solution)/shard_map/ppermute | solution.py:529
  192.9 34.2 %all-to-all-start.5 = ((bf16[128,8,768]{2,1,0:T(8,128)(2,1)}), bf16[128,8,768]{2,1,0:T(8,128)(2,1)S(1)}, u32[]{:S(2)}, u32[]{:S(2)}) async-start(bf16[128,8,768]{2,1,0:T(8,128)(2,1)} %late_kernel.1), calls=%async_computation.5 | async-start | bytes 3145728 | tf_op jit(solution)/shard_map/all_to_all | solution.py:742
  227.0 1.2 copy-start.1
  (1 other events, 0.8 us)
